TPU v7x, 32 devices: a whole 2x2x4 slice. The times are simulated.
32 devices in a mesh: batch: 4 (over z), heads: 4 (over x, core), seq: 2 (over y).
Axes of the slice: x: 2, y: 2, z: 4, core: 2. Of those that a mesh axis runs over, the one named last changes fastest.
Arguments:
- block_input: bfloat16 [4, 2, 1024, 768], P('batch', 'seq', 'heads'), may hold values from -6 to 6
- segment_ids: int32 [4, 2048], P('batch'), may hold values from 0 to 3, never falling along the last dimension, each value on 1 to 1536 neighbouring positions
- norm1_gain: bfloat16 [768], P(('batch', 'seq')), may hold values from 0.5 to 1.5
- norm1_bias: bfloat16 [768], P(('batch', 'seq')), may hold values from -3 to 3
- qkv_weight: bfloat16 [768, 3, 768], P(('batch', 'seq'), None, 'heads'), may hold values from -0.21875 to 0.21875
- conv_kernel: bfloat16 [3, 12, 192], P(None, 'heads', ('batch', 'seq')), may hold values from -3 to 3
- out_weight: bfloat16 [768, 768], P('heads', ('batch', 'seq')), may hold values from -0.875 to 0.875
- norm2_gain: bfloat16 [768], P(('batch', 'seq')), may hold values from 0.5 to 1.5
- norm2_bias: bfloat16 [768], P(('batch', 'seq')), may hold values from -3 to 3
- inner_weight: bfloat16 [768, 3072], P(('batch', 'seq'), 'heads'), may hold values from -0.21875 to 0.21875
- outer_weight: bfloat16 [3072, 768], P('heads', ('batch', 'seq')), may hold values from -0.109375 to 0.109375
- cotangent: bfloat16 [4, 2, 1024, 768], P('batch', 'seq', 'heads'), may hold values from -6 to 6
Outputs:
- block_output: bfloat16 [4, 2, 1024, 768], P('batch', 'seq', 'heads')
- input_grad: float32 [4, 2, 1024, 768], P('batch', 'seq', 'heads')
- norm1_gain_grad: float32 [768], P(('batch', 'seq'))
- norm1_bias_grad: float32 [768], P(('batch', 'seq'))
- qkv_weight_grad: float32 [768, 3, 768], P(('batch', 'seq'), None, 'heads')
- conv_kernel_grad: float32 [3, 12, 192], P(None, 'heads', ('batch', 'seq'))
- out_weight_grad: float32 [768, 768], P('heads', ('batch', 'seq'))
- norm2_gain_grad: float32 [768], P(('batch', 'seq'))
- norm2_bias_grad: float32 [768], P(('batch', 'seq'))
- inner_weight_grad: float32 [768, 3072], P(('batch', 'seq'), 'heads')
- outer_weight_grad: float32 [3072, 768], P('heads', ('batch', 'seq'))
Inputs may be any that keep to these rules, and one draw needn't show every extreme that they name: `segment_ids`: in each sequence the ids never fall, every one of the 4 documents is present with 1 to 1536 tokens, and one document has exactly that many.
All inputs are finite; a program needn't handle non-finite values.
Results may differ from a plain program's by a relative error of at most 0.015.
Values may be sent and summed in bfloat16 or wider, within the bound.
No kernel may reach another device: no remote copies, remote signals or barrier semaphores. Data moves between devices by JAX's collectives and lax.ppermute only.
A program may use at most 128 MiB of HBM per device.

v0:
```python
import jax
import jax.numpy as jnp
from jax import lax
from jax.sharding import PartitionSpec as P

HEAD_DIM = 64
KERNEL = 3
QBLOCK = 512


epsilon = 1e-05
masked_score = -1e30


def from_behind(shard, axis, by):
    count = lax.axis_size(axis)
    pairs = [(i, i + by) for i in range(count) if 0 <= i + by < count]
    return lax.ppermute(shard, axis, pairs)


def layer_norm(values, scale_vec, shift_vec):
    average = jnp.mean(values, axis=-1, keepdims=True)
    centered = values - average
    inverse = lax.rsqrt(jnp.mean(centered * centered, axis=-1, keepdims=True) + epsilon)
    normal_form = centered * inverse
    return (normal_form * scale_vec + shift_vec, normal_form, inverse)


def norm_backward(grad_out, normal_form, inverse, scale_vec):
    scaled = grad_out * scale_vec
    grad_in = inverse * (
        scaled
        - jnp.mean(scaled, axis=-1, keepdims=True)
        - normal_form * jnp.mean(scaled * normal_form, axis=-1, keepdims=True)
    )
    return (grad_in, jnp.sum(grad_out * normal_form, axis=0), jnp.sum(grad_out, axis=0))


def depthwise(extended, conv_ids, tap_weights, count):
    kernel_len = tap_weights.shape[0]
    latest_ids = conv_ids[:, kernel_len - 1 : kernel_len - 1 + count]
    summed = jnp.zeros((extended.shape[0], count, extended.shape[2]), jnp.float32)
    for offset in range(kernel_len):
        first_row = kernel_len - 1 - offset
        same_doc = (conv_ids[:, first_row : first_row + count] == latest_ids).astype(jnp.float32)
        summed = (
            summed
            + tap_weights[offset]
            * extended[:, first_row : first_row + count].astype(jnp.float32)
            * same_doc[:, :, None]
        )
    return summed


def depthwise_back(mixed_grad, extended, conv_ids, tap_weights, count):
    kernel_len = tap_weights.shape[0]
    latest_ids = conv_ids[:, kernel_len - 1 : kernel_len - 1 + count]
    grad_float = mixed_grad.astype(jnp.float32)
    ext_grad = jnp.zeros(
        (mixed_grad.shape[0], count + kernel_len - 1, mixed_grad.shape[2]), jnp.float32
    )
    tap_grads = []
    for offset in range(kernel_len):
        first_row = kernel_len - 1 - offset
        same_doc = (conv_ids[:, first_row : first_row + count] == latest_ids).astype(jnp.float32)
        kept_grad = grad_float * same_doc[:, :, None]
        ext_grad = ext_grad + jnp.pad(
            tap_weights[offset] * kept_grad,
            ((0, 0), (first_row, kernel_len - 1 - first_row), (0, 0)),
        )
        tap_grads.append(
            jnp.sum(
                kept_grad * extended[:, first_row : first_row + count].astype(jnp.float32),
                axis=(0, 1),
            )
        )
    return (ext_grad, jnp.stack(tap_grads))


def block_scores(query_block, key_rows, block_ids, key_ids, block_start, half_len):
    scores = jnp.einsum(
        "qhd,khd->hqk", query_block, key_rows, preferred_element_type=jnp.float32
    ) * HEAD_DIM ** (-0.5)
    query_pos = block_start + jnp.arange(query_block.shape[0])
    key_pos = jnp.arange(key_rows.shape[0])
    allowed = (key_pos[None, :] <= query_pos[:, None] + half_len) & (
        key_ids[None, :] == block_ids[:, None]
    )
    return jnp.where(allowed[None], scores, masked_score)


def on_device(
    block_input,
    segment_ids,
    norm1_gain,
    norm1_bias,
    qkv_weight,
    conv_kernel,
    out_weight,
    norm2_gain,
    norm2_bias,
    inner_weight,
    outer_weight,
    cotangent,
):
    (
        gain_one,
        bias_one,
        qkv_full,
        kernel_full,
        proj_full,
        gain_two,
        bias_two,
        inner_full,
        outer_full,
    ) = (
        lax.all_gather(norm1_gain, ("batch", "seq"), axis=0, tiled=True),
        lax.all_gather(norm1_bias, ("batch", "seq"), axis=0, tiled=True),
        lax.all_gather(qkv_weight, ("batch", "seq"), axis=0, tiled=True),
        lax.all_gather(conv_kernel, ("batch", "seq"), axis=2, tiled=True),
        lax.all_gather(out_weight, ("batch", "seq"), axis=1, tiled=True),
        lax.all_gather(norm2_gain, ("batch", "seq"), axis=0, tiled=True),
        lax.all_gather(norm2_bias, ("batch", "seq"), axis=0, tiled=True),
        lax.all_gather(inner_weight, ("batch", "seq"), axis=0, tiled=True),
        lax.all_gather(outer_weight, ("batch", "seq"), axis=1, tiled=True),
    )
    seqs_here = block_input.shape[0]
    quarter_len = block_input.shape[2]
    half_len = quarter_len * lax.axis_size("heads")
    model_width = qkv_full.shape[0]
    local_width = qkv_full.shape[2]
    heads_here = kernel_full.shape[1]
    kernel_len = KERNEL
    halo_rows = kernel_len - 1
    row_count = seqs_here * half_len
    own_count = seqs_here * quarter_len
    channels = 3 * local_width
    block_rows = QBLOCK
    block_count = half_len // block_rows
    score_scale = HEAD_DIM ** (-0.5)
    gain_one = gain_one.astype(jnp.float32)
    bias_one = bias_one.astype(jnp.float32)
    gain_two = gain_two.astype(jnp.float32)
    bias_two = bias_two.astype(jnp.float32)
    tap_weights = (
        kernel_full.astype(jnp.float32)
        .reshape(3, local_width, kernel_len)
        .transpose(2, 0, 1)
        .reshape(kernel_len, channels)
    )
    qkv_matrix = qkv_full.reshape(model_width, channels)
    row_shape = (seqs_here, 1, half_len, model_width)
    own_shape = (seqs_here, 1, quarter_len, model_width)
    seq_pos = lax.axis_index("seq")
    head_pos = lax.axis_index("heads")

    def own_rows(values):
        shaped = values.reshape(seqs_here, half_len, values.shape[-1])
        return lax.dynamic_slice_in_dim(shaped, head_pos * quarter_len, quarter_len, 1).reshape(
            own_count, values.shape[-1]
        )

    padded_ids = jnp.concatenate(
        [jnp.full((seqs_here, half_len), -1, jnp.int32), segment_ids], axis=1
    )
    key_ids = lax.dynamic_slice_in_dim(padded_ids, seq_pos * half_len, 2 * half_len, 1)
    query_ids = key_ids[:, half_len:]
    conv_ids = key_ids[:, half_len - halo_rows :]
    whole_input = lax.all_gather(block_input, "heads", axis=2, tiled=True)
    flat_input = whole_input.reshape(row_count, model_width).astype(jnp.float32)
    normed_one, form_one, inverse_one = layer_norm(flat_input, gain_one, bias_one)
    normed_one = normed_one.astype(jnp.bfloat16)
    projected = jnp.dot(normed_one, qkv_matrix, preferred_element_type=jnp.float32).astype(
        jnp.bfloat16
    )
    projected = projected.reshape(seqs_here, half_len, channels)
    zero_halo = jnp.zeros((seqs_here, halo_rows, channels), jnp.bfloat16)
    base_conv = depthwise(
        jnp.concatenate([zero_halo, projected], axis=1), conv_ids, tap_weights, half_len
    )
    sent_keys = base_conv[:, :, local_width:].astype(jnp.bfloat16)
    halo_in, remote_keys = from_behind((projected[:, half_len - halo_rows :], sent_keys), "seq", 1)
    extended = jnp.concatenate([halo_in, projected], axis=1)
    head_conv = depthwise(
        extended[:, : 2 * halo_rows], conv_ids[:, : 2 * halo_rows], tap_weights, halo_rows
    )
    mixed_rows = jnp.concatenate([head_conv, base_conv[:, halo_rows:]], axis=1).astype(jnp.bfloat16)
    head_shape = (seqs_here, half_len, heads_here, HEAD_DIM)
    query_heads = mixed_rows[:, :, :local_width].reshape(head_shape)
    key_heads = jnp.concatenate(
        [remote_keys[:, :, :local_width], mixed_rows[:, :, local_width : 2 * local_width]], axis=1
    )
    key_heads = key_heads.reshape(seqs_here, 2 * half_len, heads_here, HEAD_DIM)
    value_heads = jnp.concatenate(
        [remote_keys[:, :, local_width:], mixed_rows[:, :, 2 * local_width :]], axis=1
    )
    value_heads = value_heads.reshape(seqs_here, 2 * half_len, heads_here, HEAD_DIM)

    def forward_block(flat_index):
        seq_number = flat_index // block_count
        block_start = flat_index % block_count * block_rows
        query_block = lax.dynamic_slice_in_dim(query_heads[seq_number], block_start, block_rows, 0)
        block_ids = lax.dynamic_slice_in_dim(query_ids[seq_number], block_start, block_rows, 0)
        scores = block_scores(
            query_block,
            key_heads[seq_number],
            block_ids,
            key_ids[seq_number],
            block_start,
            half_len,
        )
        row_peak = jnp.max(scores, axis=-1, keepdims=True)
        log_total = row_peak + jnp.log(jnp.sum(jnp.exp(scores - row_peak), axis=-1, keepdims=True))
        soft_weights = jnp.exp(scores - log_total).astype(jnp.bfloat16)
        attended = jnp.einsum(
            "hqk,khd->qhd",
            soft_weights,
            value_heads[seq_number],
            preferred_element_type=jnp.float32,
        )
        return (attended.astype(jnp.bfloat16), log_total)

    attended_blocks, log_totals = lax.map(forward_block, jnp.arange(seqs_here * block_count))
    attended = attended_blocks.reshape(row_count, local_width)
    partial_attn = jnp.dot(attended, proj_full, preferred_element_type=jnp.float32)
    attn_part = lax.psum_scatter(
        partial_attn.reshape(row_shape), "heads", scatter_dimension=2, tiled=True
    )
    middle_part = block_input.astype(jnp.float32) + attn_part
    middle = lax.all_gather(middle_part, "heads", axis=2, tiled=True).reshape(
        row_count, model_width
    )
    normed_two, form_two, inverse_two = layer_norm(middle, gain_two, bias_two)
    normed_two = normed_two.astype(jnp.bfloat16)
    inner_act = jnp.dot(normed_two, inner_full, preferred_element_type=jnp.float32)
    relu_act = jnp.maximum(inner_act, 0.0)
    squared = (relu_act * relu_act).astype(jnp.bfloat16)
    ffn_part = jnp.dot(squared, outer_full, preferred_element_type=jnp.float32).reshape(row_shape)
    ffn_out = lax.psum_scatter(ffn_part, "heads", scatter_dimension=2, tiled=True)
    middle_local = lax.dynamic_slice_in_dim(
        middle.reshape(row_shape), head_pos * quarter_len, quarter_len, 2
    )
    block_output = (middle_local + ffn_out).astype(jnp.bfloat16)
    grad_full = lax.all_gather(cotangent, "heads", axis=2, tiled=True).reshape(
        row_count, model_width
    )
    outer_grad = jnp.einsum("rf,rd->fd", squared, grad_full, preferred_element_type=jnp.float32)
    act_grad = jnp.einsum("rd,fd->rf", grad_full, outer_full, preferred_element_type=jnp.float32)
    inner_grad_act = (act_grad * 2.0 * relu_act).astype(jnp.bfloat16)
    inner_grad = jnp.einsum(
        "rd,rf->df", normed_two, inner_grad_act, preferred_element_type=jnp.float32
    )
    norm_two_part = jnp.einsum(
        "rf,df->rd", inner_grad_act, inner_full, preferred_element_type=jnp.float32
    )
    norm_two_own = lax.psum_scatter(
        norm_two_part.reshape(row_shape), "heads", scatter_dimension=2, tiled=True
    ).reshape(own_count, model_width)
    middle_back, gain_two_grad, bias_two_grad = norm_backward(
        norm_two_own, own_rows(form_two), own_rows(inverse_two), gain_two
    )
    middle_grad_own = cotangent.reshape(own_count, model_width).astype(jnp.float32) + middle_back
    branch_grad = lax.all_gather(
        middle_grad_own.astype(jnp.bfloat16).reshape(own_shape), "heads", axis=2, tiled=True
    )
    branch_grad = branch_grad.reshape(row_count, model_width)
    proj_grad = jnp.einsum("rj,rd->jd", attended, branch_grad, preferred_element_type=jnp.float32)
    attended_grad = jnp.einsum(
        "rd,jd->rj", branch_grad, proj_full, preferred_element_type=jnp.float32
    )
    attended_grad = attended_grad.astype(jnp.bfloat16).reshape(head_shape)

    def sequence_backward(seq_number):
        key_rows = key_heads[seq_number]
        value_rows = value_heads[seq_number]

        def block_step(carry, block_number):
            key_acc, value_acc = carry
            block_start = block_number * block_rows
            query_block = lax.dynamic_slice_in_dim(
                query_heads[seq_number], block_start, block_rows, 0
            )
            grad_block = lax.dynamic_slice_in_dim(
                attended_grad[seq_number], block_start, block_rows, 0
            )
            block_ids = lax.dynamic_slice_in_dim(query_ids[seq_number], block_start, block_rows, 0)
            scores = block_scores(
                query_block, key_rows, block_ids, key_ids[seq_number], block_start, half_len
            )
            soft_weights = jnp.exp(scores - log_totals[seq_number * block_count + block_number])
            grad_weights = jnp.einsum(
                "qhd,khd->hqk", grad_block, value_rows, preferred_element_type=jnp.float32
            )
            row_dot = jnp.sum(soft_weights * grad_weights, axis=-1, keepdims=True)
            score_grad = (soft_weights * (grad_weights - row_dot)).astype(jnp.bfloat16)
            query_grad = (
                jnp.einsum("hqk,khd->qhd", score_grad, key_rows, preferred_element_type=jnp.float32)
                * score_scale
            )
            key_acc = (
                key_acc
                + jnp.einsum(
                    "hqk,qhd->khd", score_grad, query_block, preferred_element_type=jnp.float32
                )
                * score_scale
            )
            value_acc = value_acc + jnp.einsum(
                "hqk,qhd->khd",
                soft_weights.astype(jnp.bfloat16),
                grad_block,
                preferred_element_type=jnp.float32,
            )
            return ((key_acc, value_acc), query_grad)

        empty_keys = jnp.zeros((2 * half_len, heads_here, HEAD_DIM), jnp.float32)
        (key_acc, value_acc), query_grads = lax.scan(
            block_step, (empty_keys, empty_keys), jnp.arange(block_count)
        )
        return (
            query_grads.reshape(half_len, local_width),
            key_acc.reshape(2 * half_len, local_width),
            value_acc.reshape(2 * half_len, local_width),
        )

    query_grad, key_grad, value_grad = lax.map(sequence_backward, jnp.arange(seqs_here))
    own_grad = jnp.concatenate(
        [query_grad, key_grad[:, half_len:], value_grad[:, half_len:]], axis=2
    )
    remote_grad = jnp.concatenate([key_grad[:, :half_len], value_grad[:, :half_len]], axis=2)
    front_grad, unused_taps = depthwise_back(
        own_grad[:, :halo_rows].astype(jnp.bfloat16),
        extended[:, : 2 * halo_rows],
        conv_ids[:, : 2 * halo_rows],
        tap_weights,
        halo_rows,
    )
    received_keys, received_halo = from_behind((remote_grad, front_grad[:, :halo_rows]), "seq", -1)
    mixed_grad = own_grad + jnp.concatenate([jnp.zeros_like(query_grad), received_keys], axis=2)
    mixed_grad = mixed_grad.astype(jnp.bfloat16)
    ext_grad, tap_grad = depthwise_back(mixed_grad, extended, conv_ids, tap_weights, half_len)
    tail_grad = jnp.concatenate(
        [jnp.zeros((seqs_here, half_len - halo_rows, channels), jnp.float32), received_halo], axis=1
    )
    projected_grad = (
        (ext_grad[:, halo_rows:] + tail_grad).astype(jnp.bfloat16).reshape(row_count, channels)
    )
    qkv_grad = jnp.einsum(
        "rd,rc->dc", normed_one, projected_grad, preferred_element_type=jnp.float32
    )
    qkv_grad = qkv_grad.reshape(model_width, 3, local_width)
    kernel_grad = (
        tap_grad.reshape(kernel_len, 3, local_width)
        .transpose(1, 2, 0)
        .reshape(3, heads_here, HEAD_DIM * kernel_len)
    )
    norm_one_part = jnp.einsum(
        "rc,dc->rd", projected_grad, qkv_matrix, preferred_element_type=jnp.float32
    )
    norm_one_own = lax.psum_scatter(
        norm_one_part.reshape(row_shape), "heads", scatter_dimension=2, tiled=True
    ).reshape(own_count, model_width)
    input_back, gain_one_grad, bias_one_grad = norm_backward(
        norm_one_own, own_rows(form_one), own_rows(inverse_one), gain_one
    )
    input_grad = (middle_grad_own + input_back).reshape(own_shape)
    gain_one_grad, bias_one_grad, gain_two_grad, bias_two_grad = lax.psum(
        (gain_one_grad, bias_one_grad, gain_two_grad, bias_two_grad), "heads"
    )
    (
        gain_one_out,
        bias_one_out,
        qkv_out,
        kernel_out,
        proj_out,
        gain_two_out,
        bias_two_out,
        inner_out,
        outer_out,
    ) = (
        lax.psum_scatter(gain_one_grad, ("batch", "seq"), scatter_dimension=0, tiled=True),
        lax.psum_scatter(bias_one_grad, ("batch", "seq"), scatter_dimension=0, tiled=True),
        lax.psum_scatter(qkv_grad, ("batch", "seq"), scatter_dimension=0, tiled=True),
        lax.psum_scatter(kernel_grad, ("batch", "seq"), scatter_dimension=2, tiled=True),
        lax.psum_scatter(proj_grad, ("batch", "seq"), scatter_dimension=1, tiled=True),
        lax.psum_scatter(gain_two_grad, ("batch", "seq"), scatter_dimension=0, tiled=True),
        lax.psum_scatter(bias_two_grad, ("batch", "seq"), scatter_dimension=0, tiled=True),
        lax.psum_scatter(inner_grad, ("batch", "seq"), scatter_dimension=0, tiled=True),
        lax.psum_scatter(outer_grad, ("batch", "seq"), scatter_dimension=1, tiled=True),
    )
    return (
        block_output,
        input_grad,
        gain_one_out,
        bias_one_out,
        qkv_out,
        kernel_out,
        proj_out,
        gain_two_out,
        bias_two_out,
        inner_out,
        outer_out,
    )


def solution(mesh):
    return jax.shard_map(
        on_device,
        mesh=mesh,
        in_specs=(
            P("batch", "seq", "heads", None),
            P("batch", None),
            P(("batch", "seq")),
            P(("batch", "seq")),
            P(("batch", "seq"), None, "heads"),
            P(None, "heads", ("batch", "seq")),
            P("heads", ("batch", "seq")),
            P(("batch", "seq")),
            P(("batch", "seq")),
            P(("batch", "seq"), "heads"),
            P("heads", ("batch", "seq")),
            P("batch", "seq", "heads", None),
        ),
        out_specs=(
            P("batch", "seq", "heads", None),
            P("batch", "seq", "heads", None),
            P(("batch", "seq")),
            P(("batch", "seq")),
            P(("batch", "seq"), None, "heads"),
            P(None, "heads", ("batch", "seq")),
            P("heads", ("batch", "seq")),
            P(("batch", "seq")),
            P(("batch", "seq")),
            P(("batch", "seq"), "heads"),
            P("heads", ("batch", "seq")),
        ),
        check_vma=False,
    )
```

profile of v0, /device:TPU:0, one launch (start us, length us, event | category | flops | bytes accessed | tf_op | source)
XLA Modules:
  0.0 894.2 jit_solution(3658308277831252649)
XLA Ops:
  13.3 23.4 %all-reduce.21 = (bf16[768]{0:T(1024)(128)(2,1)S(1)}, bf16[768]{0:T(1024)(128)(2,1)S(1)}, bf16[768]{0:T(1024)(128)(2,1)S(1)}, bf16[768]{0:T(1024)(128)(2,1)S(1)}) all-reduce(bf16[768]{0:T(1024)(128)(2,1)S(1)} %dynamic-update-slice.1, ...), channel_id=1, replica_groups=mesh['batch'=4,'heads'=4,'seq'=2] {'batch','seq'}, use_global_device_ids=true, to_apply=%add.11 | all-reduce | flops 3072 | bytes 12288
  38.4 30.8 %all_gather.39 = bf16[3,3,192]{1,0,2:T(4,128)(2,1)S(1)} all-gather(bf16[3,3,24]{1,0,2:T(4,128)(2,1)S(1)} %copy.58), channel_id=1, replica_groups=mesh['batch'=4,'heads'=4,'seq'=2] {'batch','seq'}, dimensions={2}, use_global_device_ids=true | all-gather | bytes 3888 | tf_op jit(solution)/shard_map/all_gather | solution.py:120
  71.5 35.1 %all_gather.43 = bf16[768,3,192]{2,1,0:T(4,128)(2,1)S(1)} all-gather(bf16[96,3,192]{2,1,0:T(4,128)(2,1)S(1)} %copy.60), channel_id=1, replica_groups=mesh['batch'=4,'heads'=4,'seq'=2] {'batch','seq'}, dimensions={0}, use_global_device_ids=true | all-gather | bytes 995328 | tf_op jit(solution)/shard_map/all_gather | solution.py:119
  120.5 36.9 %all_gather.44 = bf16[192,768]{0,1:T(8,128)(2,1)} all-gather(bf16[192,96]{0,1:T(8,128)(2,1)S(1)} %copy.67), channel_id=1, replica_groups=mesh['batch'=4,'heads'=4,'seq'=2] {'batch','seq'}, dimensions={1}, use_global_device_ids=true | all-gather | bytes 331776 | tf_op jit(solution)/shard_map/all_gather | solution.py:121
  170.9 45.6 %while.43 = (s32[]{:T(128)}, bf16[2,512,3,64]{1,3,2,0:T(8,128)(2,1)S(1)}, f32[2,3,512,1]{2,1,3,0:T(4,128)S(1)}, s32[2]{0:T(128)S(1)}, s32[1,2048]{1,0:T(1,128)S(...) while((s32[]{:T(128)}, ...), condition=%wide.region_5.6_spmd, body=%wide.region_2.5_spmd.sunk | while | flops 843152896 | bytes 43987272 | solution.py:223
  174.5 5.9 fusion.134
  180.5 6.8 exponential_reduce_fusion.2
  187.2 6.5 fusion.135
  197.3 5.9 fusion.134
  203.3 6.8 exponential_reduce_fusion.2
  210.1 6.5 fusion.135
  221.1 39.0 %reduce-scatter.12.cloned.1.call-done = f32[1,1,256,768]{3,2,1,0:T(8,128)} async-done(((f32[1,1,1024,768]{3,2,1,0:T(8,128)}), f32[1,1,256,768]{3,2,1,0:T(8,128)}) %reduce-scatter.12.cloned.1.call-update) | async-done | bytes 786448 | tf_op jit(solution)/shard_map/reduce_scatter | solution.py:226
  264.4 26.4 %all-gather.10.cloned.1.call-done = f32[1,1,1024,768]{3,2,1,0:T(8,128)} async-done(((f32[1,1,256,768]{3,2,1,0:T(8,128)}), f32[1,1,1024,768]{3,2,1,0:T(8,128)}) %all-gather.10.cloned.1.call-update) | async-done | bytes 3145744 | tf_op jit(solution)/shard_map/all_gather | solution.py:230
  297.8 36.2 %all-gather.12.cloned.1.call-done = bf16[768,768]{1,0:T(8,128)(2,1)} async-done(((bf16[96,768]{1,0:T(8,128)(2,1)}), bf16[768,768]{1,0:T(8,128)(2,1)}) %all-gather.12.cloned.1.call-update) | async-done | bytes 1179664 | tf_op jit(solution)/shard_map/all_gather | solution.py:124
  339.4 36.5 %all-gather.14.cloned.1.call-done = bf16[768,768]{0,1:T(8,128)(2,1)} async-done(((bf16[768,96]{0,1:T(8,128)(2,1)}), bf16[768,768]{0,1:T(8,128)(2,1)}) %all-gather.14.cloned.1.call-update) | async-done | bytes 1179664 | tf_op jit(solution)/shard_map/all_gather | solution.py:125
  375.9 19.8 %all-gather.16.cloned.1.call-done = bf16[1,1,1024,768]{3,2,1,0:T(8,128)(2,1)} async-done(((bf16[1,1,256,768]{3,2,1,0:T(8,128)(2,1)}), bf16[1,1,1024,768]{3,2,1,0:T(8,128)(2,1)}) %all-gather.16.cloned.1.call-update) | async-done | bytes 1572880 | tf_op jit(solution)/shard_map/all_gather | solution.py:244
  404.4 37.9 %reduce-scatter.16.cloned.1.call-done = f32[1,1,256,768]{3,2,1,0:T(8,128)} async-done(((f32[1,1,1024,768]{3,2,1,0:T(8,128)}), f32[1,1,256,768]{3,2,1,0:T(8,128)}) %reduce-scatter.16.cloned.1.call-update) | async-done | bytes 786448 | tf_op jit(solution)/shard_map/reduce_scatter | solution.py:256
  452.7 14.3 %all-gather.18.cloned.1.call-done = bf16[1024,768]{1,0:T(8,128)(2,1)} async-done(((bf16[256,768]{1,0:T(8,128)(2,1)}), bf16[1024,768]{1,0:T(8,128)(2,1)}) %all-gather.18.cloned.1.call-update) | async-done | bytes 1572880 | tf_op jit(solution)/shard_map/all_gather | solution.py:263
  469.8 75.4 %while.44 = (s32[]{:T(128)}, f32[2048,3,64]{0,2,1:T(8,128)}, f32[2048,3,64]{0,2,1:T(8,128)}, f32[2,512,3,64]{1,0,3,2:T(2,128)}, s32[2]{0:T(128)S(1)}, /*index=5*...) while((s32[]{:T(128)}, f32[2048,3,64]{0,2,1:T(8,128)}, ...), condition=%wide.region_15.16_spmd.clone, body=%wide.region_13.15_spmd.clone.sunk | while | flops 2065661440 | bytes 158265872 | solution.py:316
  476.2 5.7 fusion.148
  481.9 5.8 multiply_reduce_fusion.6
  487.7 6.1 multiply_convert_fusion.6
  512.7 6.2 fusion.148
  518.9 5.8 multiply_reduce_fusion.6
  524.7 6.1 multiply_convert_fusion.6
  562.6 30.8 %collective-permute-done.2 = f32[1,1024,384]{2,1,0:T(8,128)} collective-permute-done((f32[1,1024,384]{2,1,0:T(8,128)}, f32[1,1024,384]{2,1,0:T(8,128)}, u32[]{:S(2)}, u32[]{:S(2)}) %collective-permute-start.2) | collective-permute-done | bytes 1572896 | tf_op jit(solution)/shard_map/ppermute | solution.py:18
  630.6 37.2 %reduce-scatter.18.cloned.1.call-done = f32[1,1,256,768]{3,2,1,0:T(8,128)} async-done(((f32[1,1,1024,768]{3,2,1,0:T(8,128)}), f32[1,1,256,768]{3,2,1,0:T(8,128)}) %reduce-scatter.18.cloned.1.call-update) | async-done | bytes 786448 | tf_op jit(solution)/shard_map/reduce_scatter | solution.py:359
  670.5 37.3 %all-reduce.19 = (f32[768]{0:T(1024)S(1)}, f32[768]{0:T(1024)S(1)}, f32[3,3,192]{2,1,0:T(4,128)S(1)}, f32[768]{0:T(1024)S(1)}, f32[768]{0:T(1024)S(1)}) all-reduce(f32[768]{0:T(1024)S(1)} %get-tuple-element.413, f32[768]{0:T(1024)S(1)} %reduce_sum.169, ...), channel_id=7, replica_groups=mesh['batch'=4,'heads'=4,'seq'=2] {'batch','seq'}, use_global_device_ids=true, to_apply=%region_21.22.clone | all-reduce | flops 4800 | bytes 38400
  708.1 6.1 all-reduce.20
  717.4 24.2 %reduce-scatter.24.cloned.1.call-done = f32[768,96]{0,1:T(8,128)} async-done(((f32[768,768]{0,1:T(8,128)}), f32[768,96]{0,1:T(8,128)}) %reduce-scatter.24.cloned.1.call-update) | async-done | bytes 294928 | tf_op jit(solution)/shard_map/reduce_scatter | solution.py:388
  741.6 72.9 %reduce-scatter.22.cloned.1.call-done = f32[96,768]{1,0:T(8,128)} async-done(((f32[768,768]{1,0:T(8,128)}), f32[96,768]{1,0:T(8,128)}) %reduce-scatter.22.cloned.1.call-update) | async-done | bytes 294928 | tf_op jit(solution)/shard_map/reduce_scatter | solution.py:387
  814.5 72.8 %reduce-scatter.20.cloned.1.call-done = f32[96,3,192]{2,0,1:T(8,128)} async-done(((f32[768,3,192]{2,0,1:T(8,128)}), f32[96,3,192]{2,0,1:T(8,128)}) %reduce-scatter.20.cloned.1.call-update) | async-done | bytes 221200 | tf_op jit(solution)/shard_map/reduce_scatter | solution.py:382
  (313 shorter events, 175.4 us)
Async XLA Ops:
  7.2 100.6 %all-gather.8.cloned.1.call-start = ((), (), s32[]{:S(2)}) async-start(), calls=%async_computation.8 | async-start | bytes 1966080 | tf_op jit(solution)/shard_map/all_gather | solution.py:169
  7.9 252.2 %reduce-scatter.12.cloned.1.call-start = ((), (), s32[]{:S(2)}) async-start(), calls=%async_computation.9 | async-start | bytes 3932160 | tf_op jit(solution)/shard_map/reduce_scatter | solution.py:226
  36.7 75.3 %copy-start.54 = (f32[768]{0:T(1024)}, f32[768]{0:T(1024)S(1)}, u32[]{:S(2)}) copy-start(f32[768]{0:T(1024)S(1)} %convert_element_type.174) | copy-start | bytes 9220
  36.7 75.2 %copy-start.39 = (f32[768]{0:T(1024)}, f32[768]{0:T(1024)S(1)}, u32[]{:S(2)}) copy-start(f32[768]{0:T(1024)S(1)} %convert_element_type.173) | copy-start | bytes 9220
  70.7 36.8 %copy-start.28 = (s32[1,2048]{1,0:T(1,128)S(1)}, s32[1,2048]{1,0:T(1,128)}, u32[]{:S(2)}) copy-start(s32[1,2048]{1,0:T(1,128)} %param.17) | copy-start | bytes 24580
  71.4 92.3 %copy-start.29 = (f32[576]{0:T(1024)}, f32[576]{0:T(1024)S(1)}, u32[]{:S(2)}) copy-start(f32[576]{0:T(1024)S(1)} %mul.385) | copy-start | bytes 6916
  71.4 92.3 %copy-start.31 = (f32[576]{0:T(1024)}, f32[576]{0:T(1024)S(1)}, u32[]{:S(2)}) copy-start(f32[576]{0:T(1024)S(1)} %mul.400) | copy-start | bytes 6916
  71.5 92.2 %copy-start.33 = (f32[576]{0:T(1024)}, f32[576]{0:T(1024)S(1)}, u32[]{:S(2)}) copy-start(f32[576]{0:T(1024)S(1)} %mul.393) | copy-start | bytes 6916
  113.7 50.0 %copy-start.7 = (bf16[1024,576]{1,0:T(8,128)(2,1)}, bf16[1024,576]{1,0:T(8,128)(2,1)S(1)}, u32[]{:S(2)}) copy-start(bf16[1024,576]{1,0:T(8,128)(2,1)S(1)} %convolution_convert_fusion) | copy-start | bytes 3538948
  117.5 47.0 %collective-permute-start.1 = (bf16[1,1024,384]{2,1,0:T(8,128)(2,1)}, bf16[1,1024,384]{2,1,0:T(8,128)(2,1)}, u32[]{:S(2)}, u32[]{:S(2)}) collective-permute-start(bf16[1,1024,384]{2,1,0:T(8,128)(2,1)} %slice.170), channel_id=1, source_target_pairs={{0,1},{2,3},{4,5},{6,7},{8,9},{10,11},{12,13},{14,15},{16,17},{18,... | collective-permute-start | bytes 2359304 | tf_op jit(solution)/shard_map/ppermute | solution.py:18
  157.4 6.2 collective-permute-start
  170.9 47.8 %copy-start.16 = (bf16[192,768]{0,1:T(8,128)(2,1)S(1)}, bf16[192,768]{0,1:T(8,128)(2,1)}, u32[]{:S(2)}) copy-start(bf16[192,768]{0,1:T(8,128)(2,1)} %all_gather.44) | copy-start | bytes 884740
  218.8 41.3 %copy-start.19 = (bf16[1,1,256,768]{3,2,1,0:T(8,128)(2,1)S(1)}, bf16[1,1,256,768]{3,2,1,0:T(8,128)(2,1)}, u32[]{:S(2)}) copy-start(bf16[1,1,256,768]{3,2,1,0:T(8,128)(2,1)} %param.16) | copy-start | bytes 1179652
  221.1 69.8 %all-gather.10.cloned.1.call-start = ((), (), s32[]{:S(2)}) async-start(), calls=%async_computation.10 | async-start | bytes 3932160 | tf_op jit(solution)/shard_map/all_gather | solution.py:230
  262.2 71.8 %all-gather.12.cloned.1.call-start = ((), (), s32[]{:S(2)}) async-start(), calls=%async_computation.11 | async-start | bytes 1327104 | tf_op jit(solution)/shard_map/all_gather | solution.py:124
  262.8 113.1 %all-gather.14.cloned.1.call-start = ((), (), s32[]{:S(2)}) async-start(), calls=%async_computation.12 | async-start | bytes 1327104 | tf_op jit(solution)/shard_map/all_gather | solution.py:125
  263.4 132.3 %all-gather.16.cloned.1.call-start = ((), (), s32[]{:S(2)}) async-start(), calls=%async_computation.14 | async-start | bytes 1966080 | tf_op jit(solution)/shard_map/all_gather | solution.py:244
  263.9 178.4 %reduce-scatter.16.cloned.1.call-start = ((), (), s32[]{:S(2)}) async-start(), calls=%async_computation.15 | async-start | bytes 3932160 | tf_op jit(solution)/shard_map/reduce_scatter | solution.py:256
  264.4 180.2 %copy-start.41 = (f32[768]{0:T(1024)}, f32[768]{0:T(1024)S(1)}, u32[]{:S(2)}) copy-start(f32[768]{0:T(1024)S(1)} %convert_element_type.184) | copy-start | bytes 9220
  264.4 69.6 %copy-start.56 = (f32[768]{0:T(1024)}, f32[768]{0:T(1024)S(1)}, u32[]{:S(2)}) copy-start(f32[768]{0:T(1024)S(1)} %convert_element_type.185) | copy-start | bytes 9220
  404.2 40.3 %copy-start.20 = (bf16[1,1,256,768]{3,2,1,0:T(8,128)(2,1)S(1)}, bf16[1,1,256,768]{3,2,1,0:T(8,128)(2,1)}, u32[]{:S(2)}) copy-start(bf16[1,1,256,768]{3,2,1,0:T(8,128)(2,1)} %param.27) | copy-start | bytes 1179652
  404.3 62.7 %all-gather.18.cloned.1.call-start = ((), (), s32[]{:S(2)}) async-start(), calls=%async_computation.20 | async-start | bytes 1966080 | tf_op jit(solution)/shard_map/all_gather | solution.py:263
  447.2 178.8 %reduce-scatter.14.cloned.1.call-start = ((), (), s32[]{:S(2)}) async-start(), calls=%async_computation.13 | async-start | bytes 3932160 | tf_op jit(solution)/shard_map/reduce_scatter | solution.py:239
  452.6 175.7 %reduce-scatter.26.cloned.1.call-start = ((), (), s32[]{:S(2)}) async-start(), calls=%async_computation.21 | async-start | bytes 884736
  552.3 41.1 %collective-permute-start.2 = (f32[1,1024,384]{2,1,0:T(8,128)}, f32[1,1024,384]{2,1,0:T(8,128)}, u32[]{:S(2)}, u32[]{:S(2)}) collective-permute-start(f32[1,1024,384]{2,1,0:T(8,128)} %pad_maximum_fusion.1), channel_id=1, source_target_pairs={{1,0},{3,2},{5,4},{7,6},{9,8},{11,10},{13,12},{15,14},{17,16},{19,... | collective-permute-start | bytes 4718600 | tf_op jit(solution)/shard_map/ppermute | solution.py:18
  562.5 105.2 %reduce-scatter.18.cloned.1.call-start = ((), (), s32[]{:S(2)}) async-start(), calls=%async_computation.16 | async-start | bytes 3932160 | tf_op jit(solution)/shard_map/reduce_scatter | solution.py:359
  597.5 5.5 collective-permute-start.3
  607.9 133.7 %reduce-scatter.24.cloned.1.call-start = ((), (), s32[]{:S(2)}) async-start(), calls=%async_computation.19 | async-start | bytes 2654208 | tf_op jit(solution)/shard_map/reduce_scatter | solution.py:388
  613.3 201.2 %reduce-scatter.22.cloned.1.call-start = ((), (), s32[]{:S(2)}) async-start(), calls=%async_computation.18 | async-start | bytes 2654208 | tf_op jit(solution)/shard_map/reduce_scatter | solution.py:387
  617.7 269.5 %reduce-scatter.20.cloned.1.call-start = ((), (), s32[]{:S(2)}) async-start(), calls=%async_computation.17 | async-start | bytes 2654208 | tf_op jit(solution)/shard_map/reduce_scatter | solution.py:382
  623.0 45.9 %copy-start.11 = (f32[1024,768]{1,0:T(8,128)S(1)}, f32[1024,768]{1,0:T(8,128)}, u32[]{:S(2)}) copy-start(f32[1024,768]{1,0:T(8,128)} %get-tuple-element.495) | copy-start | bytes 9437188
  626.0 44.5 %copy-start.43 = (f32[768]{0:T(1024)S(1)}, f32[768]{0:T(1024)}, u32[]{:S(2)}) copy-start(f32[768]{0:T(1024)} %get-tuple-element.415) | copy-start | bytes 9220
  (54 other events, 490.1 us)
Sparse Core Ops, SparseCore 0:
  9.5 22.3 all-gather.7
  221.2 38.8 reduce-scatter.11
  262.3 28.4 all-gather.9
  292.9 41.1 all-gather.11
  336.1 39.7 all-gather.13
  377.3 18.3 all-gather.15
  404.4 37.8 reduce-scatter.15
  447.3 19.6 all-gather.17
  469.5 37.8 reduce-scatter.13
  562.6 65.6 reduce-scatter.25
  630.9 36.8 reduce-scatter.17
  671.7 69.8 reduce-scatter.23
  745.7 68.7 reduce-scatter.21
  818.4 68.8 reduce-scatter.19
where the time goes:
time: 901 us; the launch traced here: 894 us
  waiting for transfers between devices  454 us (50%)
  blocking collectives  170 us (19%)
  matrix products  111 us (12%)
  other arithmetic  67.1 us (7%)
  local copies, waits for them, and re-layouts  54 us (6%)
  between operations  17.6 us (2%)
  starting transfers between devices  11 us (1%)
  loops' own time  9.65 us (1%)
    reduce_scatter x1, waiting for transfers between devices, on_device(): lax.psum_scatter(inner_grad, ('batch', 'seq'), scatter_dimension=0, tiled...  72.9 us
    reduce_scatter x1, waiting for transfers between devices, on_device(): lax.psum_scatter(qkv_grad, ('batch', 'seq'), scatter_dimension=0, tiled=T...  72.8 us
    unnamed x2, blocking collectives  60.7 us
    reduce_scatter x1, waiting for transfers between devices, on_device(): lax.psum_scatter(partial_attn.reshape(row_shape), 'heads', scatter_dimens...  39 us
    reduce_scatter x1, waiting for transfers between devices, on_device(): lax.psum_scatter(norm_two_part.reshape(row_shape), 'heads', scatter_dimen...  37.9 us
    reduce_scatter x1, waiting for transfers between devices, on_device(): lax.psum_scatter(norm_one_part.reshape(row_shape), 'heads', scatter_dimen...  37.2 us
    all_gather x1, blocking collectives, on_device(): lax.all_gather(out_weight, ('batch', 'seq'), axis=1, tiled=True)  36.9 us
    all_gather x1, waiting for transfers between devices, on_device(): lax.all_gather(outer_weight, ('batch', 'seq'), axis=1, tiled=True)  36.5 us
  transfers between devices with their start and end apart: 18, of which 14 were waited for; matrix products, arithmetic and copies ran while one was open for 17% of the time, Pallas kernels for 0%

commit v1 on v0

v1 whole, which is shorter than its diff:
```python
import functools

import jax
import jax.numpy as jnp
from jax import lax
from jax.experimental import pallas as pl
from jax.experimental.pallas import tpu as pltpu
from jax.sharding import PartitionSpec as P

HEAD_DIM = 64
KERNEL = 3
DOCS = 4
PADW = 256
QB = 512
KB = 256

epsilon = 1e-05
masked_score = -1e30
f32 = jnp.float32
b16 = jnp.bfloat16

VMEM = pl.BlockSpec(memory_space=pltpu.VMEM)
SMEM = pl.BlockSpec(memory_space=pltpu.SMEM)


def swap(shard, axis, by):
    return lax.ppermute(shard, axis, [(i, i ^ by) for i in range(lax.axis_size(axis))])


def gather_heads(shard):
    far = swap(shard, "heads", 2)
    near = swap(shard, "heads", 1)
    return [shard, near, far, swap(far, "heads", 1)]


def pairwise(group):
    return group % 32 == 0


def gather_rows(shard):
    if not pairwise(shard.shape[0]):
        whole = lax.all_gather(shard, ("batch", "seq"), axis=0, tiled=True)
        return tuple(whole.reshape(2, 1, -1, shard.shape[1]))
    count = lax.axis_size("batch")
    stack = jnp.stack([shard] + [swap(shard, "batch", by) for by in range(1, count)])
    return stack, swap(stack, "seq", 1)


def scatter_rows(keep, sent):
    if keep.shape[0] == 1:
        whole = jnp.concatenate([keep[0].astype(b16), sent[0]])
        return lax.psum_scatter(whole, ("batch", "seq"), scatter_dimension=0, tiled=True).astype(f32)
    got = swap(sent, "seq", 1)
    total = keep.astype(f32) + got.astype(f32)
    pieces = [swap(total[by].astype(b16), "batch", by) for by in range(1, lax.axis_size("batch"))]
    result = total[0]
    for piece in pieces:
        result = result + piece.astype(f32)
    return result


def scatter_heads(keep, sent):
    got = swap(sent, "heads", 1)
    rows = keep.shape[0] // 2
    far = (keep[rows:].astype(f32) + got[rows:].astype(f32)).astype(b16)
    here = keep[:rows].astype(f32) + got[:rows].astype(f32)
    return here, swap(far, "heads", 2)


def call(body, outs, *args, scratch=(), flops=0, limit=40):
    in_specs = [SMEM] + [VMEM] * (len(args) - 1)
    return pl.pallas_call(
        body,
        out_shape=[jax.ShapeDtypeStruct(*o) for o in outs],
        in_specs=in_specs,
        out_specs=[VMEM] * len(outs),
        scratch_shapes=list(scratch),
        compiler_params=pltpu.CompilerParams(vmem_limit_bytes=limit << 20),
        cost_estimate=pl.CostEstimate(
            flops=flops,
            transcendentals=0,
            bytes_accessed=sum(a.size * a.dtype.itemsize for a in args),
        ),
    )(*args)


def dot(a, b, ca=1, cb=0):
    return lax.dot_general(a, b, (((ca,), (cb,)), ((), ())), preferred_element_type=f32)


def edges(scal):
    return [scal[3 + d] for d in range(DOCS)]


def doc_start(pos, bounds):
    start = bounds[0] + jnp.zeros_like(pos)
    for edge in bounds[1:]:
        start = jnp.where(pos >= edge, edge, start)
    return start


def lanes_like(shape):
    return lax.broadcasted_iota(jnp.int32, shape, 1)


def half_roll(block):
    return pltpu.roll(block, 64, 1)


def norm_rows(values):
    average = jnp.mean(values, axis=-1, keepdims=True)
    centered = values - average
    inverse = lax.rsqrt(jnp.mean(centered * centered, axis=-1, keepdims=True) + epsilon)
    return centered * inverse, inverse


def group_rows(stack, rel, rel_seq, scal):
    count = stack.shape[1]
    if stack.shape[0] == 1:
        return slice(rel_seq * count, rel_seq * count + count)
    return pl.ds(pl.multiple_of(((scal[1] ^ rel) * 2 + (scal[2] ^ rel_seq)) * count, 32), count)


def ds(start, size):
    return pl.ds(pl.multiple_of(start, size), size)


def front_body(half, quarter, scal, *refs):
    pieces, refs = refs[:8], refs[8:]
    w_own, w_other, gain, bias, taps = refs[:5]
    normed, form, projected, wpad, query, key, value = refs[5:12]
    rows_in, proj = refs[12:]
    head = scal[0]
    low = lanes_like((w_own.shape[1], 128)) < 64
    for rel_seq, stack in enumerate((w_own, w_other)):
        for rel in range(stack.shape[0]):
            rows = group_rows(stack, rel, rel_seq, scal)
            for part in range(3):
                wpad[rows, part * 256 : part * 256 + 128] = stack[rel, :, part * 128 : part * 128 + 128]
            shared = stack[rel, :, 384:512].astype(f32)
            wpad[rows, 128:256] = jnp.where(low, shared, 0.0).astype(b16)
            wpad[rows, 384:512] = jnp.where(low, half_roll(shared), 0.0).astype(b16)
            wpad[rows, 640:768] = stack[rel, :, 512:640]
    for index, piece in enumerate(pieces):
        base = (head ^ (index % 4)) * quarter + (half if index < 4 else 0)
        rows_in[ds(base, quarter), :] = piece[...]
    proj[0:16, :] = jnp.zeros((16, proj.shape[1]), b16)

    def project(block, own):
        base = block * quarter
        hat, _ = norm_rows(rows_in[ds(base, quarter), :].astype(f32))
        rounded = (hat * gain[...] + bias[...]).astype(b16)
        proj[pl.ds(pl.multiple_of(base + 16, 16), quarter), :] = dot(rounded, wpad[...]).astype(b16)
        if own:
            rows = ds(base - half, quarter)
            normed[rows, :] = rounded
            form[rows, :] = hat.astype(b16)

    @pl.loop(0, 4)
    def _(block):
        project(block, False)

    @pl.loop(4, 8)
    def _(block):
        project(block, True)

    projected[...] = proj[half : 2 * half + 16, :]
    bounds = edges(scal)

    def convolve(block, own):
        base = block * quarter
        pos = base + lax.broadcasted_iota(jnp.int32, (quarter, 1), 0)
        start = doc_start(pos, bounds)
        for part, out in enumerate((query, key, value)):
            if part == 0 and not own:
                continue
            cols = slice(part * PADW, part * PADW + PADW)
            rows = proj[pl.ds(pl.multiple_of(base, 16), quarter + 16), cols].astype(f32)
            mixed = taps[0:1, cols] * rows[16:]
            for back in range(1, KERNEL):
                earlier = pltpu.roll(rows, back, 0)[16:]
                mixed = mixed + jnp.where(pos - back >= start, taps[back : back + 1, cols] * earlier, 0.0)
            mixed = mixed.astype(b16)
            if part == 0:
                out[ds(base - half, quarter), :] = mixed * jnp.asarray(HEAD_DIM**-0.5, b16)
            else:
                out[ds(base, quarter), :] = mixed

    @pl.loop(0, 4)
    def _(block):
        convolve(block, False)

    @pl.loop(4, 8)
    def _(block):
        convolve(block, True)


def masked_queries(query, slots, heads):
    lane = lanes_like(query.shape) // HEAD_DIM
    for head in range(heads):
        slots[head] = jnp.where(lane == head, query[...], jnp.zeros((), b16))


def attention_body(half, heads, scal, query, key, value, packed, out_t, lse, vt, qm, peak, total):
    bounds = edges(scal)
    masked_queries(query, qm, heads)

    @pl.loop(0, 2 * half // 256)
    def _(block):
        turned = value[ds(block * 256, 256), :].astype(f32).T
        vt[:, ds(block * 256, 256)] = turned[: heads * HEAD_DIM].astype(b16)

    out_t[...] = jnp.zeros_like(out_t)
    peak[...] = jnp.full_like(peak, masked_score)
    total[...] = jnp.zeros_like(total)
    for block in range(half // QB):
        first = half + block * QB
        cols = slice(block * QB, block * QB + QB)
        pos = first + lanes_like((1, QB))
        start = doc_start(pos, bounds)
        low = doc_start(jnp.int32(first), bounds) // KB

        @pl.loop(low, (first + QB) // KB)
        def _(kb):
            keys = key[ds(kb * KB, KB), :]
            key_pos = kb * KB + lax.broadcasted_iota(jnp.int32, (KB, 1), 0)
            allowed = (key_pos >= start) & (key_pos <= pos)
            for head in range(heads):
                rows = slice(head * HEAD_DIM, head * HEAD_DIM + HEAD_DIM)
                one = slice(head, head + 1)
                scores = dot(keys, qm[head, cols, :], 1, 1)
                scores = jnp.where(allowed, scores, masked_score)
                old = peak[one, cols]
                new = jnp.maximum(old, jnp.max(scores, axis=0, keepdims=True))
                weights = jnp.exp(scores - new)
                shrink = jnp.exp(old - new)
                peak[one, cols] = new
                total[one, cols] = shrink * total[one, cols] + jnp.sum(weights, axis=0, keepdims=True)
                out_t[rows, cols] = shrink * out_t[rows, cols] + dot(
                    vt[rows, ds(kb * KB, KB)], weights.astype(b16)
                )

    for head in range(heads):
        rows = slice(head * HEAD_DIM, head * HEAD_DIM + HEAD_DIM)
        out_t[rows, :] = out_t[rows, :] / total[head : head + 1, :]
    lse[...] = peak[...] + jnp.log(jnp.maximum(total[...], 1e-30))
    for block in range(half // 256):
        cols = slice(block * 256, block * 256 + 256)
        packed[cols, :] = out_t[0:128, cols].T.astype(b16)
    for block in range(half // 512):
        cols = slice(block * 256, block * 256 + 256)
        later = slice(half // 2 + block * 256, half // 2 + block * 256 + 256)
        both = jnp.concatenate([out_t[128:192, cols], out_t[128:192, later]], axis=0)
        packed[half + block * 256 : half + block * 256 + 256, :] = both.T.astype(b16)


def back_blocks(half, heads, scal, first_kb, last_kb, refs, finish):
    key, value, qm, dom, lse, row_dot, kt, query_t, key_sum, value_sum = refs
    bounds = edges(scal)

    @pl.loop(first_kb, last_kb)
    def _(kb):
        key_sum[...] = jnp.zeros_like(key_sum)
        value_sum[...] = jnp.zeros_like(value_sum)
        for block in range(half // QB):
            first = half + block * QB
            cols = slice(block * QB, block * QB + QB)
            low = doc_start(jnp.int32(first), bounds)

            @pl.when((kb * KB + KB > low) & (kb * KB < first + QB))
            def _():
                pos = first + lanes_like((1, QB))
                start = doc_start(pos, bounds)
                keys = key[ds(kb * KB, KB), :]
                values = value[ds(kb * KB, KB), :]
                key_pos = kb * KB + lax.broadcasted_iota(jnp.int32, (KB, 1), 0)
                allowed = (key_pos >= start) & (key_pos <= pos)
                for head in range(heads):
                    rows = slice(head * HEAD_DIM, head * HEAD_DIM + HEAD_DIM)
                    one = slice(head, head + 1)
                    own_q = qm[head, cols, :]
                    own_g = dom[head, cols, :]
                    scores = jnp.where(allowed, dot(keys, own_q, 1, 1) - lse[one, cols], masked_score)
                    weights = jnp.exp(scores)
                    grads = weights * (dot(values, own_g, 1, 1) - row_dot[one, cols])
                    grads = grads.astype(b16)
                    value_sum[...] += dot(weights.astype(b16), own_g)
                    key_sum[...] += dot(grads, own_q)
                    query_t[rows, cols] += dot(kt[rows, ds(kb * KB, KB)], grads)

        finish(kb, key_sum[...], value_sum[...])


def spread_groups(source, scal, keep, sent):
    for rel_seq, out in enumerate((keep, sent)):
        for rel in range(out.shape[0]):
            out[rel] = source[group_rows(out, rel, rel_seq, scal), :].astype(out.dtype)


def remote_back_body(half, quarter, heads, scal, *refs):
    branches, refs = refs[:4], refs[4:]
    wo, query, key, value, out_t, lse = refs[:6]
    remote, query_t, dout, row_dot, kt, proj_keep, proj_send = refs[6:13]
    qm, dom, key_sum, value_sum, proj_grad, turned = refs[13:]
    head = scal[0]
    width = heads * HEAD_DIM
    masked_queries(query, qm, heads)
    proj_grad[...] = jnp.zeros_like(proj_grad)
    row_dot[...] = jnp.zeros_like(row_dot)
    for rel, branch in enumerate(branches):
        base = (head ^ rel) * quarter
        grad = dot(branch[...], wo[...]).astype(b16)
        dout[ds(base, quarter), :] = grad
        attended = out_t[:, ds(base, quarter)]
        product = grad.astype(f32).T[:width] * attended
        for one in range(heads):
            row_dot[one : one + 1, ds(base, quarter)] = jnp.sum(
                product[one * HEAD_DIM : one * HEAD_DIM + HEAD_DIM], axis=0, keepdims=True
            )
        proj_grad[...] += dot(attended.astype(b16), branch[...])
    turned[...] = proj_grad[...].T
    spread_groups(turned, scal, proj_keep, proj_send)
    masked_queries(dout, dom, heads)

    @pl.loop(0, 2 * half // 256)
    def _(block):
        kt[:, ds(block * 256, 256)] = key[ds(block * 256, 256), :].astype(f32).T[:width].astype(b16)

    query_t[...] = jnp.zeros_like(query_t)

    def finish(kb, dk, dv):
        rows = ds(kb * KB, KB)
        remote[rows, 0:128] = dk[:, 0:128].astype(b16)
        remote[rows, 128:256] = dv[:, 0:128].astype(b16)
        remote[rows, 256:384] = (dk[:, 128:256] + half_roll(dv[:, 128:256])).astype(b16)

    back_blocks(
        half, heads, scal, 0, half // KB,
        (key, value, qm, dom, lse, row_dot, kt, query_t, key_sum, value_sum), finish,
    )


def local_back_body(half, heads, scal, *refs):
    query, key, value, dout, lse, row_dot, kt, query_in, taps = refs[:9]
    dq, dk_out, dv_out, front = refs[9:13]
    qm, dom, key_sum, value_sum, query_t = refs[13:]
    masked_queries(query, qm, heads)
    masked_queries(dout, dom, heads)
    query_t[...] = query_in[...]

    def finish(kb, dk, dv):
        rows = ds(kb * KB - half, KB)
        dk_out[rows, :] = dk
        dv_out[rows, :] = dv

    back_blocks(
        half, heads, scal, half // KB, 2 * half // KB,
        (key, value, qm, dom, lse, row_dot, kt, query_t, key_sum, value_sum), finish,
    )
    width = heads * HEAD_DIM
    scale = HEAD_DIM**-0.5
    for block in range(half // 256):
        cols = slice(block * 256, block * 256 + 256)
        turned = (query_t[:, cols] * scale).T
        dq[cols, 0:128] = turned[:, 0:128]
        dq[cols, 128:256] = jnp.concatenate(
            [turned[:, 128:width], jnp.zeros((256, PADW - width), f32)], axis=1
        )
    bounds = edges(scal)
    pos = half + lax.broadcasted_iota(jnp.int32, (8, 1), 0)
    start = doc_start(pos, bounds)
    for part, grads in enumerate((dq, dk_out, dv_out)):
        cols = slice(part * PADW, part * PADW + PADW)
        rounded = grads[0:8, :].astype(b16).astype(f32)
        result = jnp.zeros((8, PADW), f32)
        for back in range(1, KERNEL):
            moved = pltpu.roll(jnp.where(pos - back >= start, taps[back : back + 1, cols] * rounded, 0.0), 8 - back, 0)
            place = lax.broadcasted_iota(jnp.int32, (8, 1), 0)
            result = result + jnp.where(place >= 8 - back, moved, 0.0)
        front[:, cols] = result


def weights_body(scal, *refs):
    first, second, first_o, second_o, inner, wo, outer = refs
    for rel_seq, (one, two) in enumerate(((first, second), (first_o, second_o))):
        for rel in range(one.shape[0]):
            rows = group_rows(one, rel, rel_seq, scal)
            width = inner.shape[1]
            inner[rows, :] = one[rel, :, :width]
            wo[rows, :] = one[rel, :, width:]
            outer[rows, :] = two[rel]


def feed_body(half, quarter, scal, *refs):
    attended, wos, inputs, cots = refs[0:4], refs[4:8], refs[8:12], refs[12:16]
    inner, outer, gain, bias = refs[16:20]
    normed, squared, inner_grad, keep, sent, middle_own = refs[20:]
    head = scal[0]
    for rel in range(4):
        base = (head ^ rel) * quarter
        late = base >= half // 2
        middle = inputs[rel][...].astype(f32)
        for part in range(4):
            left = attended[part][ds(base, quarter), :]
            right = attended[part][ds(half + lax.rem(base, half // 2), quarter), :].astype(f32)
            right = jnp.where(late, half_roll(right), right).astype(b16)
            middle = middle + dot(jnp.concatenate([left, right], axis=1), wos[part][...], 1, 1)
        if rel == 0:
            middle_own[...] = middle
        hat, _ = norm_rows(middle)
        rounded = (hat * gain[...] + bias[...]).astype(b16)
        rows = slice(rel * quarter, rel * quarter + quarter)
        normed[rows, :] = rounded
        positive = jnp.maximum(dot(rounded, inner[...]), 0.0)
        squared[rows, :] = (positive * positive).astype(b16)
        grads = (dot(cots[rel][...], outer[...]) * 2.0 * positive).astype(b16)
        inner_grad[rows, :] = grads
        part = dot(grads, inner[...], 1, 1)
        place = slice((rel // 2) * quarter, (rel // 2) * quarter + quarter)
        if rel % 2 == 0:
            keep[place, :] = part
        else:
            sent[place, :] = part.astype(b16)


def feed_grads_body(half, quarter, scal, *refs):
    cots = refs[0:4]
    normed, squared, inner_grad, outer = refs[4:8]
    keep, sent, in_keep, in_send, out_keep, out_send = refs[8:14]
    cot, total = refs[14:]
    for rel in range(4):
        rows = slice(rel * quarter, rel * quarter + quarter)
        cot[rows, :] = cots[rel][...]
        part = dot(squared[rows, :], outer[...], 1, 1)
        place = slice((rel // 2) * quarter, (rel // 2) * quarter + quarter)
        if rel % 2 == 0:
            keep[place, :] = part
        else:
            sent[place, :] = part.astype(b16)
    for left, right, kept, away in ((cot, squared, out_keep, out_send), (normed, inner_grad, in_keep, in_send)):
        for tile in range(total.shape[0] // 256):
            cols = slice(tile * 256, tile * 256 + 256)
            total[cols, :] = dot(left[:, cols], right[...], 0, 0)
        spread_groups(total, scal, kept, away)


def norm_back_body(scal, part, got, values, skip, gain, grad_in, rounded, sums):
    del scal
    grad = part[...] + got[...].astype(f32)
    hat, inverse = norm_rows(values[...].astype(f32))
    scaled = grad * gain[...]
    back = inverse * (
        scaled
        - jnp.mean(scaled, axis=-1, keepdims=True)
        - hat * jnp.mean(scaled * hat, axis=-1, keepdims=True)
    )
    result = skip[...].astype(f32) + back
    grad_in[...] = result
    rounded[...] = result.astype(b16)
    sums[...] = jnp.zeros_like(sums)
    sums[0:1, :] = jnp.sum(grad * hat, axis=0, keepdims=True)
    sums[1:2, :] = jnp.sum(grad, axis=0, keepdims=True)


def tail_body(half, quarter, scal, *refs):
    dq, dk, dv, remote, front, projected, normed, form, wpad, taps = refs[:10]
    keep, sent, w_keep, w_send, sums = refs[10:15]
    mixed, proj_grad, total, dense = refs[15:]
    head = scal[0]
    bounds = edges(scal)
    low = lanes_like((quarter, 128)) < 64
    sums[...] = jnp.zeros_like(sums)
    for block in range(half // quarter):
        rows = slice(block * quarter, block * quarter + quarter)
        shared = remote[rows, 256:384].astype(f32)
        mixed[rows, 0:256] = dq[rows, :].astype(b16)
        mixed[rows, 256:384] = (dk[rows, 0:128] + remote[rows, 0:128].astype(f32)).astype(b16)
        mixed[rows, 384:512] = (dk[rows, 128:256] + jnp.where(low, shared, 0.0)).astype(b16)
        mixed[rows, 512:640] = (dv[rows, 0:128] + remote[rows, 128:256].astype(f32)).astype(b16)
        mixed[rows, 640:768] = (dv[rows, 128:256] + jnp.where(low, half_roll(shared), 0.0)).astype(b16)
    mixed[half : half + 16, :] = jnp.zeros((16, mixed.shape[1]), b16)

    @pl.loop(0, half // quarter)
    def _(block):
        base = block * quarter
        pos = half + base + lax.broadcasted_iota(jnp.int32, (quarter + 16, 1), 0)
        start = doc_start(pos, bounds)
        for part in range(3):
            cols = slice(part * PADW, part * PADW + PADW)
            grads = mixed[pl.ds(pl.multiple_of(base, 16), quarter + 16), cols].astype(f32)
            values = projected[pl.ds(pl.multiple_of(base, 16), quarter + 16), cols].astype(f32)
            here = grads[:quarter]
            result = taps[0:1, cols] * here
            sums[4:5, cols] += jnp.sum(here * values[16:], axis=0, keepdims=True)
            for back in range(1, KERNEL):
                same = pos - back >= start
                held = jnp.where(same, grads, 0.0)
                ahead = pltpu.roll(held, quarter + 16 - back, 0)[:quarter]
                result = result + taps[back : back + 1, cols] * ahead
                earlier = pltpu.roll(values, back, 0)[16:]
                sums[4 + back : 5 + back, cols] += jnp.sum(held[:quarter] * earlier, axis=0, keepdims=True)
            proj_grad[ds(base, quarter), cols] = result.astype(b16)

        @pl.when(block == half // quarter - 1)
        def _():
            added = jnp.concatenate([jnp.zeros((8, front.shape[1]), f32), front[...]], axis=0)
            tail_pos = 2 * half - 16 + lax.broadcasted_iota(jnp.int32, (32, 1), 0)
            tail_start = doc_start(tail_pos, bounds)
            grads = mixed[half - 16 : half + 16, :].astype(f32)
            result = taps[0:1, :] * grads[:16]
            for back in range(1, KERNEL):
                held = jnp.where(tail_pos - back >= tail_start, grads, 0.0)
                result = result + taps[back : back + 1, :] * pltpu.roll(held, 32 - back, 0)[:16]
            proj_grad[half - 16 : half, :] = (result + added).astype(b16)

    for rel in range(4):
        base = (head ^ rel) * quarter
        part = dot(proj_grad[ds(base, quarter), :], wpad[...], 1, 1)
        sums[0:1, :] += jnp.sum(part * form[ds(base, quarter), :].astype(f32), axis=0, keepdims=True)
        sums[1:2, :] += jnp.sum(part, axis=0, keepdims=True)
        place = slice((rel // 2) * quarter, (rel // 2) * quarter + quarter)
        if rel % 2 == 0:
            keep[place, :] = part
        else:
            sent[place, :] = part.astype(b16)
    for tile in range(total.shape[0] // 256):
        rows = slice(tile * 256, tile * 256 + 256)
        total[rows, :] = dot(normed[:, rows], proj_grad[...], 0, 0)
        for part in range(3):
            dense[rows, part * 128 : part * 128 + 128] = total[rows, part * 256 : part * 256 + 128]
        dense[rows, 384:512] = total[rows, 128:256] + half_roll(total[rows, 384:512])
        dense[rows, 512:640] = total[rows, 640:768]
    spread_groups(dense, scal, w_keep, w_send)


def pad_heads(values, width):
    shaped = values.reshape(values.shape[:-1] + (3, width))
    padded = jnp.pad(shaped, [(0, 0)] * (shaped.ndim - 1) + [(0, PADW - width)])
    return padded.reshape(values.shape[:-1] + (3 * PADW,))


def on_device(
    block_input, segment_ids, norm1_gain, norm1_bias, qkv_weight, conv_kernel, out_weight,
    norm2_gain, norm2_bias, inner_weight, outer_weight, cotangent,
):
    quarter = block_input.shape[2]
    half = quarter * lax.axis_size("heads")
    width = qkv_weight.shape[2]
    heads = width // HEAD_DIM
    group = qkv_weight.shape[0]
    groups = lax.axis_size("batch") * lax.axis_size("seq")
    model = group * groups
    hidden = inner_weight.shape[1]
    head, batch, seq = lax.axis_index("heads"), lax.axis_index("batch"), lax.axis_index("seq")
    own = batch * 2 + seq
    stacks = (groups // 2, group) if pairwise(group) else (1, model // 2)

    ids = segment_ids.reshape(-1)
    docs = jnp.arange(DOCS, dtype=jnp.int32)
    firsts = jnp.sum((ids[None, :] < docs[:, None]).astype(jnp.int32), axis=1) - (seq - 1) * half
    scal = jnp.concatenate([jnp.stack([head, batch, seq]), firsts, jnp.zeros((1,), jnp.int32)]).astype(jnp.int32)

    x_own = block_input.reshape(quarter, model)
    cot_own = cotangent.reshape(quarter, model)

    small = jnp.concatenate([norm1_gain, norm1_bias, norm2_gain, norm2_bias, conv_kernel.reshape(-1)])
    small = jnp.pad(small, (0, -small.shape[0] % 128)).reshape(1, -1)
    if pairwise(group):
        small_all = jnp.stack([small] + [swap(small, "batch", by) for by in range(1, groups // 2)])
        small_all = jnp.concatenate([small_all, swap(small_all, "seq", 1)]).reshape(groups, -1)
        order = jnp.arange(groups)
        rel_of = (order % 2 ^ seq) * (groups // 2) + (order // 2 ^ batch)
        small_all = jnp.sum(
            jnp.where(rel_of[:, None, None] == order[None, :, None], small_all[None].astype(f32), 0.0), axis=1
        )
    else:
        small_all = lax.all_gather(small, ("batch", "seq"), axis=0, tiled=True).astype(f32)
    gain_one, bias_one, gain_two, bias_two = (
        small_all[:, i * group : i * group + group].reshape(1, model) for i in range(4)
    )
    taps = small_all[:, 4 * group : 4 * group + conv_kernel.size].reshape((groups,) + conv_kernel.shape)
    taps = taps.transpose(1, 2, 0, 3).reshape(3, width, KERNEL).transpose(2, 0, 1).reshape(KERNEL, 3 * width)
    taps = pad_heads(taps, width)

    qkv = qkv_weight
    shard = jnp.concatenate(
        [qkv[:, 0, :128], qkv[:, 1, :128], qkv[:, 2, :128], qkv[:, 0, 128:], qkv[:, 1, 128:], qkv[:, 2, 128:],
         jnp.zeros((group, PADW - width), b16)], axis=1,
    )
    w_own, w_other = gather_rows(shard)

    x_pieces = gather_heads(x_own)
    y_pieces = gather_heads(swap(x_own, "seq", 1))

    normed_one, form_one, projected, wpad, query, key, value = call(
        functools.partial(front_body, half, quarter),
        [
            ((half, model), b16), ((half, model), b16), ((half + 16, 3 * PADW), b16), ((model, 3 * PADW), b16),
            ((half, PADW), b16), ((2 * half, PADW), b16), ((2 * half, PADW), b16),
        ],
        scal, *x_pieces, *y_pieces, w_own, w_other, gain_one, bias_one, taps,
        scratch=[pltpu.VMEM((2 * half, model), b16), pltpu.VMEM((2 * half + 16, 3 * PADW), b16)],
        flops=4 * half * model * 3 * width,
    )

    inner_wo = jnp.concatenate(
        [inner_weight, jnp.pad(out_weight.T, ((0, 0), (0, PADW - width)))], axis=1
    )
    first_own, first_other = gather_rows(inner_wo)
    second_own, second_other = gather_rows(outer_weight.T)
    inner_full, wo_own, outer_full = call(
        weights_body,
        [((model, hidden), b16), ((model, PADW), b16), ((model, hidden), b16)],
        scal, first_own, second_own, first_other, second_other,
    )
    wo_pieces = gather_heads(wo_own)
    cot_pieces = gather_heads(cot_own)

    packed, out_t, lse = call(
        functools.partial(attention_body, half, heads),
        [((half + half // 2, 128), b16), ((width, half), f32), ((8, half), f32)],
        scal, query, key, value,
        scratch=[
            pltpu.VMEM((width, 2 * half), b16), pltpu.VMEM((heads, half, PADW), b16),
            pltpu.VMEM((8, half), f32), pltpu.VMEM((8, half), f32),
        ],
        flops=4 * half * half * width,
    )
    packed_pieces = gather_heads(packed)

    normed_two, squared, inner_grad, keep, sent, middle_own = call(
        functools.partial(feed_body, half, quarter),
        [((half, model), b16), ((half, hidden), b16), ((half, hidden), b16),
         ((2 * quarter, model), f32), ((2 * quarter, model), b16), ((quarter, model), f32)],
        scal, *packed_pieces, *wo_pieces, *x_pieces, *cot_pieces, inner_full, outer_full, gain_two, bias_two,
        flops=2 * half * model * (model + 3 * hidden),
    )
    dn_here, dn_far = scatter_heads(keep, sent)
    middle_grad, branch, sums_two = call(
        norm_back_body,
        [((quarter, model), f32), ((quarter, model), b16), ((8, model), f32)],
        scal, dn_here, dn_far, middle_own, cot_own, gain_two,
    )
    branch_pieces = gather_heads(branch)

    keep, sent, in_keep, in_send, ff_keep, ff_send = call(
        functools.partial(feed_grads_body, half, quarter),
        [((2 * quarter, model), f32), ((2 * quarter, model), b16)]
        + [(stacks + (hidden,), d) for d in (f32, b16, f32, b16)],
        scal, *cot_pieces, normed_two, squared, inner_grad, outer_full,
        scratch=[pltpu.VMEM((half, model), b16), pltpu.VMEM((model, hidden), f32)],
        flops=6 * half * model * hidden,
    )
    out_here, out_far = scatter_heads(keep, sent)
    block_output = (middle_own + out_here + out_far.astype(f32)).astype(b16)
    inner_out = scatter_rows(in_keep, in_send)
    outer_out = scatter_rows(ff_keep, ff_send)

    remote, query_t, dout, row_dot, kt, pj_keep, pj_send = call(
        functools.partial(remote_back_body, half, quarter, heads),
        [((half, 384), b16), ((width, half), f32), ((half, PADW), b16), ((8, half), f32), ((width, 2 * half), b16),
         (stacks + (width,), f32), (stacks + (width,), b16)],
        scal, *branch_pieces, wo_own, query, key, value, out_t, lse,
        scratch=[
            pltpu.VMEM((heads, half, PADW), b16), pltpu.VMEM((heads, half, PADW), b16),
            pltpu.VMEM((KB, PADW), f32), pltpu.VMEM((KB, PADW), f32),
            pltpu.VMEM((width, model), f32), pltpu.VMEM((model, width), f32),
        ],
        flops=10 * half * half * width,
    )
    remote_in = lax.ppermute(remote, "seq", [(1, 0)])
    proj_out = scatter_rows(pj_keep, pj_send)

    dq, dk, dv, front = call(
        functools.partial(local_back_body, half, heads),
        [((half, PADW), f32), ((half, PADW), f32), ((half, PADW), f32), ((8, 3 * PADW), f32)],
        scal, query, key, value, dout, lse, row_dot, kt, query_t, taps,
        scratch=[
            pltpu.VMEM((heads, half, PADW), b16), pltpu.VMEM((heads, half, PADW), b16),
            pltpu.VMEM((KB, PADW), f32), pltpu.VMEM((KB, PADW), f32), pltpu.VMEM((width, half), f32),
        ],
        flops=10 * half * half * width,
    )
    front_in = lax.ppermute(front, "seq", [(1, 0)])

    keep, sent, w_keep, w_send, sums = call(
        functools.partial(tail_body, half, quarter),
        [((2 * quarter, model), f32), ((2 * quarter, model), b16),
         (stacks + (640,), f32), (stacks + (640,), b16), ((8, 3 * PADW), f32)],
        scal, dq, dk, dv, remote_in, front_in, projected, normed_one, form_one, wpad, taps,
        scratch=[
            pltpu.VMEM((half + 16, 3 * PADW), b16), pltpu.VMEM((half, 3 * PADW), b16),
            pltpu.VMEM((model, 3 * PADW), f32), pltpu.VMEM((model, 640), f32),
        ],
        flops=4 * half * model * 3 * width,
    )
    norms = jnp.concatenate([sums[0:2], sums_two[0:2]])
    norms = norms + swap(norms, "heads", 1)
    norms = norms + swap(norms, "heads", 2)
    small = jnp.concatenate([norms, sums[4:8]])
    if pairwise(group):
        small = small + swap(small, "seq", 1)
        small = sum([swap(small, "batch", by) for by in range(1, groups // 2)], small)
    else:
        small = lax.psum(small, ("batch", "seq"))

    dn_here, dn_far = scatter_heads(keep, sent)
    qkv_out = scatter_rows(w_keep, w_send)
    input_grad, _, _ = call(
        norm_back_body,
        [((quarter, model), f32), ((quarter, model), b16), ((8, model), f32)],
        scal, dn_here, dn_far, x_own, middle_grad, gain_one,
    )

    qkv_out = jnp.stack(
        [
            jnp.concatenate([qkv_out[:, 0:128], qkv_out[:, 384:448]], axis=1),
            jnp.concatenate([qkv_out[:, 128:256], qkv_out[:, 448:512]], axis=1),
            jnp.concatenate([qkv_out[:, 256:384], qkv_out[:, 512:576]], axis=1),
        ],
        axis=1,
    )
    gains = lax.dynamic_slice_in_dim(small[0:4], own * group, group, 1)
    kernel_out = small[4 : 4 + KERNEL].reshape(KERNEL, 3, PADW)[:, :, :width].reshape(KERNEL, 3, heads, HEAD_DIM)
    kernel_out = kernel_out.transpose(1, 2, 3, 0).reshape(3, heads, HEAD_DIM * KERNEL)
    share = conv_kernel.shape[2]
    kernel_out = lax.dynamic_slice_in_dim(kernel_out, own * share, share, 2)
    return (
        block_output.reshape(block_input.shape),
        input_grad.reshape(block_input.shape),
        gains[0],
        gains[1],
        qkv_out,
        kernel_out,
        proj_out.T,
        gains[2],
        gains[3],
        inner_out,
        outer_out.T,
    )


def solution(mesh):
    return jax.shard_map(
        on_device,
        mesh=mesh,
        in_specs=(
            P("batch", "seq", "heads", None),
            P("batch", None),
            P(("batch", "seq")),
            P(("batch", "seq")),
            P(("batch", "seq"), None, "heads"),
            P(None, "heads", ("batch", "seq")),
            P("heads", ("batch", "seq")),
            P(("batch", "seq")),
            P(("batch", "seq")),
            P(("batch", "seq"), "heads"),
            P("heads", ("batch", "seq")),
            P("batch", "seq", "heads", None),
        ),
        out_specs=(
            P("batch", "seq", "heads", None),
            P("batch", "seq", "heads", None),
            P(("batch", "seq")),
            P(("batch", "seq")),
            P(("batch", "seq"), None, "heads"),
            P(None, "heads", ("batch", "seq")),
            P("heads", ("batch", "seq")),
            P(("batch", "seq")),
            P(("batch", "seq")),
            P(("batch", "seq"), "heads"),
            P("heads", ("batch", "seq")),
        ),
        check_vma=False,
    )
```

time: 901 us -> 299 us (0.33)
  waiting for transfers between devices: 454 us -> 96.8 us
  blocking collectives: 170 us -> 0 us
  matrix products: 111 us -> 0 us
  starting transfers between devices: 11 us -> 82.7 us
  Pallas kernels: 0 us -> 65.2 us
  other arithmetic: 67.1 us -> 14 us
  local copies, waits for them, and re-layouts: 54 us -> 37.4 us
  between operations: 17.6 us -> 1.24 us
  loops' own time: 9.65 us -> 0 us
    reduce_scatter x7 -> x0, waiting for transfers between devices: 284 us -> none  [the longest x1 72.9 us: on_device(): lax.psum_scatter(inner_grad, ('batch', 'seq'), scatter_dimension=0, tiled...]
    all_gather x6 -> x0, waiting for transfers between devices: 133 us -> none  [the longest x1 36.5 us: on_device(): lax.all_gather(outer_weight, ('batch', 'seq'), axis=1, tiled=True)]
    dot_general x25 -> x0, matrix products: 110 us -> none  [the longest x4 15.6 us: block_scores(): jnp.einsum('qhd,khd->hqk', query_block, key_rows, preferred_element_type=...]
    all_gather x3 -> x0, blocking collectives: 103 us -> none  [the longest x1 36.9 us: on_device(): lax.all_gather(out_weight, ('batch', 'seq'), axis=1, tiled=True)]
    ppermute x4 -> x65, starting transfers between devices: 10 us -> 82.7 us  [the longest x63 79.9 us: swap(): lax.ppermute(shard, axis, [(i, i ^ by) for i in range(lax.axis_size(axis))])]
    pallas_call x0 -> x10, Pallas kernels: none -> 65.2 us  [call(): pl.pallas_call(body, out_shape=[jax.ShapeDtypeStruct(*o) for o in outs],...]
    ppermute x4 -> x65, waiting for transfers between devices: 34.4 us -> 96.8 us  [the longest x63 83.9 us: swap(): lax.ppermute(shard, axis, [(i, i ^ by) for i in range(lax.axis_size(axis))])]
    unnamed x2 -> x0, blocking collectives: 60.7 us -> none
  transfers between devices with their start and end apart: 18 -> 65, of which waited for: 14 -> 23; matrix products, arithmetic and copies ran while one was open for 17% -> 8% of each run, Pallas kernels for 0% -> 17%
where the time goes in v1:
time: 299 us; the launch traced here: 297 us
  waiting for transfers between devices  96.8 us (32%)
  starting transfers between devices  82.7 us (28%)
  Pallas kernels  65.2 us (22%)
  local copies, waits for them, and re-layouts  37.4 us (13%)
  other arithmetic  14 us (5%)
    ppermute x63, waiting for transfers between devices, swap(): lax.ppermute(shard, axis, [(i, i ^ by) for i in range(lax.axis_size(axis))])  83.9 us
    ppermute x63, starting transfers between devices, swap(): lax.ppermute(shard, axis, [(i, i ^ by) for i in range(lax.axis_size(axis))])  79.9 us
    pallas_call x10, Pallas kernels, call(): pl.pallas_call(body, out_shape=[jax.ShapeDtypeStruct(*o) for o in outs],...  65.2 us
    unnamed x104, local copies, waits for them, and re-layouts  23.5 us
    ppermute x1, waiting for transfers between devices, on_device(): front_in = lax.ppermute(front, 'seq', [(1, 0)])  12.8 us
  transfers between devices with their start and end apart: 65, of which 23 were waited for; matrix products, arithmetic and copies ran while one was open for 8% of the time, Pallas kernels for 17%

profile of v1, /device:TPU:0, one launch (start us, length us, event | category | flops | bytes accessed | tf_op | source)
XLA Modules:
  0.0 297.4 jit_solution(1335289281793544371)
XLA Ops:
  1.5 2.8 concatenate.33
  4.2 5.1 %collective-permute-start.13 = (bf16[1,640]{1,0:T(2,128)(2,1)S(1)}, bf16[1,640]{1,0:T(2,128)(2,1)S(1)}, u32[]{:S(2)}, u32[]{:S(2)}) collective-permute-start(bf16[1,640]{1,0:T(2,128)(2,1)S(1)} %reshape.141), channel_id=1, source_target_pairs={{0,24},{8,16},{16,8},{24,0},{1,25},{9,17},{17,9},{25,1},{2,26},{10... | collective-permute-start | bytes 3848 | tf_op jit(solution)/shard_map/ppermute | solution.py:27
  11.8 2.4 collective-permute-start.19
  20.4 2.9 collective-permute-start.21
  23.3 2.4 collective-permute-done.19
  25.7 6.5 %collective-permute-start.23 = (bf16[96,768]{1,0:T(8,128)(2,1)S(1)}, bf16[96,768]{1,0:T(8,128)(2,1)S(1)}, u32[]{:S(2)}, u32[]{:S(2)}) collective-permute-start(bf16[96,768]{1,0:T(8,128)(2,1)S(1)} %bitcast.148), channel_id=1, source_target_pairs={{0,24},{8,16},{16,8},{24,0},{1,25},{9,17},{17,9},{25,1},{2,26},{10... | collective-permute-start | bytes 442376 | tf_op jit(solution)/shard_map/ppermute | solution.py:27
  34.0 10.6 %collective-permute-done.22 = bf16[96,768]{1,0:T(8,128)(2,1)S(1)} collective-permute-done((bf16[96,768]{1,0:T(8,128)(2,1)S(1)}, bf16[96,768]{1,0:T(8,128)(2,1)S(1)}, u32[]{:S(2)}, u32[]{:S(2)}) %collective-permute-start.22) | collective-permute-done | bytes 147488 | tf_op jit(solution)/shard_map/ppermute | solution.py:27
  51.9 2.8 collective-permute-done.8
  56.1 3.5 %collective-permute-done.7 = bf16[96,640]{1,0:T(8,128)(2,1)S(1)} collective-permute-done((bf16[96,640]{1,0:T(8,128)(2,1)S(1)}, bf16[96,640]{1,0:T(8,128)(2,1)S(1)}, u32[]{:S(2)}, u32[]{:S(2)}) %collective-permute-start.7) | collective-permute-done | bytes 122912 | tf_op jit(solution)/shard_map/ppermute | solution.py:27
  62.9 16.3 %collective-permute-done.25.refs_3_ = bf16[4,96,768]{2,1,0:T(8,128)(2,1)S(1)} collective-permute-done((bf16[4,96,768]{2,1,0:T(8,128)(2,1)S(1)}, bf16[4,96,768]{2,1,0:T(8,128)(2,1)S(1)}, u32[]{:S(2)}, u32[]{:S(2)}) %collective-permute-start.25) | collective-permute-done | bytes 589856 | tf_op jit(solution)/shard_map/ppermute | solution.py:27
  90.8 11.0 %shard_map.203 = (bf16[1024,768]{1,0:T(8,128)(2,1)S(1)}, bf16[1024,768]{1,0:T(8,128)(2,1)S(1)}, bf16[1040,768]{1,0:T(8,128)(2,1)S(1)}, bf16[768,768]{1,0:T(8,128...) custom-call(s32[8]{0:T(128)S(1)} %concatenate.31.scal, ...), custom_call_target="tpu_custom_call" | custom-call | flops 1811939328 | bytes 4144160 | tf_op jit(solution)/shard_map/pallas_call | solution.py:72
  103.0 10.8 %shard_map.204 = (bf16[1536,128]{1,0:T(8,128)(2,1)}, f32[192,1024]{1,0:T(8,128)S(1)}, f32[8,1024]{1,0:T(8,128)S(1)}) custom-call(s32[8]{0:T(128)S(1)} %concatenate.31.scal, bf16[1024,256]{1,0:T(8,128)(2,1)S(1)} %get-tuple-element.56.query.refs_5_.refs_0_, bf16[2048,256]{1,0:T(8,128)(2,1)S(1)} %get-tuple-element.57.key.refs_6_.refs_1_, ...), custom_call_target="tpu_custom_call" | custom-call | flops 805306368 | bytes 2621472 | tf_op jit(solution)/shard_map/pallas_call | solution.py:72
  120.8 8.0 %collective-permute-done.16.refs_2_ = bf16[1536,128]{1,0:T(8,128)(2,1)S(1)} collective-permute-done((bf16[1536,128]{1,0:T(8,128)(2,1)}, bf16[1536,128]{1,0:T(8,128)(2,1)S(1)}, u32[]{:S(2)}, u32[]{:S(2)}) %collective-permute-start.16) | collective-permute-done | bytes 393248 | tf_op jit(solution)/shard_map/ppermute | solution.py:27
  136.2 11.3 %shard_map.206 = (bf16[1024,768]{1,0:T(8,128)(2,1)S(1)}, bf16[1024,768]{1,0:T(8,128)(2,1)S(1)}, bf16[1024,768]{1,0:T(8,128)(2,1)}, f32[512,768]{1,0:T(8,128)}, b...) custom-call(s32[8]{0:T(128)S(1)} %concatenate.31.scal, bf16[1536,128]{1,0:T(8,128)(2,1)} %get-tuple-element.59.refs_0_, ...), custom_call_target="tpu_custom_call" | custom-call | flops 4831838208 | bytes 8656928 | tf_op jit(solution)/shard_map/pallas_call | solution.py:72
  149.3 6.3 %shard_map.207 = (f32[512,768]{1,0:T(8,128)S(1)}, bf16[512,768]{1,0:T(8,128)(2,1)S(1)}, f32[4,96,768]{2,1,0:T(8,128)S(1)}, bf16[4,96,768]{2,1,0:T(8,128)(2,1)}, ...) custom-call(s32[8]{0:T(128)S(1)} %concatenate.31.scal, bf16[256,768]{1,0:T(8,128)(2,1)S(1)} %bitcast.135, ...), custom_call_target="tpu_custom_call" | custom-call | flops 3623878656 | bytes 7471136 | tf_op jit(solution)/shard_map/pallas_call | solution.py:72
  156.6 11.3 %collective-permute-start.57 = (bf16[4,96,768]{2,1,0:T(8,128)(2,1)}, bf16[4,96,768]{2,1,0:T(8,128)(2,1)}, u32[]{:S(2)}, u32[]{:S(2)}) collective-permute-start(bf16[4,96,768]{2,1,0:T(8,128)(2,1)} %get-tuple-element.98), channel_id=1, source_target_pairs={{0,1},{1,0},{2,3},{3,2},{4,5},{5,4},{6,7},{7,6},{8,9},{9,8},{10,11... | collective-permute-start | bytes 1769480 | tf_op jit(solution)/shard_map/ppermute | solution.py:27
  171.4 8.8 %collective-permute-done.35.got = bf16[256,768]{1,0:T(8,128)(2,1)} collective-permute-done((bf16[256,768]{1,0:T(8,128)(2,1)}, bf16[256,768]{1,0:T(8,128)(2,1)}, u32[]{:S(2)}, u32[]{:S(2)}) %collective-permute-start.35) | collective-permute-done | bytes 393248 | tf_op jit(solution)/shard_map/ppermute | solution.py:27
  185.8 2.2 collective-permute-start.58
  188.0 6.6 %collective-permute-done.61 = bf16[4,96,768]{2,1,0:T(8,128)(2,1)} collective-permute-done((bf16[4,96,768]{2,1,0:T(8,128)(2,1)}, bf16[4,96,768]{2,1,0:T(8,128)(2,1)}, u32[]{:S(2)}, u32[]{:S(2)}) %collective-permute-start.61) | collective-permute-done | bytes 589856 | tf_op jit(solution)/shard_map/ppermute | solution.py:27
  196.8 2.8 collective-permute-start.62
  199.6 3.8 %shard_map.209 = (bf16[1024,384]{1,0:T(8,128)(2,1)S(1)}, f32[192,1024]{1,0:T(8,128)S(1)}, bf16[1024,256]{1,0:T(8,128)(2,1)S(1)}, f32[8,1024]{1,0:T(8,128)S(1)}, ...) custom-call(s32[8]{0:T(128)S(1)} %concatenate.31.scal, ...), custom_call_target="tpu_custom_call" | custom-call | flops 2013265920 | bytes 5406752 | tf_op jit(solution)/shard_map/pallas_call | solution.py:72
  203.5 2.2 collective-permute-start.64
  210.7 9.5 %shard_map.210 = (f32[1024,256]{1,0:T(8,128)S(1)}, f32[1024,256]{1,0:T(8,128)S(1)}, f32[1024,256]{1,0:T(8,128)S(1)}, f32[8,768]{1,0:T(8,128)S(1)}) custom-call(s32[8]{0:T(128)S(1)} %concatenate.31.scal, bf16[1024,256]{1,0:T(8,128)(2,1)S(1)} %copy-done.44, bf16[2048,256]{1,0:T(8,128)(2,1)S(1)} %copy-done.38, bf16[2048,256]{1,0:T(8,128)(2,1)S(1)} %copy-done.40, ...), custom_call_target="tpu_custom_call" | custom-call | flops 2013265920 | bytes 4793376 | tf_op jit(solution)/shard_map/pallas_call | solution.py:72
  222.6 12.8 %collective-permute-done.40.refs_4_ = f32[8,768]{1,0:T(8,128)S(1)} collective-permute-done((f32[8,768]{1,0:T(8,128)S(1)}, f32[8,768]{1,0:T(8,128)S(1)}, u32[]{:S(2)}, u32[]{:S(2)}) %collective-permute-start.40) | collective-permute-done | bytes 24608 | tf_op jit(solution)/shard_map/ppermute | solution.py:684
  235.4 6.6 %shard_map.211 = (f32[512,768]{1,0:T(8,128)S(1)}, bf16[512,768]{1,0:T(8,128)(2,1)S(1)}, f32[4,96,640]{2,1,0:T(8,128)S(1)}, bf16[4,96,640]{2,1,0:T(8,128)(2,1)S(1)}, f32[8,768]{1,0:T(8,128)S(1)}) custom-call(s32[8]{0:T(128)S(1)} %concatenate.31.scal, f32[1024,256]{1,0:T(8,128)S(1)} %get-tuple-element.78.refs_0_, f32[1024,256]{1,0:T(8,128)S(1)} %get-tuple-element.79.refs_1_, ...), custom_call_target="tpu_custom_call" | custom-call | flops 1811939328 | bytes 9888800 | tf_op jit(solution)/shard_map/pallas_call | solution.py:72
  245.5 5.8 %collective-permute-done.53 = bf16[4,96,192]{2,1,0:T(8,128)(2,1)S(1)} collective-permute-done((bf16[4,96,192]{2,1,0:T(8,128)(2,1)S(1)}, bf16[4,96,192]{2,1,0:T(8,128)(2,1)S(1)}, u32[]{:S(2)}, u32[]{:S(2)}) %collective-permute-start.53) | collective-permute-done | bytes 147488 | tf_op jit(solution)/shard_map/ppermute | solution.py:27
  251.8 3.8 %collective-permute-start.54 = (bf16[96,192]{1,0:T(8,128)(2,1)S(1)}, bf16[96,192]{1,0:T(8,128)(2,1)S(1)}, u32[]{:S(2)}, u32[]{:S(2)}) collective-permute-start(bf16[96,192]{1,0:T(8,128)(2,1)S(1)} %get-tuple-element.161), channel_id=1, source_target_pairs={{0,8},{8,0},{16,24},{24,16},{1,9},{9,1},{17,25},{25,17},{2,10},{10... | collective-permute-start | bytes 110600 | tf_op jit(solution)/shard_map/ppermute | solution.py:27
  258.9 2.4 collective-permute-start.48
  271.5 2.6 collective-permute-start.50
  281.2 3.2 %collective-permute-done.51 = bf16[96,640]{1,0:T(8,128)(2,1)} collective-permute-done((bf16[96,640]{1,0:T(8,128)(2,1)}, bf16[96,640]{1,0:T(8,128)(2,1)}, u32[]{:S(2)}, u32[]{:S(2)}) %collective-permute-start.51) | collective-permute-done | bytes 122912 | tf_op jit(solution)/shard_map/ppermute | solution.py:27
  288.6 6.1 %collective-permute-done.42.got = bf16[256,768]{1,0:T(8,128)(2,1)S(1)} collective-permute-done((bf16[256,768]{1,0:T(8,128)(2,1)S(1)}, bf16[256,768]{1,0:T(8,128)(2,1)S(1)}, u32[]{:S(2)}, u32[]{:S(2)}) %collective-permute-start.42) | collective-permute-done | bytes 393248 | tf_op jit(solution)/shard_map/ppermute | solution.py:27
  294.7 2.7 shard_map.212
  (283 shorter events, 100.4 us)
Async XLA Ops:
  4.2 13.6 %collective-permute-start.13 = (bf16[1,640]{1,0:T(2,128)(2,1)S(1)}, bf16[1,640]{1,0:T(2,128)(2,1)S(1)}, u32[]{:S(2)}, u32[]{:S(2)}) collective-permute-start(bf16[1,640]{1,0:T(2,128)(2,1)S(1)} %reshape.141), channel_id=1, source_target_pairs={{0,24},{8,16},{16,8},{24,0},{1,25},{9,17},{17,9},{25,1},{2,26},{10... | collective-permute-start | bytes 3848 | tf_op jit(solution)/shard_map/ppermute | solution.py:27
  11.8 13.8 %collective-permute-start.19 = (bf16[96,1024]{1,0:T(8,128)(2,1)S(1)}, bf16[96,1024]{1,0:T(8,128)(2,1)S(1)}, u32[]{:S(2)}, u32[]{:S(2)}) collective-permute-start(bf16[96,1024]{1,0:T(8,128)(2,1)S(1)} %get-tuple-element.165), channel_id=1, source_target_pairs={{0,16},{8,24},{16,0},{24,8},{1,17},{9,25},{17,1},{25,9},{2,18},{10... | collective-permute-start | bytes 589832 | tf_op jit(solution)/shard_map/ppermute | solution.py:27
  14.2 18.0 %collective-permute-start.18 = (bf16[96,1024]{1,0:T(8,128)(2,1)S(1)}, bf16[96,1024]{1,0:T(8,128)(2,1)S(1)}, u32[]{:S(2)}, u32[]{:S(2)}) collective-permute-start(bf16[96,1024]{1,0:T(8,128)(2,1)S(1)} %get-tuple-element.165), channel_id=1, source_target_pairs={{0,8},{8,0},{16,24},{24,16},{1,9},{9,1},{17,25},{25,17},{2,10},{10... | collective-permute-start | bytes 589832 | tf_op jit(solution)/shard_map/ppermute | solution.py:27
  17.8 14.5 %collective-permute-start.20 = (bf16[96,1024]{1,0:T(8,128)(2,1)S(1)}, bf16[96,1024]{1,0:T(8,128)(2,1)S(1)}, u32[]{:S(2)}, u32[]{:S(2)}) collective-permute-start(bf16[96,1024]{1,0:T(8,128)(2,1)S(1)} %get-tuple-element.165), channel_id=1, source_target_pairs={{0,24},{8,16},{16,8},{24,0},{1,25},{9,17},{17,9},{25,1},{2,26},{10... | collective-permute-start | bytes 589832 | tf_op jit(solution)/shard_map/ppermute | solution.py:27
  18.9 25.6 %collective-permute-start.22 = (bf16[96,768]{1,0:T(8,128)(2,1)S(1)}, bf16[96,768]{1,0:T(8,128)(2,1)S(1)}, u32[]{:S(2)}, u32[]{:S(2)}) collective-permute-start(bf16[96,768]{1,0:T(8,128)(2,1)S(1)} %bitcast.146), channel_id=1, source_target_pairs={{0,16},{8,24},{16,0},{24,8},{1,17},{9,25},{17,1},{25,9},{2,18},{10... | collective-permute-start | bytes 442376 | tf_op jit(solution)/shard_map/ppermute | solution.py:27
  20.4 24.2 %collective-permute-start.21 = (bf16[96,768]{1,0:T(8,128)(2,1)S(1)}, bf16[96,768]{1,0:T(8,128)(2,1)S(1)}, u32[]{:S(2)}, u32[]{:S(2)}) collective-permute-start(bf16[96,768]{1,0:T(8,128)(2,1)S(1)} %bitcast.147), channel_id=1, source_target_pairs={{0,8},{8,0},{16,24},{24,16},{1,9},{9,1},{17,25},{25,17},{2,10},{10... | collective-permute-start | bytes 442376 | tf_op jit(solution)/shard_map/ppermute | solution.py:27
  25.7 20.4 %collective-permute-start.23 = (bf16[96,768]{1,0:T(8,128)(2,1)S(1)}, bf16[96,768]{1,0:T(8,128)(2,1)S(1)}, u32[]{:S(2)}, u32[]{:S(2)}) collective-permute-start(bf16[96,768]{1,0:T(8,128)(2,1)S(1)} %bitcast.148), channel_id=1, source_target_pairs={{0,24},{8,16},{16,8},{24,0},{1,25},{9,17},{17,9},{25,1},{2,26},{10... | collective-permute-start | bytes 442376 | tf_op jit(solution)/shard_map/ppermute | solution.py:27
  32.2 17.5 %collective-permute-start.9 = (bf16[96,640]{1,0:T(8,128)(2,1)S(1)}, bf16[96,640]{1,0:T(8,128)(2,1)S(1)}, u32[]{:S(2)}, u32[]{:S(2)}) collective-permute-start(bf16[96,640]{1,0:T(8,128)(2,1)S(1)} %concatenate.32), channel_id=1, source_target_pairs={{0,24},{8,16},{16,8},{24,0},{1,25},{9,17},{17,9},{25,1},{2,26},{10... | collective-permute-start | bytes 368648 | tf_op jit(solution)/shard_map/ppermute | solution.py:27
  32.3 19.0 %collective-permute-start.3 = (bf16[256,768]{1,0:T(8,128)(2,1)}, bf16[256,768]{1,0:T(8,128)(2,1)}, u32[]{:S(2)}, u32[]{:S(2)}) collective-permute-start(bf16[256,768]{1,0:T(8,128)(2,1)} %bitcast.4.refs_0_.refs_8_.values), channel_id=1, source_target_pairs={{0,1},{1,0},{2,3},{3,2},{4,5},{5,4},{6,7},{7,6},{8,9},{9,8},{10,11... | collective-permute-start | bytes 1179656 | tf_op jit(solution)/shard_map/ppermute | solution.py:27
  46.1 33.6 %collective-permute-start.24 = (bf16[4,96,1024]{2,1,0:T(8,128)(2,1)S(1)}, bf16[4,96,1024]{2,1,0:T(8,128)(2,1)S(1)}, u32[]{:S(2)}, u32[]{:S(2)}) collective-permute-start(bf16[4,96,1024]{2,1,0:T(8,128)(2,1)S(1)} %pad_maximum_fusion.refs_0_), channel_id=1, source_target_pairs={{0,1},{1,0},{2,3},{3,2},{4,5},{5,4},{6,7},{7,6},{8,9},{9,8},{10,11... | collective-permute-start | bytes 2359304 | tf_op jit(solution)/shard_map/ppermute | solution.py:27
  48.3 30.9 %collective-permute-start.25 = (bf16[4,96,768]{2,1,0:T(8,128)(2,1)S(1)}, bf16[4,96,768]{2,1,0:T(8,128)(2,1)S(1)}, u32[]{:S(2)}, u32[]{:S(2)}) collective-permute-start(bf16[4,96,768]{2,1,0:T(8,128)(2,1)S(1)} %pad_maximum_fusion.1.refs_1_), channel_id=1, source_target_pairs={{0,1},{1,0},{2,3},{3,2},{4,5},{5,4},{6,7},{7,6},{8,9},{9,8},{10,11... | collective-permute-start | bytes 1769480 | tf_op jit(solution)/shard_map/ppermute | solution.py:27
  49.8 12.3 %collective-permute-start.1 = (bf16[256,768]{1,0:T(8,128)(2,1)}, bf16[256,768]{1,0:T(8,128)(2,1)}, u32[]{:S(2)}, u32[]{:S(2)}) collective-permute-start(bf16[256,768]{1,0:T(8,128)(2,1)} %bitcast.4.refs_0_.refs_8_.values), channel_id=1, source_target_pairs={{0,4},{2,6},{4,0},{6,2},{1,5},{3,7},{5,1},{7,3},{8,12},{10,14},{12... | collective-permute-start | bytes 1179656 | tf_op jit(solution)/shard_map/ppermute | solution.py:27
  51.3 27.9 %collective-permute-start.5 = (bf16[256,768]{1,0:T(8,128)(2,1)}, bf16[256,768]{1,0:T(8,128)(2,1)}, u32[]{:S(2)}, u32[]{:S(2)}) collective-permute-start(bf16[256,768]{1,0:T(8,128)(2,1)} %collective-permute-done.3.refs_4_), channel_id=1, source_target_pairs={{0,4},{2,6},{4,0},{6,2},{1,5},{3,7},{5,1},{7,3},{8,12},{10,14},{12... | collective-permute-start | bytes 1179656 | tf_op jit(solution)/shard_map/ppermute | solution.py:27
  59.6 28.0 %collective-permute-start = (bf16[256,768]{1,0:T(8,128)(2,1)}, bf16[256,768]{1,0:T(8,128)(2,1)}, u32[]{:S(2)}, u32[]{:S(2)}) collective-permute-start(bf16[256,768]{1,0:T(8,128)(2,1)} %bitcast.4.refs_0_.refs_8_.values), channel_id=1, source_target_pairs={{0,2},{2,0},{4,6},{6,4},{1,3},{3,1},{5,7},{7,5},{8,10},{10,8},{12,... | collective-permute-start | bytes 1179656 | tf_op jit(solution)/shard_map/ppermute | solution.py:27
  62.1 27.0 %collective-permute-start.10 = (bf16[4,96,640]{2,1,0:T(8,128)(2,1)S(1)}, bf16[4,96,640]{2,1,0:T(8,128)(2,1)}, u32[]{:S(2)}, u32[]{:S(2)}) collective-permute-start(bf16[4,96,640]{2,1,0:T(8,128)(2,1)S(1)} %pad_maximum_fusion.2.refs_8_), channel_id=1, source_target_pairs={{0,1},{1,0},{2,3},{3,2},{4,5},{5,4},{6,7},{7,6},{8,9},{9,8},{10,11... | collective-permute-start | bytes 1474568 | tf_op jit(solution)/shard_map/ppermute | solution.py:27
  87.6 31.4 %collective-permute-start.30 = (bf16[256,768]{1,0:T(8,128)(2,1)S(1)}, bf16[256,768]{1,0:T(8,128)(2,1)}, u32[]{:S(2)}, u32[]{:S(2)}) collective-permute-start(bf16[256,768]{1,0:T(8,128)(2,1)S(1)} %bitcast.132), channel_id=1, source_target_pairs={{0,4},{2,6},{4,0},{6,2},{1,5},{3,7},{5,1},{7,3},{8,12},{10,14},{12... | collective-permute-start | bytes 1179656 | tf_op jit(solution)/shard_map/ppermute | solution.py:27
  89.1 30.4 %collective-permute-start.29 = (bf16[256,768]{1,0:T(8,128)(2,1)S(1)}, bf16[256,768]{1,0:T(8,128)(2,1)S(1)}, u32[]{:S(2)}, u32[]{:S(2)}) collective-permute-start(bf16[256,768]{1,0:T(8,128)(2,1)S(1)} %bitcast.133), channel_id=1, source_target_pairs={{0,2},{2,0},{4,6},{6,4},{1,3},{3,1},{5,7},{7,5},{8,10},{10,8},{12,... | collective-permute-start | bytes 1179656 | tf_op jit(solution)/shard_map/ppermute | solution.py:27
  89.2 31.0 %collective-permute-start.27 = (bf16[768,256]{1,0:T(8,128)(2,1)}, bf16[768,256]{1,0:T(8,128)(2,1)}, u32[]{:S(2)}, u32[]{:S(2)}) collective-permute-start(bf16[768,256]{1,0:T(8,128)(2,1)} %get-tuple-element.60.refs_4_), channel_id=1, source_target_pairs={{0,4},{2,6},{4,0},{6,2},{1,5},{3,7},{5,1},{7,3},{8,12},{10,14},{12... | collective-permute-start | bytes 1179656 | tf_op jit(solution)/shard_map/ppermute | solution.py:27
  147.5 20.4 %collective-permute-start.34 = (bf16[512,768]{1,0:T(8,128)(2,1)S(1)}, bf16[512,768]{1,0:T(8,128)(2,1)S(1)}, u32[]{:S(2)}, u32[]{:S(2)}) collective-permute-start(bf16[512,768]{1,0:T(8,128)(2,1)S(1)} %get-tuple-element.70), channel_id=1, source_target_pairs={{0,2},{2,0},{4,6},{6,4},{1,3},{3,1},{5,7},{7,5},{8,10},{10,8},{12,... | collective-permute-start | bytes 2359304 | tf_op jit(solution)/shard_map/ppermute | solution.py:27
  156.6 27.8 %collective-permute-start.57 = (bf16[4,96,768]{2,1,0:T(8,128)(2,1)}, bf16[4,96,768]{2,1,0:T(8,128)(2,1)}, u32[]{:S(2)}, u32[]{:S(2)}) collective-permute-start(bf16[4,96,768]{2,1,0:T(8,128)(2,1)} %get-tuple-element.98), channel_id=1, source_target_pairs={{0,1},{1,0},{2,3},{3,2},{4,5},{5,4},{6,7},{7,6},{8,9},{9,8},{10,11... | collective-permute-start | bytes 1769480 | tf_op jit(solution)/shard_map/ppermute | solution.py:27
  170.4 24.1 %collective-permute-start.61 = (bf16[4,96,768]{2,1,0:T(8,128)(2,1)}, bf16[4,96,768]{2,1,0:T(8,128)(2,1)}, u32[]{:S(2)}, u32[]{:S(2)}) collective-permute-start(bf16[4,96,768]{2,1,0:T(8,128)(2,1)} %get-tuple-element.100), channel_id=1, source_target_pairs={{0,1},{1,0},{2,3},{3,2},{4,5},{5,4},{6,7},{7,6},{8,9},{9,8},{10,11... | collective-permute-start | bytes 1769480 | tf_op jit(solution)/shard_map/ppermute | solution.py:27
  171.4 37.1 %collective-permute-start.32 = (bf16[512,768]{1,0:T(8,128)(2,1)}, bf16[512,768]{1,0:T(8,128)(2,1)S(1)}, u32[]{:S(2)}, u32[]{:S(2)}) collective-permute-start(bf16[512,768]{1,0:T(8,128)(2,1)} %copy-done.30), channel_id=1, source_target_pairs={{0,2},{2,0},{4,6},{6,4},{1,3},{3,1},{5,7},{7,5},{8,10},{10,8},{12,... | collective-permute-start | bytes 2359304 | tf_op jit(solution)/shard_map/ppermute | solution.py:27
  182.9 11.7 %collective-permute-start.37 = (bf16[256,768]{1,0:T(8,128)(2,1)S(1)}, bf16[256,768]{1,0:T(8,128)(2,1)S(1)}, u32[]{:S(2)}, u32[]{:S(2)}) collective-permute-start(bf16[256,768]{1,0:T(8,128)(2,1)S(1)} %get-tuple-element.71.refs_0_), channel_id=1, source_target_pairs={{0,4},{2,6},{4,0},{6,2},{1,5},{3,7},{5,1},{7,3},{8,12},{10,14},{12... | collective-permute-start | bytes 1179656 | tf_op jit(solution)/shard_map/ppermute | solution.py:27
  185.8 17.7 %collective-permute-start.58 = (bf16[96,768]{1,0:T(8,128)(2,1)S(1)}, bf16[96,768]{1,0:T(8,128)(2,1)S(1)}, u32[]{:S(2)}, u32[]{:S(2)}) collective-permute-start(bf16[96,768]{1,0:T(8,128)(2,1)S(1)} %get-tuple-element.149), channel_id=1, source_target_pairs={{0,8},{8,0},{16,24},{24,16},{1,9},{9,1},{17,25},{25,17},{2,10},{10... | collective-permute-start | bytes 442376 | tf_op jit(solution)/shard_map/ppermute | solution.py:27
  188.0 17.7 %collective-permute-start.60 = (bf16[96,768]{1,0:T(8,128)(2,1)S(1)}, bf16[96,768]{1,0:T(8,128)(2,1)S(1)}, u32[]{:S(2)}, u32[]{:S(2)}) collective-permute-start(bf16[96,768]{1,0:T(8,128)(2,1)S(1)} %get-tuple-element.150), channel_id=1, source_target_pairs={{0,24},{8,16},{16,8},{24,0},{1,25},{9,17},{17,9},{25,1},{2,26},{10... | collective-permute-start | bytes 442376 | tf_op jit(solution)/shard_map/ppermute | solution.py:27
  196.8 23.4 %collective-permute-start.62 = (bf16[96,768]{1,0:T(8,128)(2,1)S(1)}, bf16[96,768]{1,0:T(8,128)(2,1)S(1)}, u32[]{:S(2)}, u32[]{:S(2)}) collective-permute-start(bf16[96,768]{1,0:T(8,128)(2,1)S(1)} %get-tuple-element.146), channel_id=1, source_target_pairs={{0,8},{8,0},{16,24},{24,16},{1,9},{9,1},{17,25},{25,17},{2,10},{10... | collective-permute-start | bytes 442376 | tf_op jit(solution)/shard_map/ppermute | solution.py:27
  203.5 18.3 %collective-permute-start.64 = (bf16[96,768]{1,0:T(8,128)(2,1)S(1)}, bf16[96,768]{1,0:T(8,128)(2,1)S(1)}, u32[]{:S(2)}, u32[]{:S(2)}) collective-permute-start(bf16[96,768]{1,0:T(8,128)(2,1)S(1)} %get-tuple-element.147), channel_id=1, source_target_pairs={{0,24},{8,16},{16,8},{24,0},{1,25},{9,17},{17,9},{25,1},{2,26},{10... | collective-permute-start | bytes 442376 | tf_op jit(solution)/shard_map/ppermute | solution.py:27
  205.6 16.1 %collective-permute-start.63 = (bf16[96,768]{1,0:T(8,128)(2,1)S(1)}, bf16[96,768]{1,0:T(8,128)(2,1)S(1)}, u32[]{:S(2)}, u32[]{:S(2)}) collective-permute-start(bf16[96,768]{1,0:T(8,128)(2,1)S(1)} %get-tuple-element.148), channel_id=1, source_target_pairs={{0,16},{8,24},{16,0},{24,8},{1,17},{9,25},{17,1},{25,9},{2,18},{10... | collective-permute-start | bytes 442376 | tf_op jit(solution)/shard_map/ppermute | solution.py:27
  206.4 29.0 %collective-permute-start.39 = (bf16[1024,384]{1,0:T(8,128)(2,1)S(1)}, bf16[1024,384]{1,0:T(8,128)(2,1)S(1)}, u32[]{:S(2)}, u32[]{:S(2)}) collective-permute-start(bf16[1024,384]{1,0:T(8,128)(2,1)S(1)} %get-tuple-element.81), channel_id=1, source_target_pairs={{1,0},{3,2},{5,4},{7,6},{9,8},{11,10},{13,12},{15,14},{17,16},{19,... | collective-permute-start | bytes 2359304 | tf_op jit(solution)/shard_map/ppermute | solution.py:671
  208.6 34.5 %collective-permute-start.33 = (bf16[256,768]{1,0:T(8,128)(2,1)S(1)}, bf16[256,768]{1,0:T(8,128)(2,1)S(1)}, u32[]{:S(2)}, u32[]{:S(2)}) collective-permute-start(bf16[256,768]{1,0:T(8,128)(2,1)S(1)} %add_convert_fusion.3), channel_id=1, source_target_pairs={{0,4},{2,6},{4,0},{6,2},{1,5},{3,7},{5,1},{7,3},{8,12},{10,14},{12... | collective-permute-start | bytes 1179656 | tf_op jit(solution)/shard_map/ppermute | solution.py:27
  220.2 15.2 %collective-permute-start.40 = (f32[8,768]{1,0:T(8,128)S(1)}, f32[8,768]{1,0:T(8,128)S(1)}, u32[]{:S(2)}, u32[]{:S(2)}) collective-permute-start(f32[8,768]{1,0:T(8,128)S(1)} %get-tuple-element.82), channel_id=1, source_target_pairs={{1,0},{3,2},{5,4},{7,6},{9,8},{11,10},{13,12},{15,14},{17,16},{19,... | collective-permute-start | bytes 73736 | tf_op jit(solution)/shard_map/ppermute | solution.py:684
  264.1 21.4 %collective-permute-start.41 = (bf16[512,768]{1,0:T(8,128)(2,1)S(1)}, bf16[512,768]{1,0:T(8,128)(2,1)}, u32[]{:S(2)}, u32[]{:S(2)}) collective-permute-start(bf16[512,768]{1,0:T(8,128)(2,1)S(1)} %copy-done.29), channel_id=1, source_target_pairs={{0,2},{2,0},{4,6},{6,4},{1,3},{3,1},{5,7},{7,5},{8,10},{10,8},{12,... | collective-permute-start | bytes 2359304 | tf_op jit(solution)/shard_map/ppermute | solution.py:27
  (84 other events, 626.3 us)

commit v2 on v1

--- a/solution.py
+++ b/solution.py
@@ -23,6 +23,10 @@
 SMEM = pl.BlockSpec(memory_space=pltpu.SMEM)
 
 
+def after(value, *others):
+    return lax.optimization_barrier((value,) + others)[0]
+
+
 def swap(shard, axis, by):
     return lax.ppermute(shard, axis, [(i, i ^ by) for i in range(lax.axis_size(axis))])
 
@@ -37,38 +41,58 @@
     return group % 32 == 0
 
 
-def gather_rows(shard):
+def gather_batch(shard):
     if not pairwise(shard.shape[0]):
-        whole = lax.all_gather(shard, ("batch", "seq"), axis=0, tiled=True)
-        return tuple(whole.reshape(2, 1, -1, shard.shape[1]))
-    count = lax.axis_size("batch")
-    stack = jnp.stack([shard] + [swap(shard, "batch", by) for by in range(1, count)])
+        return (shard,)
+    return (shard,) + tuple(swap(shard, "batch", by) for by in range(1, lax.axis_size("batch")))
+
+
+def gather_seq(shards):
+    rows, columns = shards[0].shape
+    if not pairwise(rows):
+        whole = lax.all_gather(shards[0], ("batch", "seq"), axis=0, tiled=True)
+        return tuple(whole.reshape(2, 1, -1, columns))
+    stack = jnp.stack(shards)
     return stack, swap(stack, "seq", 1)
 
 
-def scatter_rows(keep, sent):
-    if keep.shape[0] == 1:
-        whole = jnp.concatenate([keep[0].astype(b16), sent[0]])
-        return lax.psum_scatter(whole, ("batch", "seq"), scatter_dimension=0, tiled=True).astype(f32)
-    got = swap(sent, "seq", 1)
-    total = keep.astype(f32) + got.astype(f32)
-    pieces = [swap(total[by].astype(b16), "batch", by) for by in range(1, lax.axis_size("batch"))]
-    result = total[0]
-    for piece in pieces:
-        result = result + piece.astype(f32)
-    return result
-
-
-def scatter_heads(keep, sent):
-    got = swap(sent, "heads", 1)
-    rows = keep.shape[0] // 2
+def scatter_seq(sent):
+    return sent if sent.shape[0] == 1 else swap(sent, "seq", 1)
+
+
+def join_seq(*parts):
+    if parts[0][0].shape[0] == 1:
+        whole = [jnp.concatenate([keep[0].astype(b16), sent[0]]) for keep, sent in parts]
+        return None, jnp.concatenate(whole, axis=-1)
+    total = jnp.concatenate([keep.astype(f32) + got.astype(f32) for keep, got in parts], axis=-1)
+    return total[0], total[1:].astype(b16)
+
+
+def scatter_batch(own, rest, more, *others):
+    if own is None:
+        total = lax.psum_scatter(rest, ("batch", "seq"), scatter_dimension=0, tiled=True).astype(f32)
+        return total, None if more is None else lax.psum(more, "batch")
+    count = own.shape[0]
+    payloads = [rest[by] for by in range(rest.shape[0])]
+    if more is not None:
+        tail = jnp.pad(more, ((0, 0), (0, own.shape[1] - more.shape[1]))).astype(b16)
+        payloads = [jnp.concatenate([payload, tail]) for payload in payloads]
+    pieces = [swap(payload, "batch", by + 1) for by, payload in enumerate(payloads)]
+    for piece in after(pieces, *others):
+        own = own + piece[:count].astype(f32)
+        if more is not None:
+            more = more + piece[count:, : more.shape[1]].astype(f32)
+    return own, more
+
+
+def scatter_far(keep, got, rows):
     far = (keep[rows:].astype(f32) + got[rows:].astype(f32)).astype(b16)
     here = keep[:rows].astype(f32) + got[:rows].astype(f32)
     return here, swap(far, "heads", 2)
 
 
-def call(body, outs, *args, scratch=(), flops=0, limit=40):
-    in_specs = [SMEM] + [VMEM] * (len(args) - 1)
+def call(body, outs, *args, scratch=(), flops=0, limit=16, plain=False):
+    in_specs = [pl.BlockSpec()] * len(args) if plain else [SMEM] + [VMEM] * (len(args) - 1)
     return pl.pallas_call(
         body,
         out_shape=[jax.ShapeDtypeStruct(*o) for o in outs],
@@ -125,12 +149,57 @@
     return pl.ds(pl.multiple_of(start, size), size)
 
 
-def front_body(half, quarter, scal, *refs):
-    pieces, refs = refs[:8], refs[8:]
-    w_own, w_other, gain, bias, taps = refs[:5]
-    normed, form, projected, wpad, query, key, value = refs[5:12]
-    rows_in, proj = refs[12:]
+def shard_body(heads, qkv, out_w, small, kernel, shard, rows):
+    for part in range(3):
+        shard[:, part * 128 : part * 128 + 128] = qkv[part, :, 0:128]
+    thirds = [qkv[part, :, 128:192].astype(f32) for part in range(3)]
+    turned = out_w[...].astype(f32).T
+    shard[:, 384:512] = jnp.concatenate(thirds[:2], axis=1).astype(b16)
+    shard[:, 512:640] = jnp.concatenate([thirds[2], turned[:, 0:64]], axis=1).astype(b16)
+    shard[:, 640:768] = turned[:, 64:192].astype(b16)
+    rows[...] = jnp.zeros_like(rows)
+    count = kernel.shape[2]
+    rows[0:4, 0 : small.shape[1]] = small[...].astype(f32)
+    for part in range(3):
+        rows[4 + part * heads : 4 + part * heads + heads, 0:count] = kernel[part].astype(f32)
+    shard[:, 768:896] = rows[...].T[: shard.shape[0]].astype(b16)
+
+
+def small_rows(scal, stacks, heads, norms, taps, columns, features):
+    count = features.shape[0] // (2 * stacks[0].shape[0])
+    for rel_seq, stack in enumerate(stacks):
+        for rel in range(stack.shape[0]):
+            block = stack[rel, :, 768:896].astype(f32)
+            columns[group_rows(stack, rel, rel_seq, scal), :] = block
+            group = (scal[1] ^ rel) * 2 + (scal[2] ^ rel_seq)
+            features[pl.ds(pl.multiple_of(group * count, 8), count), :] = block[0:count]
+    norms[...] = columns[...].T[0:8]
+    taps[...] = jnp.zeros_like(taps)
+    low = lanes_like((1, 128)) < 64
+    for tap in range(KERNEL):
+        turned = features[pl.ds(tap, HEAD_DIM, stride=KERNEL), :].T
+        turned = jnp.concatenate([turned, jnp.zeros_like(turned)], axis=1)
+        for part in range(3):
+            one, two, three = (turned[4 + part * heads + i : 5 + part * heads + i] for i in range(3))
+            taps[4 + tap : 5 + tap, part * PADW : part * PADW + 128] = jnp.where(low, one, half_roll(two))
+            taps[4 + tap : 5 + tap, part * PADW + 128 : part * PADW + 256] = jnp.where(low, three, 0.0)
+
+
+def front_body(half, quarter, heads, paired, scal, *refs):
+    pieces, refs = refs[:4], refs[4:]
+    w_own, w_other, cot = refs[:3]
+    refs = refs[3:]
+    if not paired:
+        norms_in, taps_in, refs = refs[0], refs[1], refs[2:]
+    normed, form, projected, wpad, query, key, value, extra, norms, taps = refs[:10]
+    rows_in, proj, columns, features, wo = refs[10:]
     head = scal[0]
+    if paired:
+        small_rows(scal, (w_own, w_other), heads, norms, taps, columns, features)
+    else:
+        norms[...] = norms_in[...]
+        taps[...] = taps_in[...]
+    gain, bias = norms[0:1, :], norms[1:2, :]
     low = lanes_like((w_own.shape[1], 128)) < 64
     for rel_seq, stack in enumerate((w_own, w_other)):
         for rel in range(stack.shape[0]):
@@ -140,16 +209,24 @@
             shared = stack[rel, :, 384:512].astype(f32)
             wpad[rows, 128:256] = jnp.where(low, shared, 0.0).astype(b16)
             wpad[rows, 384:512] = jnp.where(low, half_roll(shared), 0.0).astype(b16)
-            wpad[rows, 640:768] = stack[rel, :, 512:640]
+            mid = stack[rel, :, 512:640].astype(f32)
+            last = half_roll(stack[rel, :, 640:768].astype(f32))
+            wpad[rows, 640:768] = jnp.where(low, mid, 0.0).astype(b16)
+            wo[rows, 0:128] = jnp.where(low, half_roll(mid), last)
+            wo[rows, 128:256] = last
+    extra[0:quarter, :] = cot[...]
+    width = heads * HEAD_DIM
+    extra[quarter : quarter + width, :] = wo[...].T[0:width].astype(b16)
     for index, piece in enumerate(pieces):
-        base = (head ^ (index % 4)) * quarter + (half if index < 4 else 0)
-        rows_in[ds(base, quarter), :] = piece[...]
+        base = (head ^ index) * quarter
+        rows_in[ds(half + base, quarter), :] = piece[0:quarter, :]
+        rows_in[ds(base, quarter), :] = piece[quarter : 2 * quarter, :]
     proj[0:16, :] = jnp.zeros((16, proj.shape[1]), b16)
 
     def project(block, own):
         base = block * quarter
         hat, _ = norm_rows(rows_in[ds(base, quarter), :].astype(f32))
-        rounded = (hat * gain[...] + bias[...]).astype(b16)
+        rounded = (hat * gain + bias).astype(b16)
         proj[pl.ds(pl.multiple_of(base + 16, 16), quarter), :] = dot(rounded, wpad[...]).astype(b16)
         if own:
             rows = ds(base - half, quarter)
@@ -176,10 +253,10 @@
                 continue
             cols = slice(part * PADW, part * PADW + PADW)
             rows = proj[pl.ds(pl.multiple_of(base, 16), quarter + 16), cols].astype(f32)
-            mixed = taps[0:1, cols] * rows[16:]
+            mixed = taps[4:5, cols] * rows[16:]
             for back in range(1, KERNEL):
                 earlier = pltpu.roll(rows, back, 0)[16:]
-                mixed = mixed + jnp.where(pos - back >= start, taps[back : back + 1, cols] * earlier, 0.0)
+                mixed = mixed + jnp.where(pos - back >= start, taps[4 + back : 5 + back, cols] * earlier, 0.0)
             mixed = mixed.astype(b16)
             if part == 0:
                 out[ds(base - half, quarter), :] = mixed * jnp.asarray(HEAD_DIM**-0.5, b16)
@@ -291,25 +368,23 @@
         finish(kb, key_sum[...], value_sum[...])
 
 
-def spread_groups(source, scal, keep, sent):
+def spread_groups(source, scal, keep, sent, cols=slice(None)):
     for rel_seq, out in enumerate((keep, sent)):
         for rel in range(out.shape[0]):
-            out[rel] = source[group_rows(out, rel, rel_seq, scal), :].astype(out.dtype)
-
-
-def remote_back_body(half, quarter, heads, scal, *refs):
-    branches, refs = refs[:4], refs[4:]
-    wo, query, key, value, out_t, lse = refs[:6]
-    remote, query_t, dout, row_dot, kt, proj_keep, proj_send = refs[6:13]
-    qm, dom, key_sum, value_sum, proj_grad, turned = refs[13:]
+            out[rel, :, cols] = source[group_rows(out, rel, rel_seq, scal), :].astype(out.dtype)
+
+
+def branch_body(quarter, heads, scal, *refs):
+    branches = refs[:4]
+    extra, out_t, dout, row_dot, keep, sent, proj_grad, turned = refs[4:]
     head = scal[0]
     width = heads * HEAD_DIM
-    masked_queries(query, qm, heads)
+    weights = jnp.concatenate([extra[quarter:, :], jnp.zeros((PADW - width, extra.shape[1]), b16)], axis=0)
     proj_grad[...] = jnp.zeros_like(proj_grad)
     row_dot[...] = jnp.zeros_like(row_dot)
     for rel, branch in enumerate(branches):
         base = (head ^ rel) * quarter
-        grad = dot(branch[...], wo[...]).astype(b16)
+        grad = dot(branch[...], weights, 1, 1).astype(b16)
         dout[ds(base, quarter), :] = grad
         attended = out_t[:, ds(base, quarter)]
         product = grad.astype(f32).T[:width] * attended
@@ -319,7 +394,15 @@
             )
         proj_grad[...] += dot(attended.astype(b16), branch[...])
     turned[...] = proj_grad[...].T
-    spread_groups(turned, scal, proj_keep, proj_send)
+    spread_groups(turned, scal, keep, sent)
+
+
+def remote_back_body(half, heads, scal, *refs):
+    query, key, value, dout, lse, row_dot = refs[:6]
+    remote, query_t, kt = refs[6:9]
+    qm, dom, key_sum, value_sum = refs[9:]
+    width = heads * HEAD_DIM
+    masked_queries(query, qm, heads)
     masked_queries(dout, dom, heads)
 
     @pl.loop(0, 2 * half // 256)
@@ -362,58 +445,59 @@
     for block in range(half // 256):
         cols = slice(block * 256, block * 256 + 256)
         turned = (query_t[:, cols] * scale).T
-        dq[cols, 0:128] = turned[:, 0:128]
+        dq[cols, 0:128] = turned[:, 0:128].astype(b16)
         dq[cols, 128:256] = jnp.concatenate(
             [turned[:, 128:width], jnp.zeros((256, PADW - width), f32)], axis=1
-        )
+        ).astype(b16)
     bounds = edges(scal)
     pos = half + lax.broadcasted_iota(jnp.int32, (8, 1), 0)
     start = doc_start(pos, bounds)
     for part, grads in enumerate((dq, dk_out, dv_out)):
         cols = slice(part * PADW, part * PADW + PADW)
-        rounded = grads[0:8, :].astype(b16).astype(f32)
+        rounded = grads[0:16, :].astype(b16).astype(f32)[0:8]
         result = jnp.zeros((8, PADW), f32)
         for back in range(1, KERNEL):
-            moved = pltpu.roll(jnp.where(pos - back >= start, taps[back : back + 1, cols] * rounded, 0.0), 8 - back, 0)
+            moved = pltpu.roll(jnp.where(pos - back >= start, taps[4 + back : 5 + back, cols] * rounded, 0.0), 8 - back, 0)
             place = lax.broadcasted_iota(jnp.int32, (8, 1), 0)
             result = result + jnp.where(place >= 8 - back, moved, 0.0)
         front[:, cols] = result
 
 
 def weights_body(scal, *refs):
-    first, second, first_o, second_o, inner, wo, outer = refs
-    for rel_seq, (one, two) in enumerate(((first, second), (first_o, second_o))):
-        for rel in range(one.shape[0]):
-            rows = group_rows(one, rel, rel_seq, scal)
-            width = inner.shape[1]
-            inner[rows, :] = one[rel, :, :width]
-            wo[rows, :] = one[rel, :, width:]
-            outer[rows, :] = two[rel]
+    own, other, inner, outer = refs
+    width = inner.shape[1]
+    for rel_seq, stack in enumerate((own, other)):
+        for rel in range(stack.shape[0]):
+            rows = group_rows(stack, rel, rel_seq, scal)
+            inner[rows, :] = stack[rel, :, :width]
+            outer[rows, :] = stack[rel, :, width:]
 
 
 def feed_body(half, quarter, scal, *refs):
-    attended, wos, inputs, cots = refs[0:4], refs[4:8], refs[8:12], refs[12:16]
-    inner, outer, gain, bias = refs[16:20]
-    normed, squared, inner_grad, keep, sent, middle_own = refs[20:]
+    attended, extras, inputs = refs[0:4], refs[4:8], refs[8:12]
+    inner, outer, norms = refs[12:15]
+    normed, squared, inner_grad, keep, sent, middle_own = refs[15:]
     head = scal[0]
     for rel in range(4):
         base = (head ^ rel) * quarter
         late = base >= half // 2
-        middle = inputs[rel][...].astype(f32)
+        middle = inputs[rel][0:quarter, :].astype(f32)
         for part in range(4):
             left = attended[part][ds(base, quarter), :]
             right = attended[part][ds(half + lax.rem(base, half // 2), quarter), :].astype(f32)
             right = jnp.where(late, half_roll(right), right).astype(b16)
-            middle = middle + dot(jnp.concatenate([left, right], axis=1), wos[part][...], 1, 1)
+            both = jnp.concatenate([left, right], axis=1)
+            weights = extras[part][quarter:, :]
+            middle = middle + dot(both[:, : weights.shape[0]], weights)
         if rel == 0:
             middle_own[...] = middle
         hat, _ = norm_rows(middle)
-        rounded = (hat * gain[...] + bias[...]).astype(b16)
+        rounded = (hat * norms[2:3, :] + norms[3:4, :]).astype(b16)
         rows = slice(rel * quarter, rel * quarter + quarter)
         normed[rows, :] = rounded
         positive = jnp.maximum(dot(rounded, inner[...]), 0.0)
         squared[rows, :] = (positive * positive).astype(b16)
-        grads = (dot(cots[rel][...], outer[...]) * 2.0 * positive).astype(b16)
+        grads = (dot(extras[rel][0:quarter, :], outer[...]) * 2.0 * positive).astype(b16)
         inner_grad[rows, :] = grads
         part = dot(grads, inner[...], 1, 1)
         place = slice((rel // 2) * quarter, (rel // 2) * quarter + quarter)
@@ -424,31 +508,32 @@
 
 
 def feed_grads_body(half, quarter, scal, *refs):
-    cots = refs[0:4]
+    extras = refs[0:4]
     normed, squared, inner_grad, outer = refs[4:8]
-    keep, sent, in_keep, in_send, out_keep, out_send = refs[8:14]
-    cot, total = refs[14:]
+    keep, sent, kept, away = refs[8:12]
+    cot, total = refs[12:]
+    width = total.shape[1]
     for rel in range(4):
         rows = slice(rel * quarter, rel * quarter + quarter)
-        cot[rows, :] = cots[rel][...]
+        cot[rows, :] = extras[rel][0:quarter, :]
         part = dot(squared[rows, :], outer[...], 1, 1)
         place = slice((rel // 2) * quarter, (rel // 2) * quarter + quarter)
         if rel % 2 == 0:
             keep[place, :] = part
         else:
             sent[place, :] = part.astype(b16)
-    for left, right, kept, away in ((cot, squared, out_keep, out_send), (normed, inner_grad, in_keep, in_send)):
+    for place, left, right in ((0, normed, inner_grad), (width, cot, squared)):
         for tile in range(total.shape[0] // 256):
             cols = slice(tile * 256, tile * 256 + 256)
             total[cols, :] = dot(left[:, cols], right[...], 0, 0)
-        spread_groups(total, scal, kept, away)
-
-
-def norm_back_body(scal, part, got, values, skip, gain, grad_in, rounded, sums):
+        spread_groups(total, scal, kept, away, slice(place, place + width))
+
+
+def norm_back_body(row, scal, part, got, values, skip, norms, grad_in, rounded, sums):
     del scal
-    grad = part[...] + got[...].astype(f32)
+    grad = part[...] + got[0 : part.shape[0], :].astype(f32)
     hat, inverse = norm_rows(values[...].astype(f32))
-    scaled = grad * gain[...]
+    scaled = grad * norms[row : row + 1, :]
     back = inverse * (
         scaled
         - jnp.mean(scaled, axis=-1, keepdims=True)
@@ -463,17 +548,16 @@
 
 
 def tail_body(half, quarter, scal, *refs):
-    dq, dk, dv, remote, front, projected, normed, form, wpad, taps = refs[:10]
-    keep, sent, w_keep, w_send, sums = refs[10:15]
-    mixed, proj_grad, total, dense = refs[15:]
-    head = scal[0]
+    dq, dk, dv, remote, front, projected, normed, taps = refs[:8]
+    proj_grad, w_keep, w_send, sums = refs[8:12]
+    mixed, total, dense = refs[12:]
     bounds = edges(scal)
     low = lanes_like((quarter, 128)) < 64
     sums[...] = jnp.zeros_like(sums)
     for block in range(half // quarter):
         rows = slice(block * quarter, block * quarter + quarter)
         shared = remote[rows, 256:384].astype(f32)
-        mixed[rows, 0:256] = dq[rows, :].astype(b16)
+        mixed[rows, 0:256] = dq[rows, :]
         mixed[rows, 256:384] = (dk[rows, 0:128] + remote[rows, 0:128].astype(f32)).astype(b16)
         mixed[rows, 384:512] = (dk[rows, 128:256] + jnp.where(low, shared, 0.0)).astype(b16)
         mixed[rows, 512:640] = (dv[rows, 0:128] + remote[rows, 128:256].astype(f32)).astype(b16)
@@ -490,13 +574,13 @@
             grads = mixed[pl.ds(pl.multiple_of(base, 16), quarter + 16), cols].astype(f32)
             values = projected[pl.ds(pl.multiple_of(base, 16), quarter + 16), cols].astype(f32)
             here = grads[:quarter]
-            result = taps[0:1, cols] * here
+            result = taps[4:5, cols] * here
             sums[4:5, cols] += jnp.sum(here * values[16:], axis=0, keepdims=True)
             for back in range(1, KERNEL):
                 same = pos - back >= start
                 held = jnp.where(same, grads, 0.0)
                 ahead = pltpu.roll(held, quarter + 16 - back, 0)[:quarter]
-                result = result + taps[back : back + 1, cols] * ahead
+                result = result + taps[4 + back : 5 + back, cols] * ahead
                 earlier = pltpu.roll(values, back, 0)[16:]
                 sums[4 + back : 5 + back, cols] += jnp.sum(held[:quarter] * earlier, axis=0, keepdims=True)
             proj_grad[ds(base, quarter), cols] = result.astype(b16)
@@ -507,13 +591,27 @@
             tail_pos = 2 * half - 16 + lax.broadcasted_iota(jnp.int32, (32, 1), 0)
             tail_start = doc_start(tail_pos, bounds)
             grads = mixed[half - 16 : half + 16, :].astype(f32)
-            result = taps[0:1, :] * grads[:16]
+            result = taps[4:5, :] * grads[:16]
             for back in range(1, KERNEL):
                 held = jnp.where(tail_pos - back >= tail_start, grads, 0.0)
-                result = result + taps[back : back + 1, :] * pltpu.roll(held, 32 - back, 0)[:16]
+                result = result + taps[4 + back : 5 + back, :] * pltpu.roll(held, 32 - back, 0)[:16]
             proj_grad[half - 16 : half, :] = (result + added).astype(b16)
 
-    for rel in range(4):
+    for tile in range(total.shape[0] // 256):
+        rows = slice(tile * 256, tile * 256 + 256)
+        total[rows, :] = dot(normed[:, rows], proj_grad[...], 0, 0)
+        for part in range(3):
+            dense[rows, part * 128 : part * 128 + 128] = total[rows, part * 256 : part * 256 + 128]
+        dense[rows, 384:512] = total[rows, 128:256] + half_roll(total[rows, 384:512])
+        dense[rows, 512:640] = total[rows, 640:768]
+    spread_groups(dense, scal, w_keep, w_send)
+
+
+def tail_norm_body(quarter, scal, proj_grad, wpad, form, second, keep, sent, sums):
+    head = scal[0]
+    sums[...] = jnp.zeros_like(sums)
+    sums[2:4, :] = second[0:2, :]
+    for rel in (1, 3, 0, 2):
         base = (head ^ rel) * quarter
         part = dot(proj_grad[ds(base, quarter), :], wpad[...], 1, 1)
         sums[0:1, :] += jnp.sum(part * form[ds(base, quarter), :].astype(f32), axis=0, keepdims=True)
@@ -523,20 +621,21 @@
             keep[place, :] = part
         else:
             sent[place, :] = part.astype(b16)
-    for tile in range(total.shape[0] // 256):
-        rows = slice(tile * 256, tile * 256 + 256)
-        total[rows, :] = dot(normed[:, rows], proj_grad[...], 0, 0)
-        for part in range(3):
-            dense[rows, part * 128 : part * 128 + 128] = total[rows, part * 256 : part * 256 + 128]
-        dense[rows, 384:512] = total[rows, 128:256] + half_roll(total[rows, 384:512])
-        dense[rows, 512:640] = total[rows, 640:768]
-    spread_groups(dense, scal, w_keep, w_send)
+    keep[2 * quarter :, :] = sums[...]
+    sent[2 * quarter :, :] = sums[...].astype(b16)
 
 
 def pad_heads(values, width):
     shaped = values.reshape(values.shape[:-1] + (3, width))
     padded = jnp.pad(shaped, [(0, 0)] * (shaped.ndim - 1) + [(0, PADW - width)])
     return padded.reshape(values.shape[:-1] + (3 * PADW,))
+
+
+def gather_small(norms, conv_kernel, model, width):
+    norms = lax.all_gather(norms, ("batch", "seq"), axis=0, tiled=True).astype(f32).T
+    taps = lax.all_gather(conv_kernel, ("batch", "seq"), axis=2, tiled=True).astype(f32)
+    taps = taps.reshape(3, width, KERNEL).transpose(2, 0, 1).reshape(KERNEL, 3 * width)
+    return jnp.pad(norms, ((0, 4), (0, 0))), jnp.pad(pad_heads(taps, width), ((4, 1), (0, 0)))
 
 
 def on_device(
@@ -563,58 +662,49 @@
     x_own = block_input.reshape(quarter, model)
     cot_own = cotangent.reshape(quarter, model)
 
-    small = jnp.concatenate([norm1_gain, norm1_bias, norm2_gain, norm2_bias, conv_kernel.reshape(-1)])
-    small = jnp.pad(small, (0, -small.shape[0] % 128)).reshape(1, -1)
-    if pairwise(group):
-        small_all = jnp.stack([small] + [swap(small, "batch", by) for by in range(1, groups // 2)])
-        small_all = jnp.concatenate([small_all, swap(small_all, "seq", 1)]).reshape(groups, -1)
-        order = jnp.arange(groups)
-        rel_of = (order % 2 ^ seq) * (groups // 2) + (order // 2 ^ batch)
-        small_all = jnp.sum(
-            jnp.where(rel_of[:, None, None] == order[None, :, None], small_all[None].astype(f32), 0.0), axis=1
+    share = conv_kernel.shape[2]
+
+    x_other = swap(x_own, "seq", 1)
+    x_pieces = gather_heads(jnp.concatenate([x_own, x_other]))
+
+    paired = pairwise(group)
+    qkv = qkv_weight
+    small = [norm1_gain, norm1_bias, norm2_gain, norm2_bias]
+    small_args = []
+    if paired:
+        (shard,) = call(
+            functools.partial(shard_body, heads), [((group, 896), b16)],
+            qkv.transpose(1, 0, 2), out_weight, jnp.stack(small), conv_kernel,
+            scratch=[pltpu.VMEM((128, 128), f32)], limit=4, plain=True,
         )
     else:
-        small_all = lax.all_gather(small, ("batch", "seq"), axis=0, tiled=True).astype(f32)
-    gain_one, bias_one, gain_two, bias_two = (
-        small_all[:, i * group : i * group + group].reshape(1, model) for i in range(4)
-    )
-    taps = small_all[:, 4 * group : 4 * group + conv_kernel.size].reshape((groups,) + conv_kernel.shape)
-    taps = taps.transpose(1, 2, 0, 3).reshape(3, width, KERNEL).transpose(2, 0, 1).reshape(KERNEL, 3 * width)
-    taps = pad_heads(taps, width)
-
-    qkv = qkv_weight
-    shard = jnp.concatenate(
-        [qkv[:, 0, :128], qkv[:, 1, :128], qkv[:, 2, :128], qkv[:, 0, 128:], qkv[:, 1, 128:], qkv[:, 2, 128:],
-         jnp.zeros((group, PADW - width), b16)], axis=1,
-    )
-    w_own, w_other = gather_rows(shard)
-
-    x_pieces = gather_heads(x_own)
-    y_pieces = gather_heads(swap(x_own, "seq", 1))
-
-    normed_one, form_one, projected, wpad, query, key, value = call(
-        functools.partial(front_body, half, quarter),
+        small_args = gather_small(jnp.stack(small, axis=1), conv_kernel, model, width)
+        shard = jnp.concatenate(
+            [qkv[:, 0, :128], qkv[:, 1, :128], qkv[:, 2, :128], qkv[:, 0, 128:], qkv[:, 1, 128:], qkv[:, 2, 128:],
+             out_weight.T, jnp.zeros((group, 128), b16)], axis=1,
+        )
+    shards = gather_batch(shard)
+    w_own, w_other = gather_seq(shards)
+
+    feed_shards = gather_batch(after(jnp.concatenate([inner_weight, outer_weight.T], axis=1), shards))
+
+    normed_one, form_one, projected, wpad, query, key, value, extra, norms, taps = call(
+        functools.partial(front_body, half, quarter, heads, paired),
         [
             ((half, model), b16), ((half, model), b16), ((half + 16, 3 * PADW), b16), ((model, 3 * PADW), b16),
-            ((half, PADW), b16), ((2 * half, PADW), b16), ((2 * half, PADW), b16),
+            ((half, PADW), b16), ((2 * half, PADW), b16), ((2 * half, PADW), b16), ((quarter + width, model), b16),
+            ((8, model), f32), ((8, 3 * PADW), f32),
         ],
-        scal, *x_pieces, *y_pieces, w_own, w_other, gain_one, bias_one, taps,
-        scratch=[pltpu.VMEM((2 * half, model), b16), pltpu.VMEM((2 * half + 16, 3 * PADW), b16)],
-        flops=4 * half * model * 3 * width,
-    )
-
-    inner_wo = jnp.concatenate(
-        [inner_weight, jnp.pad(out_weight.T, ((0, 0), (0, PADW - width)))], axis=1
-    )
-    first_own, first_other = gather_rows(inner_wo)
-    second_own, second_other = gather_rows(outer_weight.T)
-    inner_full, wo_own, outer_full = call(
-        weights_body,
-        [((model, hidden), b16), ((model, PADW), b16), ((model, hidden), b16)],
-        scal, first_own, second_own, first_other, second_other,
-    )
-    wo_pieces = gather_heads(wo_own)
-    cot_pieces = gather_heads(cot_own)
+        scal, *x_pieces, w_own, w_other, cot_own, *small_args,
+        scratch=[
+            pltpu.VMEM((2 * half, model), b16), pltpu.VMEM((2 * half + 16, 3 * PADW), b16),
+            pltpu.VMEM((model, 128), f32), pltpu.VMEM((KERNEL * HEAD_DIM, 128), f32), pltpu.VMEM((model, PADW), f32),
+        ],
+        flops=4 * half * model * 3 * width, limit=12,
+    )
+
+    feed_own, feed_other = gather_seq(after(feed_shards, query))
+    extra_pieces = gather_heads(extra)
 
     packed, out_t, lse = call(
         functools.partial(attention_body, half, heads),
@@ -624,93 +714,109 @@
             pltpu.VMEM((width, 2 * half), b16), pltpu.VMEM((heads, half, PADW), b16),
             pltpu.VMEM((8, half), f32), pltpu.VMEM((8, half), f32),
         ],
-        flops=4 * half * half * width,
+        flops=4 * half * half * width, limit=7,
     )
     packed_pieces = gather_heads(packed)
+    feed_own, feed_other, _ = lax.optimization_barrier((feed_own, feed_other, packed))
+    inner_full, outer_full = call(
+        weights_body, [((model, hidden), b16), ((model, hidden), b16)], scal, feed_own, feed_other, limit=4,
+    )
 
     normed_two, squared, inner_grad, keep, sent, middle_own = call(
         functools.partial(feed_body, half, quarter),
         [((half, model), b16), ((half, hidden), b16), ((half, hidden), b16),
          ((2 * quarter, model), f32), ((2 * quarter, model), b16), ((quarter, model), f32)],
-        scal, *packed_pieces, *wo_pieces, *x_pieces, *cot_pieces, inner_full, outer_full, gain_two, bias_two,
-        flops=2 * half * model * (model + 3 * hidden),
-    )
-    dn_here, dn_far = scatter_heads(keep, sent)
+        scal, *packed_pieces, *extra_pieces, *x_pieces, inner_full, outer_full, norms,
+        flops=2 * half * model * (model + 3 * hidden), limit=12,
+    )
+    got = swap(sent, "heads", 1)
+    out_keep, out_sent, ff_keep, ff_send = call(
+        functools.partial(feed_grads_body, half, quarter),
+        [((2 * quarter, model), f32), ((2 * quarter, model), b16),
+         (stacks + (2 * hidden,), b16), (stacks + (2 * hidden,), b16)],
+        scal, *extra_pieces, normed_two, squared, inner_grad, outer_full,
+        scratch=[pltpu.VMEM((half, model), b16), pltpu.VMEM((model, hidden), f32)],
+        flops=6 * half * model * hidden, limit=10,
+    )
+    ff_got = scatter_seq(ff_send)
+    dn_here, dn_far = scatter_far(keep, after(got, ff_send), quarter)
     middle_grad, branch, sums_two = call(
-        norm_back_body,
+        functools.partial(norm_back_body, 2),
         [((quarter, model), f32), ((quarter, model), b16), ((8, model), f32)],
-        scal, dn_here, dn_far, middle_own, cot_own, gain_two,
+        scal, dn_here, dn_far, middle_own, cot_own, norms, limit=6,
     )
     branch_pieces = gather_heads(branch)
-
-    keep, sent, in_keep, in_send, ff_keep, ff_send = call(
-        functools.partial(feed_grads_body, half, quarter),
-        [((2 * quarter, model), f32), ((2 * quarter, model), b16)]
-        + [(stacks + (hidden,), d) for d in (f32, b16, f32, b16)],
-        scal, *cot_pieces, normed_two, squared, inner_grad, outer_full,
-        scratch=[pltpu.VMEM((half, model), b16), pltpu.VMEM((model, hidden), f32)],
-        flops=6 * half * model * hidden,
-    )
-    out_here, out_far = scatter_heads(keep, sent)
-    block_output = (middle_own + out_here + out_far.astype(f32)).astype(b16)
-    inner_out = scatter_rows(in_keep, in_send)
-    outer_out = scatter_rows(ff_keep, ff_send)
-
-    remote, query_t, dout, row_dot, kt, pj_keep, pj_send = call(
-        functools.partial(remote_back_body, half, quarter, heads),
-        [((half, 384), b16), ((width, half), f32), ((half, PADW), b16), ((8, half), f32), ((width, 2 * half), b16),
-         (stacks + (width,), f32), (stacks + (width,), b16)],
-        scal, *branch_pieces, wo_own, query, key, value, out_t, lse,
+    out_got = swap(after(out_sent, branch), "heads", 1)
+
+    dout, row_dot, pj_keep, pj_send = call(
+        functools.partial(branch_body, quarter, heads),
+        [((half, PADW), b16), ((8, half), f32), (stacks + (width,), f32), (stacks + (width,), b16)],
+        scal, *branch_pieces, extra, out_t,
+        scratch=[pltpu.VMEM((width, model), f32), pltpu.VMEM((model, width), f32)],
+        flops=4 * half * model * width, limit=6,
+    )
+    pj_got = scatter_seq(pj_send)
+    out_here, out_far = scatter_far(out_keep, after(out_got, dout), quarter)
+    remote, query_t, kt = call(
+        functools.partial(remote_back_body, half, heads),
+        [((half, 384), b16), ((width, half), f32), ((width, 2 * half), b16)],
+        scal, query, key, value, dout, lse, row_dot,
         scratch=[
             pltpu.VMEM((heads, half, PADW), b16), pltpu.VMEM((heads, half, PADW), b16),
             pltpu.VMEM((KB, PADW), f32), pltpu.VMEM((KB, PADW), f32),
-            pltpu.VMEM((width, model), f32), pltpu.VMEM((model, width), f32),
         ],
-        flops=10 * half * half * width,
+        flops=10 * half * half * width, limit=8,
     )
     remote_in = lax.ppermute(remote, "seq", [(1, 0)])
-    proj_out = scatter_rows(pj_keep, pj_send)
 
     dq, dk, dv, front = call(
         functools.partial(local_back_body, half, heads),
-        [((half, PADW), f32), ((half, PADW), f32), ((half, PADW), f32), ((8, 3 * PADW), f32)],
+        [((half, PADW), b16), ((half, PADW), f32), ((half, PADW), f32), ((8, 3 * PADW), f32)],
         scal, query, key, value, dout, lse, row_dot, kt, query_t, taps,
         scratch=[
             pltpu.VMEM((heads, half, PADW), b16), pltpu.VMEM((heads, half, PADW), b16),
             pltpu.VMEM((KB, PADW), f32), pltpu.VMEM((KB, PADW), f32), pltpu.VMEM((width, half), f32),
         ],
-        flops=10 * half * half * width,
+        flops=10 * half * half * width, limit=8,
     )
     front_in = lax.ppermute(front, "seq", [(1, 0)])
-
-    keep, sent, w_keep, w_send, sums = call(
+    ff_got, pj_got = after((ff_got, pj_got), dq)
+    ff_own, ff_rest = join_seq((ff_keep, ff_got), (pj_keep, pj_got))
+
+    proj_grad, w_keep, w_send, sums_taps = call(
         functools.partial(tail_body, half, quarter),
-        [((2 * quarter, model), f32), ((2 * quarter, model), b16),
-         (stacks + (640,), f32), (stacks + (640,), b16), ((8, 3 * PADW), f32)],
-        scal, dq, dk, dv, remote_in, front_in, projected, normed_one, form_one, wpad, taps,
+        [((half, 3 * PADW), b16), (stacks + (640,), f32), (stacks + (640,), b16), ((8, 3 * PADW), f32)],
+        scal, dq, dk, dv, remote_in, front_in, projected, normed_one, taps,
         scratch=[
-            pltpu.VMEM((half + 16, 3 * PADW), b16), pltpu.VMEM((half, 3 * PADW), b16),
-            pltpu.VMEM((model, 3 * PADW), f32), pltpu.VMEM((model, 640), f32),
+            pltpu.VMEM((half + 16, 3 * PADW), b16), pltpu.VMEM((model, 3 * PADW), f32), pltpu.VMEM((model, 640), f32),
         ],
-        flops=4 * half * model * 3 * width,
-    )
-    norms = jnp.concatenate([sums[0:2], sums_two[0:2]])
-    norms = norms + swap(norms, "heads", 1)
-    norms = norms + swap(norms, "heads", 2)
-    small = jnp.concatenate([norms, sums[4:8]])
-    if pairwise(group):
-        small = small + swap(small, "seq", 1)
-        small = sum([swap(small, "batch", by) for by in range(1, groups // 2)], small)
-    else:
-        small = lax.psum(small, ("batch", "seq"))
-
-    dn_here, dn_far = scatter_heads(keep, sent)
-    qkv_out = scatter_rows(w_keep, w_send)
+        flops=2 * half * model * 3 * width, limit=12,
+    )
+    w_got = scatter_seq(w_send)
+    keep, sent, sums = call(
+        functools.partial(tail_norm_body, quarter),
+        [((2 * quarter + 8, model), f32), ((2 * quarter + 8, model), b16), ((8, model), f32)],
+        scal, proj_grad, wpad, form_one, sums_two,
+        flops=2 * half * model * 3 * width, limit=8,
+    )
+    got = swap(sent, "heads", 1)
+    dn_here, dn_far = scatter_far(keep, got, quarter)
+    ff_out, _ = scatter_batch(ff_own, ff_rest, None, sent)
+
+    small = sums + got[2 * quarter :].astype(f32) + dn_far[quarter:].astype(f32)
+    small = jnp.concatenate([small[0:4], sums_taps[4:8]])
+    small = small + swap(small, "seq", 1)
+    cut = small.shape[1] // 2
+    small = jnp.concatenate([small[:, :cut], small[:, cut:]])
+    qkv_own, qkv_rest = join_seq((w_keep, w_got))
+    qkv_out, small = scatter_batch(qkv_own, qkv_rest, small)
+    small = jnp.concatenate([small[:8], small[8:]], axis=1)
     input_grad, _, _ = call(
-        norm_back_body,
+        functools.partial(norm_back_body, 0),
         [((quarter, model), f32), ((quarter, model), b16), ((8, model), f32)],
-        scal, dn_here, dn_far, x_own, middle_grad, gain_one,
-    )
+        scal, dn_here, dn_far, x_own, middle_grad, norms, limit=6,
+    )
+    block_output = (middle_own + out_here + out_far.astype(f32)).astype(b16)
 
     qkv_out = jnp.stack(
         [
@@ -723,7 +829,6 @@
     gains = lax.dynamic_slice_in_dim(small[0:4], own * group, group, 1)
     kernel_out = small[4 : 4 + KERNEL].reshape(KERNEL, 3, PADW)[:, :, :width].reshape(KERNEL, 3, heads, HEAD_DIM)
     kernel_out = kernel_out.transpose(1, 2, 3, 0).reshape(3, heads, HEAD_DIM * KERNEL)
-    share = conv_kernel.shape[2]
     kernel_out = lax.dynamic_slice_in_dim(kernel_out, own * share, share, 2)
     return (
         block_output.reshape(block_input.shape),
@@ -732,11 +837,11 @@
         gains[1],
         qkv_out,
         kernel_out,
-        proj_out.T,
+        ff_out[:, 2 * hidden :].T,
         gains[2],
         gains[3],
-        inner_out,
-        outer_out.T,
+        ff_out[:, :hidden],
+        ff_out[:, hidden : 2 * hidden].T,
     )
 
 

time: 299 us -> 240 us (0.80)
  starting transfers between devices: 82.7 us -> 50.2 us
  local copies, waits for them, and re-layouts: 37.4 us -> 12.2 us
  waiting for transfers between devices: 96.8 us -> 103 us
  Pallas kernels: 65.2 us -> 61.2 us
    ppermute x63 -> x37, starting transfers between devices: 79.9 us -> 47.4 us  [swap(): lax.ppermute(shard, axis, [(i, i ^ by) for i in range(lax.axis_size(axis))])]
    ppermute x1, waiting for transfers between devices: 0.01 us -> 15.8 us  [on_device(): remote_in = lax.ppermute(remote, 'seq', [(1, 0)])]
    unnamed x104 -> x81, local copies, waits for them, and re-layouts: 23.5 us -> 9.47 us
    ppermute x1, waiting for transfers between devices: 12.8 us -> 3.53 us  [on_device(): front_in = lax.ppermute(front, 'seq', [(1, 0)])]
    pallas_call x10 -> x13, Pallas kernels: 65.2 us -> 61.2 us  [call(): pl.pallas_call(body, out_shape=[jax.ShapeDtypeStruct(*o) for o in outs],...]
    reshape x9 -> x0, local copies, waits for them, and re-layouts: 3.2 us -> none  [the longest x1 1.14 us: pad_heads(): return padded.reshape(values.shape[:-1] + (3 * PADW,))]
    another operation x9 -> x6, other arithmetic: 6.05 us -> 3.17 us  [the longest x2 1.86 us: gather_seq(): stack = jnp.stack(shards)]
    ppermute x63 -> x37, waiting for transfers between devices: 83.9 us -> 83.6 us  [swap(): lax.ppermute(shard, axis, [(i, i ^ by) for i in range(lax.axis_size(axis))])]
  transfers between devices with their start and end apart: 65 -> 39, of which waited for: 23 -> 17; matrix products, arithmetic and copies ran while one was open for 8% -> 5% of each run, Pallas kernels for 17% -> 21%
where the time goes in v2:
time: 240 us
  waiting for transfers between devices  103 us (43%)
  Pallas kernels  61.2 us (26%)
  starting transfers between devices  50.2 us (21%)
  local copies, waits for them, and re-layouts  12.2 us (5%)
  other arithmetic  12 us (5%)
    ppermute x37, waiting for transfers between devices, swap(): lax.ppermute(shard, axis, [(i, i ^ by) for i in range(lax.axis_size(axis))])  83.6 us
    pallas_call x13, Pallas kernels, call(): pl.pallas_call(body, out_shape=[jax.ShapeDtypeStruct(*o) for o in outs],...  61.2 us
    ppermute x37, starting transfers between devices, swap(): lax.ppermute(shard, axis, [(i, i ^ by) for i in range(lax.axis_size(axis))])  47.4 us
    ppermute x1, waiting for transfers between devices, on_device(): remote_in = lax.ppermute(remote, 'seq', [(1, 0)])  15.8 us
    unnamed x81, local copies, waits for them, and re-layouts  9.47 us
  transfers between devices with their start and end apart: 39, of which 17 were waited for; matrix products, arithmetic and copies ran while one was open for 5% of the time, Pallas kernels for 21%

profile of v2, /device:TPU:0, one launch (start us, length us, event | category | flops | bytes accessed | tf_op | source)
XLA Modules:
  0.0 239.9 jit_solution(13757782082891204898)
XLA Ops:
  0.7 3.1 %collective-permute-start = (bf16[256,768]{1,0:T(8,128)(2,1)}, bf16[256,768]{1,0:T(8,128)(2,1)S(1)}, u32[]{:S(2)}, u32[]{:S(2)}) collective-permute-start(bf16[256,768]{1,0:T(8,128)(2,1)} %bitcast.75), channel_id=1, source_target_pairs={{0,1},{1,0},{2,3},{3,2},{4,5},{5,4},{6,7},{7,6},{8,9},{9,8},{10,11... | collective-permute-start | bytes 1179656 | tf_op jit(solution)/shard_map/ppermute | solution.py:31
  3.8 9.3 %collective-permute-done = bf16[256,768]{1,0:T(8,128)(2,1)S(1)} collective-permute-done((bf16[256,768]{1,0:T(8,128)(2,1)}, bf16[256,768]{1,0:T(8,128)(2,1)S(1)}, u32[]{:S(2)}, u32[]{:S(2)}) %collective-permute-start) | collective-permute-done | bytes 393248 | tf_op jit(solution)/shard_map/ppermute | solution.py:31
  16.2 3.7 %collective-permute-start.6 = (bf16[96,896]{1,0:T(8,128)(2,1)S(1)}, bf16[96,896]{1,0:T(8,128)(2,1)S(1)}, u32[]{:S(2)}, u32[]{:S(2)}) collective-permute-start(bf16[96,896]{1,0:T(8,128)(2,1)S(1)} %shard_map.203), channel_id=1, source_target_pairs={{0,24},{8,16},{16,8},{24,0},{1,25},{9,17},{17,9},{25,1},{2,26},{10... | collective-permute-start | bytes 516104 | tf_op jit(solution)/shard_map/ppermute | solution.py:31
  20.7 4.7 %collective-permute-done.6 = bf16[96,896]{1,0:T(8,128)(2,1)S(1)} collective-permute-done((bf16[96,896]{1,0:T(8,128)(2,1)S(1)}, bf16[96,896]{1,0:T(8,128)(2,1)S(1)}, u32[]{:S(2)}, u32[]{:S(2)}) %collective-permute-start.6) | collective-permute-done | bytes 172064 | tf_op jit(solution)/shard_map/ppermute | solution.py:31
  25.3 8.0 %collective-permute-done.5 = bf16[96,896]{1,0:T(8,128)(2,1)S(1)} collective-permute-done((bf16[96,896]{1,0:T(8,128)(2,1)S(1)}, bf16[96,896]{1,0:T(8,128)(2,1)S(1)}, u32[]{:S(2)}, u32[]{:S(2)}) %collective-permute-start.5) | collective-permute-done | bytes 172064 | tf_op jit(solution)/shard_map/ppermute | solution.py:31
  37.3 2.5 %collective-permute-start.16 = (bf16[96,1536]{1,0:T(8,128)(2,1)}, bf16[96,1536]{1,0:T(8,128)(2,1)}, u32[]{:S(2)}, u32[]{:S(2)}) collective-permute-start(bf16[96,1536]{1,0:T(8,128)(2,1)} %pad_maximum_fusion.4), channel_id=1, source_target_pairs={{0,24},{8,16},{16,8},{24,0},{1,25},{9,17},{17,9},{25,1},{2,26},{10... | collective-permute-start | bytes 884744 | tf_op jit(solution)/shard_map/ppermute | solution.py:31
  39.8 10.3 %collective-permute-done.7.refs_5_ = bf16[4,96,896]{2,1,0:T(8,128)(2,1)} collective-permute-done((bf16[4,96,896]{2,1,0:T(8,128)(2,1)S(1)}, bf16[4,96,896]{2,1,0:T(8,128)(2,1)}, u32[]{:S(2)}, u32[]{:S(2)}) %collective-permute-start.7) | collective-permute-done | bytes 688160 | tf_op jit(solution)/shard_map/ppermute | solution.py:31
  52.4 11.0 %shard_map.204 = (bf16[1024,768]{1,0:T(8,128)(2,1)S(1)}, bf16[1024,768]{1,0:T(8,128)(2,1)S(1)}, bf16[1040,768]{1,0:T(8,128)(2,1)S(1)}, bf16[768,768]{1,0:T(8,128...) custom-call(s32[8]{0:T(128)S(1)} %concatenate.39.scal, ...), custom_call_target="tpu_custom_call" | custom-call | flops 1811939328 | bytes 4915232 | tf_op jit(solution)/shard_map/pallas_call | solution.py:96
  69.2 8.7 %shard_map.205 = (bf16[1536,128]{1,0:T(8,128)(2,1)S(1)}, f32[192,1024]{1,0:T(8,128)S(1)}, f32[8,1024]{1,0:T(8,128)S(1)}) custom-call(s32[8]{0:T(128)S(1)} %concatenate.39.scal, bf16[1024,256]{1,0:T(8,128)(2,1)S(1)} %get-tuple-element.76.query.refs_0_, bf16[2048,256]{1,0:T(8,128)(2,1)S(1)} %get-tuple-element.77.key.refs_1_, ...), custom_call_target="tpu_custom_call" | custom-call | flops 805306368 | bytes 2621472 | tf_op jit(solution)/shard_map/pallas_call | solution.py:96
  79.5 2.5 %collective-permute-done.12.refs_6_.refs_2_ = bf16[448,768]{1,0:T(8,128)(2,1)S(1)} collective-permute-done((bf16[448,768]{1,0:T(8,128)(2,1)S(1)}, bf16[448,768]{1,0:T(8,128)(2,1)S(1)}, u32[]{:S(2)}, u32[]{:S(2)}) %collective-permute-start.12) | collective-permute-done | bytes 688160 | tf_op jit(solution)/shard_map/ppermute | solution.py:31
  82.5 7.1 %collective-permute-done.9.refs_2_ = bf16[1536,128]{1,0:T(8,128)(2,1)S(1)} collective-permute-done((bf16[1536,128]{1,0:T(8,128)(2,1)S(1)}, bf16[1536,128]{1,0:T(8,128)(2,1)S(1)}, u32[]{:S(2)}, u32[]{:S(2)}) %collective-permute-start.9) | collective-permute-done | bytes 393248 | tf_op jit(solution)/shard_map/ppermute | solution.py:31
  89.5 5.0 %collective-permute-done.17.refs_1_ = bf16[4,96,1536]{2,1,0:T(8,128)(2,1)S(1)} collective-permute-done((bf16[4,96,1536]{2,1,0:T(8,128)(2,1)S(1)}, bf16[4,96,1536]{2,1,0:T(8,128)(2,1)S(1)}, u32[]{:S(2)}, u32[]{:S(2)}) %collective-permute-start.17) | collective-permute-done | bytes 1179680 | tf_op jit(solution)/shard_map/ppermute | solution.py:31
  95.3 9.4 %shard_map.207 = (bf16[1024,768]{1,0:T(8,128)(2,1)S(1)}, bf16[1024,768]{1,0:T(8,128)(2,1)S(1)}, bf16[1024,768]{1,0:T(8,128)(2,1)S(1)}, f32[512,768]{1,0:T(8,128)...) custom-call(s32[8]{0:T(128)S(1)} %concatenate.39.scal, bf16[1536,128]{1,0:T(8,128)(2,1)S(1)} %get-tuple-element.79.refs_0_, ...), custom_call_target="tpu_custom_call" | custom-call | flops 4831838208 | bytes 9855008 | tf_op jit(solution)/shard_map/pallas_call | solution.py:96
  104.8 5.8 %shard_map.208 = (f32[512,768]{1,0:T(8,128)S(1)}, bf16[512,768]{1,0:T(8,128)(2,1)}, bf16[4,96,1536]{2,1,0:T(8,128)(2,1)S(1)}, bf16[4,96,1536]{2,1,0:T(8,128)(2,1)}) custom-call(s32[8]{0:T(128)S(1)} %concatenate.39.scal, bf16[448,768]{1,0:T(8,128)(2,1)S(1)} %get-tuple-element.80.refs_4_.refs_0_, bf16[448,768]{1,0:T(8,128)(2,1)S(1)} %collective-permute-done.11.refs_5_.refs_1_, ...), custom_call_target="tpu_custom_call" | custom-call | flops 3623878656 | bytes 8650784 | tf_op jit(solution)/shard_map/pallas_call | solution.py:96
  112.5 11.2 %collective-permute-done.19.got = bf16[256,768]{1,0:T(8,128)(2,1)S(1)} collective-permute-done((bf16[256,768]{1,0:T(8,128)(2,1)S(1)}, bf16[256,768]{1,0:T(8,128)(2,1)S(1)}, u32[]{:S(2)}, u32[]{:S(2)}) %collective-permute-start.19) | collective-permute-done | bytes 393248 | tf_op jit(solution)/shard_map/ppermute | solution.py:31
  126.9 5.0 %collective-permute-start.34 = (bf16[4,96,1536]{2,1,0:T(8,128)(2,1)}, bf16[4,96,1536]{2,1,0:T(8,128)(2,1)}, u32[]{:S(2)}, u32[]{:S(2)}) collective-permute-start(bf16[4,96,1536]{2,1,0:T(8,128)(2,1)} %get-tuple-element.99), channel_id=1, source_target_pairs={{0,1},{1,0},{2,3},{3,2},{4,5},{5,4},{6,7},{7,6},{8,9},{9,8},{10,11... | collective-permute-start | bytes 3538952 | tf_op jit(solution)/shard_map/ppermute | solution.py:31
  132.1 5.4 %collective-permute-done.22.refs_2_ = bf16[256,768]{1,0:T(8,128)(2,1)} collective-permute-done((bf16[256,768]{1,0:T(8,128)(2,1)}, bf16[256,768]{1,0:T(8,128)(2,1)}, u32[]{:S(2)}, u32[]{:S(2)}) %collective-permute-start.22) | collective-permute-done | bytes 393248 | tf_op jit(solution)/shard_map/ppermute | solution.py:31
  137.5 2.1 collective-permute-done.23.refs_3_
  140.7 2.9 %shard_map.210 = (bf16[1024,256]{1,0:T(8,128)(2,1)S(1)}, f32[8,1024]{1,0:T(8,128)S(1)}, f32[4,96,192]{2,1,0:T(8,128)S(1)}, bf16[4,96,192]{2,1,0:T(8,128)(2,1)S(1)}) custom-call(s32[8]{0:T(128)S(1)} %concatenate.39.scal, bf16[256,768]{1,0:T(8,128)(2,1)} %get-tuple-element.101.refs_0_, bf16[256,768]{1,0:T(8,128)(2,1)} %collective-permute-done.21.refs_1_, ...), custom_call_target="tpu_custom_call" | custom-call | flops 603979776 | bytes 3047456 | tf_op jit(solution)/shard_map/pallas_call | solution.py:96
  143.5 5.0 %collective-permute-start.35 = (bf16[4,96,192]{2,1,0:T(8,128)(2,1)S(1)}, bf16[4,96,192]{2,1,0:T(8,128)(2,1)S(1)}, u32[]{:S(2)}, u32[]{:S(2)}) collective-permute-start(bf16[4,96,192]{2,1,0:T(8,128)(2,1)S(1)} %get-tuple-element.134), channel_id=1, source_target_pairs={{0,1},{1,0},{2,3},{3,2},{4,5},{5,4},{6,7},{7,6},{8,9},{9,8},{10,11... | collective-permute-start | bytes 442376 | tf_op jit(solution)/shard_map/ppermute | solution.py:31
  150.0 2.2 shard_map.211
  152.3 8.0 %shard_map.212 = (bf16[1024,256]{1,0:T(8,128)(2,1)S(1)}, f32[1024,256]{1,0:T(8,128)S(1)}, f32[1024,256]{1,0:T(8,128)S(1)}, f32[8,768]{1,0:T(8,128)S(1)}) custom-call(s32[8]{0:T(128)S(1)} %concatenate.39.scal, bf16[1024,256]{1,0:T(8,128)(2,1)S(1)} %copy-done.30, bf16[2048,256]{1,0:T(8,128)(2,1)S(1)} %copy-done.26, bf16[2048,256]{1,0:T(8,128)(2,1)S(1)} %copy-done.28, ...), custom_call_target="tpu_custom_call" | custom-call | flops 2013265920 | bytes 4808736 | tf_op jit(solution)/shard_map/pallas_call | solution.py:96
  165.1 2.8 %collective-permute-start.38 = (bf16[96,1728]{1,0:T(8,128)(2,1)S(1)}, bf16[96,1728]{1,0:T(8,128)(2,1)S(1)}, u32[]{:S(2)}, u32[]{:S(2)}) collective-permute-start(bf16[96,1728]{1,0:T(8,128)(2,1)S(1)} %get-tuple-element.178), channel_id=1, source_target_pairs={{0,24},{8,16},{16,8},{24,0},{1,25},{9,17},{17,9},{25,1},{2,26},{10... | collective-permute-start | bytes 995336 | tf_op jit(solution)/shard_map/ppermute | solution.py:31
  169.2 3.5 %collective-permute-done.26.refs_4_ = f32[8,768]{1,0:T(8,128)S(1)} collective-permute-done((f32[8,768]{1,0:T(8,128)S(1)}, f32[8,768]{1,0:T(8,128)S(1)}, u32[]{:S(2)}, u32[]{:S(2)}) %collective-permute-start.26) | collective-permute-done | bytes 24608 | tf_op jit(solution)/shard_map/ppermute | solution.py:782
  174.0 15.8 %collective-permute-done.25.refs_3_ = bf16[1024,384]{1,0:T(8,128)(2,1)S(1)} collective-permute-done((bf16[1024,384]{1,0:T(8,128)(2,1)S(1)}, bf16[1024,384]{1,0:T(8,128)(2,1)S(1)}, u32[]{:S(2)}, u32[]{:S(2)}) %collective-permute-start.25) | collective-permute-done | bytes 786464 | tf_op jit(solution)/shard_map/ppermute | solution.py:770
  189.8 6.1 %shard_map.213 = (bf16[1024,768]{1,0:T(8,128)(2,1)S(1)}, f32[4,96,640]{2,1,0:T(8,128)S(1)}, bf16[4,96,640]{2,1,0:T(8,128)(2,1)}, f32[8,768]{1,0:T(8,128)S(1)}) custom-call(s32[8]{0:T(128)S(1)} %concatenate.39.scal, bf16[1024,256]{1,0:T(8,128)(2,1)S(1)} %get-tuple-element.111.refs_0_, f32[1024,256]{1,0:T(8,128)S(1)} %get-tuple-element.112.refs_1_, ...), custom_call_target="tpu_custom_call" | custom-call | flops 905969664 | bytes 6627360 | tf_op jit(solution)/shard_map/pallas_call | solution.py:96
  195.9 2.1 shard_map.214
  204.4 9.5 %collective-permute-done.30 = bf16[4,96,640]{2,1,0:T(8,128)(2,1)} collective-permute-done((bf16[4,96,640]{2,1,0:T(8,128)(2,1)}, bf16[4,96,640]{2,1,0:T(8,128)(2,1)}, u32[]{:S(2)}, u32[]{:S(2)}) %collective-permute-start.30) | collective-permute-done | bytes 491552 | tf_op jit(solution)/shard_map/ppermute | solution.py:31
  215.1 6.7 %collective-permute-start.29 = (f32[8,768]{1,0:T(8,128)S(1)}, f32[8,768]{1,0:T(8,128)S(1)}, u32[]{:S(2)}, u32[]{:S(2)}) collective-permute-start(f32[8,768]{1,0:T(8,128)S(1)} %pad_maximum_fusion.6), channel_id=1, source_target_pairs={{0,1},{1,0},{2,3},{3,2},{4,5},{5,4},{6,7},{7,6},{8,9},{9,8},{10,11... | collective-permute-start | bytes 73736 | tf_op jit(solution)/shard_map/ppermute | solution.py:31
  223.7 2.7 %collective-permute-start.33 = (bf16[112,640]{1,0:T(8,128)(2,1)S(1)}, bf16[112,640]{1,0:T(8,128)(2,1)S(1)}, u32[]{:S(2)}, u32[]{:S(2)}) collective-permute-start(bf16[112,640]{1,0:T(8,128)(2,1)S(1)} %get-tuple-element.196), channel_id=1, source_target_pairs={{0,24},{8,16},{16,8},{24,0},{1,25},{9,17},{17,9},{25,1},{2,26},{10... | collective-permute-start | bytes 430088 | tf_op jit(solution)/shard_map/ppermute | solution.py:31
  228.3 2.2 shard_map.215
  234.3 2.9 %collective-permute-done.32 = bf16[112,640]{1,0:T(8,128)(2,1)S(1)} collective-permute-done((bf16[112,640]{1,0:T(8,128)(2,1)S(1)}, bf16[112,640]{1,0:T(8,128)(2,1)S(1)}, u32[]{:S(2)}, u32[]{:S(2)}) %collective-permute-start.32) | collective-permute-done | bytes 143392 | tf_op jit(solution)/shard_map/ppermute | solution.py:31
  (188 shorter events, 51.6 us)
Async XLA Ops:
  0.7 12.4 %collective-permute-start = (bf16[256,768]{1,0:T(8,128)(2,1)}, bf16[256,768]{1,0:T(8,128)(2,1)S(1)}, u32[]{:S(2)}, u32[]{:S(2)}) collective-permute-start(bf16[256,768]{1,0:T(8,128)(2,1)} %bitcast.75), channel_id=1, source_target_pairs={{0,1},{1,0},{2,3},{3,2},{4,5},{5,4},{6,7},{7,6},{8,9},{9,8},{10,11... | collective-permute-start | bytes 1179656 | tf_op jit(solution)/shard_map/ppermute | solution.py:31
  14.2 20.9 %collective-permute-start.2 = (bf16[512,768]{1,0:T(8,128)(2,1)S(1)}, bf16[512,768]{1,0:T(8,128)(2,1)S(1)}, u32[]{:S(2)}, u32[]{:S(2)}) collective-permute-start(bf16[512,768]{1,0:T(8,128)(2,1)S(1)} %pad_maximum_fusion.2.refs_0_.refs_8_), channel_id=1, source_target_pairs={{0,4},{2,6},{4,0},{6,2},{1,5},{3,7},{5,1},{7,3},{8,12},{10,14},{12... | collective-permute-start | bytes 2359304 | tf_op jit(solution)/shard_map/ppermute | solution.py:31
  16.2 9.1 %collective-permute-start.6 = (bf16[96,896]{1,0:T(8,128)(2,1)S(1)}, bf16[96,896]{1,0:T(8,128)(2,1)S(1)}, u32[]{:S(2)}, u32[]{:S(2)}) collective-permute-start(bf16[96,896]{1,0:T(8,128)(2,1)S(1)} %shard_map.203), channel_id=1, source_target_pairs={{0,24},{8,16},{16,8},{24,0},{1,25},{9,17},{17,9},{25,1},{2,26},{10... | collective-permute-start | bytes 516104 | tf_op jit(solution)/shard_map/ppermute | solution.py:31
  19.9 13.4 %collective-permute-start.5 = (bf16[96,896]{1,0:T(8,128)(2,1)S(1)}, bf16[96,896]{1,0:T(8,128)(2,1)S(1)}, u32[]{:S(2)}, u32[]{:S(2)}) collective-permute-start(bf16[96,896]{1,0:T(8,128)(2,1)S(1)} %shard_map.203), channel_id=1, source_target_pairs={{0,16},{8,24},{16,0},{24,8},{1,17},{9,25},{17,1},{25,9},{2,18},{10... | collective-permute-start | bytes 516104 | tf_op jit(solution)/shard_map/ppermute | solution.py:31
  19.9 13.4 %collective-permute-start.4 = (bf16[96,896]{1,0:T(8,128)(2,1)S(1)}, bf16[96,896]{1,0:T(8,128)(2,1)S(1)}, u32[]{:S(2)}, u32[]{:S(2)}) collective-permute-start(bf16[96,896]{1,0:T(8,128)(2,1)S(1)} %shard_map.203), channel_id=1, source_target_pairs={{0,8},{8,0},{16,24},{24,16},{1,9},{9,1},{17,25},{25,17},{2,10},{10... | collective-permute-start | bytes 516104 | tf_op jit(solution)/shard_map/ppermute | solution.py:31
  33.5 16.7 %collective-permute-start.7 = (bf16[4,96,896]{2,1,0:T(8,128)(2,1)S(1)}, bf16[4,96,896]{2,1,0:T(8,128)(2,1)}, u32[]{:S(2)}, u32[]{:S(2)}) collective-permute-start(bf16[4,96,896]{2,1,0:T(8,128)(2,1)S(1)} %pad_maximum_fusion.3.refs_4_), channel_id=1, source_target_pairs={{0,1},{1,0},{2,3},{3,2},{4,5},{5,4},{6,7},{7,6},{8,9},{9,8},{10,11... | collective-permute-start | bytes 2064392 | tf_op jit(solution)/shard_map/ppermute | solution.py:31
  35.0 15.2 %collective-permute-start.1 = (bf16[512,768]{1,0:T(8,128)(2,1)S(1)}, bf16[512,768]{1,0:T(8,128)(2,1)}, u32[]{:S(2)}, u32[]{:S(2)}) collective-permute-start(bf16[512,768]{1,0:T(8,128)(2,1)S(1)} %pad_maximum_fusion.2.refs_0_.refs_8_), channel_id=1, source_target_pairs={{0,2},{2,0},{4,6},{6,4},{1,3},{3,1},{5,7},{7,5},{8,10},{10,8},{12,... | collective-permute-start | bytes 2359304 | tf_op jit(solution)/shard_map/ppermute | solution.py:31
  35.1 15.2 %collective-permute-start.3 = (bf16[512,768]{1,0:T(8,128)(2,1)S(1)}, bf16[512,768]{1,0:T(8,128)(2,1)}, u32[]{:S(2)}, u32[]{:S(2)}) collective-permute-start(bf16[512,768]{1,0:T(8,128)(2,1)S(1)} %collective-permute-done.2.refs_2_.refs_10_), channel_id=1, source_target_pairs={{0,2},{2,0},{4,6},{6,4},{1,3},{3,1},{5,7},{7,5},{8,10},{10,8},{12,... | collective-permute-start | bytes 2359304 | tf_op jit(solution)/shard_map/ppermute | solution.py:31
  37.3 27.3 %collective-permute-start.16 = (bf16[96,1536]{1,0:T(8,128)(2,1)}, bf16[96,1536]{1,0:T(8,128)(2,1)}, u32[]{:S(2)}, u32[]{:S(2)}) collective-permute-start(bf16[96,1536]{1,0:T(8,128)(2,1)} %pad_maximum_fusion.4), channel_id=1, source_target_pairs={{0,24},{8,16},{16,8},{24,0},{1,25},{9,17},{17,9},{25,1},{2,26},{10... | collective-permute-start | bytes 884744 | tf_op jit(solution)/shard_map/ppermute | solution.py:31
  39.8 24.8 %collective-permute-start.15 = (bf16[96,1536]{1,0:T(8,128)(2,1)}, bf16[96,1536]{1,0:T(8,128)(2,1)}, u32[]{:S(2)}, u32[]{:S(2)}) collective-permute-start(bf16[96,1536]{1,0:T(8,128)(2,1)} %pad_maximum_fusion.4), channel_id=1, source_target_pairs={{0,16},{8,24},{16,0},{24,8},{1,17},{9,25},{17,1},{25,9},{2,18},{10... | collective-permute-start | bytes 884744 | tf_op jit(solution)/shard_map/ppermute | solution.py:31
  50.1 14.5 %collective-permute-start.14 = (bf16[96,1536]{1,0:T(8,128)(2,1)}, bf16[96,1536]{1,0:T(8,128)(2,1)}, u32[]{:S(2)}, u32[]{:S(2)}) collective-permute-start(bf16[96,1536]{1,0:T(8,128)(2,1)} %pad_maximum_fusion.4), channel_id=1, source_target_pairs={{0,8},{8,0},{16,24},{24,16},{1,9},{9,1},{17,25},{25,17},{2,10},{10... | collective-permute-start | bytes 884744 | tf_op jit(solution)/shard_map/ppermute | solution.py:31
  64.6 17.3 %collective-permute-start.12 = (bf16[448,768]{1,0:T(8,128)(2,1)S(1)}, bf16[448,768]{1,0:T(8,128)(2,1)S(1)}, u32[]{:S(2)}, u32[]{:S(2)}) collective-permute-start(bf16[448,768]{1,0:T(8,128)(2,1)S(1)} %get-tuple-element.80.refs_4_.refs_0_), channel_id=1, source_target_pairs={{0,4},{2,6},{4,0},{6,2},{1,5},{3,7},{5,1},{7,3},{8,12},{10,14},{12... | collective-permute-start | bytes 2064392 | tf_op jit(solution)/shard_map/ppermute | solution.py:31
  67.6 26.9 %collective-permute-start.17 = (bf16[4,96,1536]{2,1,0:T(8,128)(2,1)S(1)}, bf16[4,96,1536]{2,1,0:T(8,128)(2,1)S(1)}, u32[]{:S(2)}, u32[]{:S(2)}) collective-permute-start(bf16[4,96,1536]{2,1,0:T(8,128)(2,1)S(1)} %pad_maximum_fusion.1.refs_0_), channel_id=1, source_target_pairs={{0,1},{1,0},{2,3},{3,2},{4,5},{5,4},{6,7},{7,6},{8,9},{9,8},{10,11... | collective-permute-start | bytes 3538952 | tf_op jit(solution)/shard_map/ppermute | solution.py:31
  78.9 10.6 %collective-permute-start.9 = (bf16[1536,128]{1,0:T(8,128)(2,1)S(1)}, bf16[1536,128]{1,0:T(8,128)(2,1)S(1)}, u32[]{:S(2)}, u32[]{:S(2)}) collective-permute-start(bf16[1536,128]{1,0:T(8,128)(2,1)S(1)} %get-tuple-element.79.refs_0_), channel_id=1, source_target_pairs={{0,4},{2,6},{4,0},{6,2},{1,5},{3,7},{5,1},{7,3},{8,12},{10,14},{12... | collective-permute-start | bytes 1179656 | tf_op jit(solution)/shard_map/ppermute | solution.py:31
  79.5 15.8 %collective-permute-start.11 = (bf16[448,768]{1,0:T(8,128)(2,1)S(1)}, bf16[448,768]{1,0:T(8,128)(2,1)S(1)}, u32[]{:S(2)}, u32[]{:S(2)}) collective-permute-start(bf16[448,768]{1,0:T(8,128)(2,1)S(1)} %get-tuple-element.80.refs_4_.refs_0_), channel_id=1, source_target_pairs={{0,2},{2,0},{4,6},{6,4},{1,3},{3,1},{5,7},{7,5},{8,10},{10,8},{12,... | collective-permute-start | bytes 2064392 | tf_op jit(solution)/shard_map/ppermute | solution.py:31
  82.0 13.3 %collective-permute-start.13 = (bf16[448,768]{1,0:T(8,128)(2,1)S(1)}, bf16[448,768]{1,0:T(8,128)(2,1)S(1)}, u32[]{:S(2)}, u32[]{:S(2)}) collective-permute-start(bf16[448,768]{1,0:T(8,128)(2,1)S(1)} %collective-permute-done.12.refs_6_.refs_2_), channel_id=1, source_target_pairs={{0,2},{2,0},{4,6},{6,4},{1,3},{3,1},{5,7},{7,5},{8,10},{10,8},{12,... | collective-permute-start | bytes 2064392 | tf_op jit(solution)/shard_map/ppermute | solution.py:31
  82.0 13.3 %collective-permute-start.8 = (bf16[1536,128]{1,0:T(8,128)(2,1)S(1)}, bf16[1536,128]{1,0:T(8,128)(2,1)S(1)}, u32[]{:S(2)}, u32[]{:S(2)}) collective-permute-start(bf16[1536,128]{1,0:T(8,128)(2,1)S(1)} %get-tuple-element.79.refs_0_), channel_id=1, source_target_pairs={{0,2},{2,0},{4,6},{6,4},{1,3},{3,1},{5,7},{7,5},{8,10},{10,8},{12,... | collective-permute-start | bytes 1179656 | tf_op jit(solution)/shard_map/ppermute | solution.py:31
  112.2 11.5 %collective-permute-start.19 = (bf16[256,768]{1,0:T(8,128)(2,1)S(1)}, bf16[256,768]{1,0:T(8,128)(2,1)S(1)}, u32[]{:S(2)}, u32[]{:S(2)}) collective-permute-start(bf16[256,768]{1,0:T(8,128)(2,1)S(1)} %get-tuple-element.176), channel_id=1, source_target_pairs={{0,4},{2,6},{4,0},{6,2},{1,5},{3,7},{5,1},{7,3},{8,12},{10,14},{12... | collective-permute-start | bytes 1179656 | tf_op jit(solution)/shard_map/ppermute | solution.py:31
  126.5 11.0 %collective-permute-start.22 = (bf16[256,768]{1,0:T(8,128)(2,1)}, bf16[256,768]{1,0:T(8,128)(2,1)}, u32[]{:S(2)}, u32[]{:S(2)}) collective-permute-start(bf16[256,768]{1,0:T(8,128)(2,1)} %get-tuple-element.101.refs_0_), channel_id=1, source_target_pairs={{0,4},{2,6},{4,0},{6,2},{1,5},{3,7},{5,1},{7,3},{8,12},{10,14},{12... | collective-permute-start | bytes 1179656 | tf_op jit(solution)/shard_map/ppermute | solution.py:31
  126.9 21.7 %collective-permute-start.20 = (bf16[512,768]{1,0:T(8,128)(2,1)}, bf16[512,768]{1,0:T(8,128)(2,1)}, u32[]{:S(2)}, u32[]{:S(2)}) collective-permute-start(bf16[512,768]{1,0:T(8,128)(2,1)} %get-tuple-element.102), channel_id=1, source_target_pairs={{0,2},{2,0},{4,6},{6,4},{1,3},{3,1},{5,7},{7,5},{8,10},{10,8},{12,... | collective-permute-start | bytes 2359304 | tf_op jit(solution)/shard_map/ppermute | solution.py:31
  126.9 36.3 %collective-permute-start.34 = (bf16[4,96,1536]{2,1,0:T(8,128)(2,1)}, bf16[4,96,1536]{2,1,0:T(8,128)(2,1)}, u32[]{:S(2)}, u32[]{:S(2)}) collective-permute-start(bf16[4,96,1536]{2,1,0:T(8,128)(2,1)} %get-tuple-element.99), channel_id=1, source_target_pairs={{0,1},{1,0},{2,3},{3,2},{4,5},{5,4},{6,7},{7,6},{8,9},{9,8},{10,11... | collective-permute-start | bytes 3538952 | tf_op jit(solution)/shard_map/ppermute | solution.py:31
  143.5 19.6 %collective-permute-start.35 = (bf16[4,96,192]{2,1,0:T(8,128)(2,1)S(1)}, bf16[4,96,192]{2,1,0:T(8,128)(2,1)S(1)}, u32[]{:S(2)}, u32[]{:S(2)}) collective-permute-start(bf16[4,96,192]{2,1,0:T(8,128)(2,1)S(1)} %get-tuple-element.134), channel_id=1, source_target_pairs={{0,1},{1,0},{2,3},{3,2},{4,5},{5,4},{6,7},{7,6},{8,9},{9,8},{10,11... | collective-permute-start | bytes 442376 | tf_op jit(solution)/shard_map/ppermute | solution.py:31
  149.6 48.4 %collective-permute-start.24 = (bf16[256,768]{1,0:T(8,128)(2,1)S(1)}, bf16[256,768]{1,0:T(8,128)(2,1)S(1)}, u32[]{:S(2)}, u32[]{:S(2)}) collective-permute-start(bf16[256,768]{1,0:T(8,128)(2,1)S(1)} %add_convert_fusion.2), channel_id=1, source_target_pairs={{0,4},{2,6},{4,0},{6,2},{1,5},{3,7},{5,1},{7,3},{8,12},{10,14},{12... | collective-permute-start | bytes 1179656 | tf_op jit(solution)/shard_map/ppermute | solution.py:31
  160.3 12.4 %collective-permute-start.26 = (f32[8,768]{1,0:T(8,128)S(1)}, f32[8,768]{1,0:T(8,128)S(1)}, u32[]{:S(2)}, u32[]{:S(2)}) collective-permute-start(f32[8,768]{1,0:T(8,128)S(1)} %get-tuple-element.115), channel_id=1, source_target_pairs={{1,0},{3,2},{5,4},{7,6},{9,8},{11,10},{13,12},{15,14},{17,16},{19,... | collective-permute-start | bytes 73736 | tf_op jit(solution)/shard_map/ppermute | solution.py:782
  161.6 28.2 %collective-permute-start.25 = (bf16[1024,384]{1,0:T(8,128)(2,1)S(1)}, bf16[1024,384]{1,0:T(8,128)(2,1)S(1)}, u32[]{:S(2)}, u32[]{:S(2)}) collective-permute-start(bf16[1024,384]{1,0:T(8,128)(2,1)S(1)} %get-tuple-element.114), channel_id=1, source_target_pairs={{1,0},{3,2},{5,4},{7,6},{9,8},{11,10},{13,12},{15,14},{17,16},{19,... | collective-permute-start | bytes 2359304 | tf_op jit(solution)/shard_map/ppermute | solution.py:770
  165.1 34.9 %collective-permute-start.38 = (bf16[96,1728]{1,0:T(8,128)(2,1)S(1)}, bf16[96,1728]{1,0:T(8,128)(2,1)S(1)}, u32[]{:S(2)}, u32[]{:S(2)}) collective-permute-start(bf16[96,1728]{1,0:T(8,128)(2,1)S(1)} %get-tuple-element.178), channel_id=1, source_target_pairs={{0,24},{8,16},{16,8},{24,0},{1,25},{9,17},{17,9},{25,1},{2,26},{10... | collective-permute-start | bytes 995336 | tf_op jit(solution)/shard_map/ppermute | solution.py:31
  167.8 32.2 %collective-permute-start.37 = (bf16[96,1728]{1,0:T(8,128)(2,1)S(1)}, bf16[96,1728]{1,0:T(8,128)(2,1)S(1)}, u32[]{:S(2)}, u32[]{:S(2)}) collective-permute-start(bf16[96,1728]{1,0:T(8,128)(2,1)S(1)} %get-tuple-element.179), channel_id=1, source_target_pairs={{0,16},{8,24},{16,0},{24,8},{1,17},{9,25},{17,1},{25,9},{2,18},{10... | collective-permute-start | bytes 995336 | tf_op jit(solution)/shard_map/ppermute | solution.py:31
  172.7 27.3 %collective-permute-start.36 = (bf16[96,1728]{1,0:T(8,128)(2,1)S(1)}, bf16[96,1728]{1,0:T(8,128)(2,1)S(1)}, u32[]{:S(2)}, u32[]{:S(2)}) collective-permute-start(bf16[96,1728]{1,0:T(8,128)(2,1)S(1)} %get-tuple-element.180), channel_id=1, source_target_pairs={{0,8},{8,0},{16,24},{24,16},{1,9},{9,1},{17,25},{25,17},{2,10},{10... | collective-permute-start | bytes 995336 | tf_op jit(solution)/shard_map/ppermute | solution.py:31
  200.0 13.9 %collective-permute-start.30 = (bf16[4,96,640]{2,1,0:T(8,128)(2,1)}, bf16[4,96,640]{2,1,0:T(8,128)(2,1)}, u32[]{:S(2)}, u32[]{:S(2)}) collective-permute-start(bf16[4,96,640]{2,1,0:T(8,128)(2,1)} %get-tuple-element.129), channel_id=1, source_target_pairs={{0,1},{1,0},{2,3},{3,2},{4,5},{5,4},{6,7},{7,6},{8,9},{9,8},{10,11... | collective-permute-start | bytes 1474568 | tf_op jit(solution)/shard_map/ppermute | solution.py:31
  201.9 13.1 %collective-permute-start.28 = (bf16[264,768]{1,0:T(8,128)(2,1)}, bf16[264,768]{1,0:T(8,128)(2,1)S(1)}, u32[]{:S(2)}, u32[]{:S(2)}) collective-permute-start(bf16[264,768]{1,0:T(8,128)(2,1)} %add_convert_fusion), channel_id=1, source_target_pairs={{0,4},{2,6},{4,0},{6,2},{1,5},{3,7},{5,1},{7,3},{8,12},{10,14},{12... | collective-permute-start | bytes 1216520 | tf_op jit(solution)/shard_map/ppermute | solution.py:31
  223.7 8.6 %collective-permute-start.33 = (bf16[112,640]{1,0:T(8,128)(2,1)S(1)}, bf16[112,640]{1,0:T(8,128)(2,1)S(1)}, u32[]{:S(2)}, u32[]{:S(2)}) collective-permute-start(bf16[112,640]{1,0:T(8,128)(2,1)S(1)} %get-tuple-element.196), channel_id=1, source_target_pairs={{0,24},{8,16},{16,8},{24,0},{1,25},{9,17},{17,9},{25,1},{2,26},{10... | collective-permute-start | bytes 430088 | tf_op jit(solution)/shard_map/ppermute | solution.py:31
  226.4 10.8 %collective-permute-start.32 = (bf16[112,640]{1,0:T(8,128)(2,1)S(1)}, bf16[112,640]{1,0:T(8,128)(2,1)S(1)}, u32[]{:S(2)}, u32[]{:S(2)}) collective-permute-start(bf16[112,640]{1,0:T(8,128)(2,1)S(1)} %get-tuple-element.198), channel_id=1, source_target_pairs={{0,16},{8,24},{16,0},{24,8},{1,17},{9,25},{17,1},{25,9},{2,18},{10... | collective-permute-start | bytes 430088 | tf_op jit(solution)/shard_map/ppermute | solution.py:31
  (48 other events, 557.1 us)

commit v3 on v2

--- a/solution.py
+++ b/solution.py
@@ -12,6 +12,7 @@
 DOCS = 4
 PADW = 256
 QB = 512
+QF = 256
 KB = 256
 
 epsilon = 1e-05
@@ -37,6 +38,11 @@
     return [shard, near, far, swap(far, "heads", 1)]
 
 
+def gather_cores(shard, far):
+    both = jnp.concatenate([shard, far])
+    return [both, swap(both, "heads", 1)]
+
+
 def pairwise(group):
     return group % 32 == 0
 
@@ -45,6 +51,16 @@
     if not pairwise(shard.shape[0]):
         return (shard,)
     return (shard,) + tuple(swap(shard, "batch", by) for by in range(1, lax.axis_size("batch")))
+
+
+def gather_batch_steps(shard):
+    if not pairwise(shard.shape[0]) or lax.axis_size("batch") != 4:
+        shards = gather_batch(shard)
+        return shards, shards[-1]
+    far = swap(shard, "batch", 2)
+    near = swap(jnp.concatenate([shard, far]), "batch", 1)
+    rows = shard.shape[0]
+    return (shard, near[:rows], far, near[rows:]), far
 
 
 def gather_seq(shards):
@@ -78,7 +94,7 @@
         tail = jnp.pad(more, ((0, 0), (0, own.shape[1] - more.shape[1]))).astype(b16)
         payloads = [jnp.concatenate([payload, tail]) for payload in payloads]
     pieces = [swap(payload, "batch", by + 1) for by, payload in enumerate(payloads)]
-    for piece in after(pieces, *others):
+    for piece in after(pieces, *others) if others else pieces:
         own = own + piece[:count].astype(f32)
         if more is not None:
             more = more + piece[count:, : more.shape[1]].astype(f32)
@@ -86,13 +102,13 @@
 
 
 def scatter_far(keep, got, rows):
-    far = (keep[rows:].astype(f32) + got[rows:].astype(f32)).astype(b16)
+    far = (keep[rows : 2 * rows].astype(f32) + got[rows : 2 * rows].astype(f32)).astype(b16)
     here = keep[:rows].astype(f32) + got[:rows].astype(f32)
     return here, swap(far, "heads", 2)
 
 
 def call(body, outs, *args, scratch=(), flops=0, limit=16, plain=False):
-    in_specs = [pl.BlockSpec()] * len(args) if plain else [SMEM] + [VMEM] * (len(args) - 1)
+    in_specs = [pl.BlockSpec(memory_space=pl.ANY)] * len(args) if plain else [SMEM] + [VMEM] * (len(args) - 1)
     return pl.pallas_call(
         body,
         out_shape=[jax.ShapeDtypeStruct(*o) for o in outs],
@@ -100,11 +116,7 @@
         out_specs=[VMEM] * len(outs),
         scratch_shapes=list(scratch),
         compiler_params=pltpu.CompilerParams(vmem_limit_bytes=limit << 20),
-        cost_estimate=pl.CostEstimate(
-            flops=flops,
-            transcendentals=0,
-            bytes_accessed=sum(a.size * a.dtype.itemsize for a in args),
-        ),
+        cost_estimate=pl.CostEstimate(flops=flops // 16, transcendentals=0, bytes_accessed=0),
     )(*args)
 
 
@@ -139,8 +151,11 @@
 
 
 def group_rows(stack, rel, rel_seq, scal):
-    count = stack.shape[1]
-    if stack.shape[0] == 1:
+    return some_rows(stack.shape[1], stack.shape[0] > 1, rel, rel_seq, scal)
+
+
+def some_rows(count, paired, rel, rel_seq, scal):
+    if not paired:
         return slice(rel_seq * count, rel_seq * count + count)
     return pl.ds(pl.multiple_of(((scal[1] ^ rel) * 2 + (scal[2] ^ rel_seq)) * count, 32), count)
 
@@ -149,7 +164,16 @@
     return pl.ds(pl.multiple_of(start, size), size)
 
 
-def shard_body(heads, qkv, out_w, small, kernel, shard, rows):
+def shard_body(heads, *refs):
+    sources, shard, (qkv, out_w, small, kernel), rows, sems = refs[:4], refs[4], refs[5:9], refs[9], refs[10]
+    copies = [
+        pltpu.make_async_copy(source, target, sems.at[index])
+        for index, (source, target) in enumerate(zip(sources, (qkv, out_w, small, kernel)))
+    ]
+    for copy in copies:
+        copy.start()
+    for copy in copies:
+        copy.wait()
     for part in range(3):
         shard[:, part * 128 : part * 128 + 128] = qkv[part, :, 0:128]
     thirds = [qkv[part, :, 128:192].astype(f32) for part in range(3)]
@@ -185,15 +209,29 @@
             taps[4 + tap : 5 + tap, part * PADW + 128 : part * PADW + 256] = jnp.where(low, three, 0.0)
 
 
+def norm_body(half, quarter, scal, *refs):
+    pieces, hats, form = refs[:4], refs[4], refs[5]
+    head = scal[0]
+    for side in range(2):
+        for rel in range(4):
+            base = (head ^ rel) * quarter
+            piece = pieces[2 * side + rel % 2]
+            hat, _ = norm_rows(piece[rel // 2 * quarter : rel // 2 * quarter + quarter, :].astype(f32))
+            if side == 0:
+                hats[ds(half + base, quarter), :] = hat
+                form[ds(base, quarter), :] = hat.astype(b16)
+            else:
+                hats[ds(base, quarter), :] = hat
+
+
 def front_body(half, quarter, heads, paired, scal, *refs):
-    pieces, refs = refs[:4], refs[4:]
-    w_own, w_other, cot = refs[:3]
+    hats, w_own, w_other, cot = refs[:4]
+    refs = refs[1:]
     refs = refs[3:]
     if not paired:
         norms_in, taps_in, refs = refs[0], refs[1], refs[2:]
-    normed, form, projected, wpad, query, key, value, extra, norms, taps = refs[:10]
-    rows_in, proj, columns, features, wo = refs[10:]
-    head = scal[0]
+    normed, projected, wpad, query, key, value, extra, norms, taps = refs[:9]
+    proj, columns, features, wo = refs[9:]
     if paired:
         small_rows(scal, (w_own, w_other), heads, norms, taps, columns, features)
     else:
@@ -217,21 +255,15 @@
     extra[0:quarter, :] = cot[...]
     width = heads * HEAD_DIM
     extra[quarter : quarter + width, :] = wo[...].T[0:width].astype(b16)
-    for index, piece in enumerate(pieces):
-        base = (head ^ index) * quarter
-        rows_in[ds(half + base, quarter), :] = piece[0:quarter, :]
-        rows_in[ds(base, quarter), :] = piece[quarter : 2 * quarter, :]
     proj[0:16, :] = jnp.zeros((16, proj.shape[1]), b16)
 
     def project(block, own):
         base = block * quarter
-        hat, _ = norm_rows(rows_in[ds(base, quarter), :].astype(f32))
-        rounded = (hat * gain + bias).astype(b16)
+        rounded = (hats[ds(base, quarter), :] * gain + bias).astype(b16)
         proj[pl.ds(pl.multiple_of(base + 16, 16), quarter), :] = dot(rounded, wpad[...]).astype(b16)
         if own:
             rows = ds(base - half, quarter)
             normed[rows, :] = rounded
-            form[rows, :] = hat.astype(b16)
 
     @pl.loop(0, 4)
     def _(block):
@@ -290,14 +322,14 @@
     out_t[...] = jnp.zeros_like(out_t)
     peak[...] = jnp.full_like(peak, masked_score)
     total[...] = jnp.zeros_like(total)
-    for block in range(half // QB):
-        first = half + block * QB
-        cols = slice(block * QB, block * QB + QB)
-        pos = first + lanes_like((1, QB))
+    for block in range(half // QF):
+        first = half + block * QF
+        cols = slice(block * QF, block * QF + QF)
+        pos = first + lanes_like((1, QF))
         start = doc_start(pos, bounds)
         low = doc_start(jnp.int32(first), bounds) // KB
 
-        @pl.loop(low, (first + QB) // KB)
+        @pl.loop(low, (first + QF) // KB)
         def _(kb):
             keys = key[ds(kb * KB, KB), :]
             key_pos = kb * KB + lax.broadcasted_iota(jnp.int32, (KB, 1), 0)
@@ -433,8 +465,8 @@
 
     def finish(kb, dk, dv):
         rows = ds(kb * KB - half, KB)
-        dk_out[rows, :] = dk
-        dv_out[rows, :] = dv
+        dk_out[rows, :] = dk.astype(b16)
+        dv_out[rows, :] = dv.astype(b16)
 
     back_blocks(
         half, heads, scal, half // KB, 2 * half // KB,
@@ -474,14 +506,14 @@
 
 
 def feed_body(half, quarter, scal, *refs):
-    attended, extras, inputs = refs[0:4], refs[4:8], refs[8:12]
-    inner, outer, norms = refs[12:15]
-    normed, squared, inner_grad, keep, sent, middle_own = refs[15:]
+    attended, extras, inputs = refs[0:4], refs[4:8], refs[8:10]
+    inner, outer, norms = refs[10:13]
+    normed, squared, inner_grad, keep, sent, middle_own = refs[13:]
     head = scal[0]
     for rel in range(4):
         base = (head ^ rel) * quarter
         late = base >= half // 2
-        middle = inputs[rel][0:quarter, :].astype(f32)
+        middle = inputs[rel % 2][rel // 2 * quarter : rel // 2 * quarter + quarter, :].astype(f32)
         for part in range(4):
             left = attended[part][ds(base, quarter), :]
             right = attended[part][ds(half + lax.rem(base, half // 2), quarter), :].astype(f32)
@@ -507,26 +539,32 @@
             sent[place, :] = part.astype(b16)
 
 
-def feed_grads_body(half, quarter, scal, *refs):
-    extras = refs[0:4]
-    normed, squared, inner_grad, outer = refs[4:8]
-    keep, sent, kept, away = refs[8:12]
-    cot, total = refs[12:]
+def outer_grads_body(quarter, scal, *refs):
+    extras, squared, total, cot = refs[0:4], refs[4], refs[5], refs[6]
+    for rel in range(4):
+        cot[rel * quarter : rel * quarter + quarter, :] = extras[rel][0:quarter, :]
+    for tile in range(total.shape[0] // 256):
+        cols = slice(tile * 256, tile * 256 + 256)
+        total[cols, :] = dot(cot[:, cols], squared[...], 0, 0)
+
+
+def feed_grads_body(quarter, scal, *refs):
+    normed, squared, inner_grad, outer, outer_total = refs[:5]
+    keep, sent, kept, away, total = refs[5:]
     width = total.shape[1]
     for rel in range(4):
         rows = slice(rel * quarter, rel * quarter + quarter)
-        cot[rows, :] = extras[rel][0:quarter, :]
         part = dot(squared[rows, :], outer[...], 1, 1)
         place = slice((rel // 2) * quarter, (rel // 2) * quarter + quarter)
         if rel % 2 == 0:
             keep[place, :] = part
         else:
             sent[place, :] = part.astype(b16)
-    for place, left, right in ((0, normed, inner_grad), (width, cot, squared)):
-        for tile in range(total.shape[0] // 256):
-            cols = slice(tile * 256, tile * 256 + 256)
-            total[cols, :] = dot(left[:, cols], right[...], 0, 0)
-        spread_groups(total, scal, kept, away, slice(place, place + width))
+    for tile in range(total.shape[0] // 256):
+        cols = slice(tile * 256, tile * 256 + 256)
+        total[cols, :] = dot(normed[:, cols], inner_grad[...], 0, 0)
+    spread_groups(total, scal, kept, away, slice(0, width))
+    spread_groups(outer_total, scal, kept, away, slice(width, 2 * width))
 
 
 def norm_back_body(row, scal, part, got, values, skip, norms, grad_in, rounded, sums):
@@ -558,10 +596,10 @@
         rows = slice(block * quarter, block * quarter + quarter)
         shared = remote[rows, 256:384].astype(f32)
         mixed[rows, 0:256] = dq[rows, :]
-        mixed[rows, 256:384] = (dk[rows, 0:128] + remote[rows, 0:128].astype(f32)).astype(b16)
-        mixed[rows, 384:512] = (dk[rows, 128:256] + jnp.where(low, shared, 0.0)).astype(b16)
-        mixed[rows, 512:640] = (dv[rows, 0:128] + remote[rows, 128:256].astype(f32)).astype(b16)
-        mixed[rows, 640:768] = (dv[rows, 128:256] + jnp.where(low, half_roll(shared), 0.0)).astype(b16)
+        mixed[rows, 256:384] = (dk[rows, 0:128].astype(f32) + remote[rows, 0:128].astype(f32)).astype(b16)
+        mixed[rows, 384:512] = (dk[rows, 128:256].astype(f32) + jnp.where(low, shared, 0.0)).astype(b16)
+        mixed[rows, 512:640] = (dv[rows, 0:128].astype(f32) + remote[rows, 128:256].astype(f32)).astype(b16)
+        mixed[rows, 640:768] = (dv[rows, 128:256].astype(f32) + jnp.where(low, half_roll(shared), 0.0)).astype(b16)
     mixed[half : half + 16, :] = jnp.zeros((16, mixed.shape[1]), b16)
 
     @pl.loop(0, half // quarter)
@@ -664,9 +702,6 @@
 
     share = conv_kernel.shape[2]
 
-    x_other = swap(x_own, "seq", 1)
-    x_pieces = gather_heads(jnp.concatenate([x_own, x_other]))
-
     paired = pairwise(group)
     qkv = qkv_weight
     small = [norm1_gain, norm1_bias, norm2_gain, norm2_bias]
@@ -675,7 +710,11 @@
         (shard,) = call(
             functools.partial(shard_body, heads), [((group, 896), b16)],
             qkv.transpose(1, 0, 2), out_weight, jnp.stack(small), conv_kernel,
-            scratch=[pltpu.VMEM((128, 128), f32)], limit=4, plain=True,
+            scratch=[
+                pltpu.VMEM((3, group, width), b16), pltpu.VMEM(out_weight.shape, b16), pltpu.VMEM((4, group), b16),
+                pltpu.VMEM(conv_kernel.shape, b16), pltpu.VMEM((128, 128), f32), pltpu.SemaphoreType.DMA((4,)),
+            ],
+            limit=4, plain=True,
         )
     else:
         small_args = gather_small(jnp.stack(small, axis=1), conv_kernel, model, width)
@@ -683,21 +722,33 @@
             [qkv[:, 0, :128], qkv[:, 1, :128], qkv[:, 2, :128], qkv[:, 0, 128:], qkv[:, 1, 128:], qkv[:, 2, 128:],
              out_weight.T, jnp.zeros((group, 128), b16)], axis=1,
         )
-    shards = gather_batch(shard)
+    shards, first_shard = gather_batch_steps(shard)
+    far_seq = [(2 * h + t, 2 * (h ^ 2) + (t ^ 1)) for h in range(lax.axis_size("heads")) for t in range(2)]
+    x_other, x_far, x_far_other = after(
+        (swap(x_own, "seq", 1), swap(x_own, "heads", 2), lax.ppermute(x_own, ("heads", "seq"), far_seq)), first_shard
+    )
+    x_pieces = gather_cores(x_own, x_far)
+    y_pieces = gather_cores(x_other, x_far_other)
+    hats, form_one = call(
+        functools.partial(norm_body, half, quarter),
+        [((2 * half, model), f32), ((half, model), b16)],
+        scal, *x_pieces, *y_pieces, flops=2 * half * model, limit=6,
+    )
     w_own, w_other = gather_seq(shards)
+    w_other = after(w_other, hats)
 
     feed_shards = gather_batch(after(jnp.concatenate([inner_weight, outer_weight.T], axis=1), shards))
 
-    normed_one, form_one, projected, wpad, query, key, value, extra, norms, taps = call(
+    normed_one, projected, wpad, query, key, value, extra, norms, taps = call(
         functools.partial(front_body, half, quarter, heads, paired),
         [
-            ((half, model), b16), ((half, model), b16), ((half + 16, 3 * PADW), b16), ((model, 3 * PADW), b16),
+            ((half, model), b16), ((half + 16, 3 * PADW), b16), ((model, 3 * PADW), b16),
             ((half, PADW), b16), ((2 * half, PADW), b16), ((2 * half, PADW), b16), ((quarter + width, model), b16),
             ((8, model), f32), ((8, 3 * PADW), f32),
         ],
-        scal, *x_pieces, w_own, w_other, cot_own, *small_args,
+        scal, hats, w_own, w_other, cot_own, *small_args,
         scratch=[
-            pltpu.VMEM((2 * half, model), b16), pltpu.VMEM((2 * half + 16, 3 * PADW), b16),
+            pltpu.VMEM((2 * half + 16, 3 * PADW), b16),
             pltpu.VMEM((model, 128), f32), pltpu.VMEM((KERNEL * HEAD_DIM, 128), f32), pltpu.VMEM((model, PADW), f32),
         ],
         flops=4 * half * model * 3 * width, limit=12,
@@ -730,16 +781,23 @@
         flops=2 * half * model * (model + 3 * hidden), limit=12,
     )
     got = swap(sent, "heads", 1)
+    (outer_total,) = call(
+        functools.partial(outer_grads_body, quarter), [((model, hidden), f32)],
+        scal, *extra_pieces, squared,
+        scratch=[pltpu.VMEM((half, model), b16)], flops=2 * half * model * hidden, limit=8,
+    )
+    got = after(got, outer_total)
+    dn_here, dn_far = scatter_far(keep, got, quarter)
     out_keep, out_sent, ff_keep, ff_send = call(
-        functools.partial(feed_grads_body, half, quarter),
+        functools.partial(feed_grads_body, quarter),
         [((2 * quarter, model), f32), ((2 * quarter, model), b16),
          (stacks + (2 * hidden,), b16), (stacks + (2 * hidden,), b16)],
-        scal, *extra_pieces, normed_two, squared, inner_grad, outer_full,
-        scratch=[pltpu.VMEM((half, model), b16), pltpu.VMEM((model, hidden), f32)],
-        flops=6 * half * model * hidden, limit=10,
-    )
+        scal, after(normed_two, got), squared, inner_grad, outer_full, outer_total,
+        scratch=[pltpu.VMEM((model, hidden), f32)],
+        flops=4 * half * model * hidden, limit=8,
+    )
+    dn_far = after(dn_far, out_sent)
     ff_got = scatter_seq(ff_send)
-    dn_here, dn_far = scatter_far(keep, after(got, ff_send), quarter)
     middle_grad, branch, sums_two = call(
         functools.partial(norm_back_body, 2),
         [((quarter, model), f32), ((quarter, model), b16), ((8, model), f32)],
@@ -755,7 +813,6 @@
         scratch=[pltpu.VMEM((width, model), f32), pltpu.VMEM((model, width), f32)],
         flops=4 * half * model * width, limit=6,
     )
-    pj_got = scatter_seq(pj_send)
     out_here, out_far = scatter_far(out_keep, after(out_got, dout), quarter)
     remote, query_t, kt = call(
         functools.partial(remote_back_body, half, heads),
@@ -768,11 +825,12 @@
         flops=10 * half * half * width, limit=8,
     )
     remote_in = lax.ppermute(remote, "seq", [(1, 0)])
+    ff_own, ff_rest = join_seq((ff_keep, after(ff_got, remote)))
 
     dq, dk, dv, front = call(
         functools.partial(local_back_body, half, heads),
-        [((half, PADW), b16), ((half, PADW), f32), ((half, PADW), f32), ((8, 3 * PADW), f32)],
-        scal, query, key, value, dout, lse, row_dot, kt, query_t, taps,
+        [((half, PADW), b16), ((half, PADW), b16), ((half, PADW), b16), ((8, 3 * PADW), f32)],
+        scal, query, key, value, dout, lse, row_dot, kt, after(query_t, ff_rest), taps,
         scratch=[
             pltpu.VMEM((heads, half, PADW), b16), pltpu.VMEM((heads, half, PADW), b16),
             pltpu.VMEM((KB, PADW), f32), pltpu.VMEM((KB, PADW), f32), pltpu.VMEM((width, half), f32),
@@ -780,8 +838,10 @@
         flops=10 * half * half * width, limit=8,
     )
     front_in = lax.ppermute(front, "seq", [(1, 0)])
-    ff_got, pj_got = after((ff_got, pj_got), dq)
-    ff_own, ff_rest = join_seq((ff_keep, ff_got), (pj_keep, pj_got))
+    pj_got = scatter_seq(after(pj_send, ff_rest))
+    remote_in = after(remote_in, dq)
+    front_in = after(front_in, pj_got)
+    block_output = (middle_own + out_here + after(out_far, dq).astype(f32)).astype(b16)
 
     proj_grad, w_keep, w_send, sums_taps = call(
         functools.partial(tail_body, half, quarter),
@@ -801,23 +861,21 @@
     )
     got = swap(sent, "heads", 1)
     dn_here, dn_far = scatter_far(keep, got, quarter)
-    ff_out, _ = scatter_batch(ff_own, ff_rest, None, sent)
-
-    small = sums + got[2 * quarter :].astype(f32) + dn_far[quarter:].astype(f32)
+    small = sums + got[2 * quarter :].astype(f32)
     small = jnp.concatenate([small[0:4], sums_taps[4:8]])
     small = small + swap(small, "seq", 1)
+    ff_out, _ = scatter_batch(ff_own, ff_rest, None, small)
     cut = small.shape[1] // 2
     small = jnp.concatenate([small[:, :cut], small[:, cut:]])
-    qkv_own, qkv_rest = join_seq((w_keep, w_got))
+    qkv_own, qkv_rest = join_seq((w_keep, w_got), (pj_keep, pj_got))
     qkv_out, small = scatter_batch(qkv_own, qkv_rest, small)
+    pj_out = qkv_out[:, 640:]
     small = jnp.concatenate([small[:8], small[8:]], axis=1)
     input_grad, _, _ = call(
         functools.partial(norm_back_body, 0),
         [((quarter, model), f32), ((quarter, model), b16), ((8, model), f32)],
         scal, dn_here, dn_far, x_own, middle_grad, norms, limit=6,
     )
-    block_output = (middle_own + out_here + out_far.astype(f32)).astype(b16)
-
     qkv_out = jnp.stack(
         [
             jnp.concatenate([qkv_out[:, 0:128], qkv_out[:, 384:448]], axis=1),
@@ -827,6 +885,7 @@
         axis=1,
     )
     gains = lax.dynamic_slice_in_dim(small[0:4], own * group, group, 1)
+    gains = gains + swap(gains, "heads", 2)
     kernel_out = small[4 : 4 + KERNEL].reshape(KERNEL, 3, PADW)[:, :, :width].reshape(KERNEL, 3, heads, HEAD_DIM)
     kernel_out = kernel_out.transpose(1, 2, 3, 0).reshape(3, heads, HEAD_DIM * KERNEL)
     kernel_out = lax.dynamic_slice_in_dim(kernel_out, own * share, share, 2)
@@ -837,7 +896,7 @@
         gains[1],
         qkv_out,
         kernel_out,
-        ff_out[:, 2 * hidden :].T,
+        pj_out.T,
         gains[2],
         gains[3],
         ff_out[:, :hidden],

time: 240 us -> 217 us (0.904)
  waiting for transfers between devices: 103 us -> 74.1 us
  starting transfers between devices: 50.2 us -> 53.5 us
    ppermute x1, waiting for transfers between devices: 15.8 us -> 0.01 us  [on_device(): remote_in = lax.ppermute(remote, 'seq', [(1, 0)])]
    ppermute x37, waiting for transfers between devices: 83.6 us -> 74.1 us  [swap(): lax.ppermute(shard, axis, [(i, i ^ by) for i in range(lax.axis_size(axis))])]
    ppermute x0 -> x1, starting transfers between devices: none -> 3.99 us  [on_device(): lax.ppermute(x_own, ('heads', 'seq'), far_seq)]
    ppermute x1, waiting for transfers between devices: 3.53 us -> 0.01 us  [on_device(): front_in = lax.ppermute(front, 'seq', [(1, 0)])]
    pallas_call x13 -> x15, Pallas kernels: 61.2 us -> 62.6 us  [call(): pl.pallas_call(body, out_shape=[jax.ShapeDtypeStruct(*o) for o in outs],...]
    unnamed x81 -> x68, local copies, waits for them, and re-layouts: 9.47 us -> 10.4 us
  transfers between devices with their start and end apart: 39 -> 40, of which waited for: 17 -> 16; matrix products, arithmetic and copies ran while one was open for 5% -> 7% of each run, Pallas kernels for 21% -> 24%
where the time goes in v3:
time: 217 us; the launch traced here: 216 us
  waiting for transfers between devices  74.1 us (34%)
  Pallas kernels  62.6 us (29%)
  starting transfers between devices  53.5 us (25%)
  local copies, waits for them, and re-layouts  13.9 us (6%)
  other arithmetic  10.3 us (5%)
    ppermute x37, waiting for transfers between devices, swap(): lax.ppermute(shard, axis, [(i, i ^ by) for i in range(lax.axis_size(axis))])  74.1 us
    pallas_call x15, Pallas kernels, call(): pl.pallas_call(body, out_shape=[jax.ShapeDtypeStruct(*o) for o in outs],...  62.6 us
    ppermute x37, starting transfers between devices, swap(): lax.ppermute(shard, axis, [(i, i ^ by) for i in range(lax.axis_size(axis))])  46.6 us
    unnamed x68, local copies, waits for them, and re-layouts  10.4 us
  transfers between devices with their start and end apart: 40, of which 16 were waited for; matrix products, arithmetic and copies ran while one was open for 7% of the time, Pallas kernels for 24%

profile of v3, /device:TPU:0, one launch (start us, length us, event | category | flops | bytes accessed | tf_op | source)
XLA Modules:
  0.0 215.8 jit_solution(3392987626272759705)
XLA Ops:
  0.7 4.0 %collective-permute-start.2 = (bf16[256,768]{1,0:T(8,128)(2,1)}, bf16[256,768]{1,0:T(8,128)(2,1)S(1)}, u32[]{:S(2)}, u32[]{:S(2)}) collective-permute-start(bf16[256,768]{1,0:T(8,128)(2,1)} %bitcast.79), channel_id=1, source_target_pairs={{0,5},{1,4},{2,7},{3,6},{4,1},{5,0},{6,3},{7,2},{8,13},{9,12},{10,... | collective-permute-start | bytes 1179656 | tf_op jit(solution)/shard_map/ppermute | solution.py:728
  8.9 3.1 %collective-permute-start.3 = (bf16[96,896]{1,0:T(8,128)(2,1)S(1)}, bf16[96,896]{1,0:T(8,128)(2,1)S(1)}, u32[]{:S(2)}, u32[]{:S(2)}) collective-permute-start(bf16[96,896]{1,0:T(8,128)(2,1)S(1)} %shard_map.203), channel_id=1, source_target_pairs={{0,16},{8,24},{16,0},{24,8},{1,17},{9,25},{17,1},{25,9},{2,18},{10... | collective-permute-start | bytes 516104 | tf_op jit(solution)/shard_map/ppermute | solution.py:32
  11.9 7.2 %collective-permute-done.3 = bf16[96,896]{1,0:T(8,128)(2,1)S(1)} collective-permute-done((bf16[96,896]{1,0:T(8,128)(2,1)S(1)}, bf16[96,896]{1,0:T(8,128)(2,1)S(1)}, u32[]{:S(2)}, u32[]{:S(2)}) %collective-permute-start.3) | collective-permute-done | bytes 172064 | tf_op jit(solution)/shard_map/ppermute | solution.py:32
  20.0 2.7 %collective-permute-done.1 = bf16[256,768]{1,0:T(8,128)(2,1)S(1)} collective-permute-done((bf16[256,768]{1,0:T(8,128)(2,1)}, bf16[256,768]{1,0:T(8,128)(2,1)S(1)}, u32[]{:S(2)}, u32[]{:S(2)}) %collective-permute-start.1) | collective-permute-done | bytes 393248 | tf_op jit(solution)/shard_map/ppermute | solution.py:32
  24.9 3.3 %collective-permute-done.6 = bf16[192,896]{1,0:T(8,128)(2,1)S(1)} collective-permute-done((bf16[192,896]{1,0:T(8,128)(2,1)S(1)}, bf16[192,896]{1,0:T(8,128)(2,1)S(1)}, u32[]{:S(2)}, u32[]{:S(2)}) %collective-permute-start.6) | collective-permute-done | bytes 344096 | tf_op jit(solution)/shard_map/ppermute | solution.py:32
  30.8 4.5 %collective-permute-start.16 = (bf16[96,1536]{1,0:T(8,128)(2,1)}, bf16[96,1536]{1,0:T(8,128)(2,1)}, u32[]{:S(2)}, u32[]{:S(2)}) collective-permute-start(bf16[96,1536]{1,0:T(8,128)(2,1)} %pad_maximum_fusion.5), channel_id=1, source_target_pairs={{0,24},{8,16},{16,8},{24,0},{1,25},{9,17},{17,9},{25,1},{2,26},{10... | collective-permute-start | bytes 884744 | tf_op jit(solution)/shard_map/ppermute | solution.py:32
  36.0 3.6 %shard_map.204 = (f32[2048,768]{1,0:T(8,128)S(1)}, bf16[1024,768]{1,0:T(8,128)(2,1)S(1)}) custom-call(s32[8]{0:T(128)S(1)} %concatenate.45.scal, bf16[512,768]{1,0:T(8,128)(2,1)S(1)} %pad_maximum_fusion.2.refs_0_.refs_8_, bf16[512,768]{1,0:T(8,128)(2,1)S(1)} %collective-permute-done.4.refs_1_.refs_9_, ...), custom_call_target="tpu_custom_call" | custom-call | flops 98304 | tf_op jit(solution)/shard_map/pallas_call | solution.py:112
  40.8 3.4 %collective-permute-done.7.refs_2_ = bf16[4,96,896]{2,1,0:T(8,128)(2,1)} collective-permute-done((bf16[4,96,896]{2,1,0:T(8,128)(2,1)S(1)}, bf16[4,96,896]{2,1,0:T(8,128)(2,1)}, u32[]{:S(2)}, u32[]{:S(2)}) %collective-permute-start.7) | collective-permute-done | bytes 688160 | tf_op jit(solution)/shard_map/ppermute | solution.py:32
  45.3 8.7 %shard_map.205 = (bf16[1024,768]{1,0:T(8,128)(2,1)S(1)}, bf16[1040,768]{1,0:T(8,128)(2,1)S(1)}, bf16[768,768]{1,0:T(8,128)(2,1)S(1)}, bf16[1024,256]{1,0:T(8,128...) custom-call(s32[8]{0:T(128)S(1)} %concatenate.45.scal, ...), custom_call_target="tpu_custom_call" | custom-call | flops 113246208 | tf_op jit(solution)/shard_map/pallas_call | solution.py:112
  55.2 4.4 %collective-permute-done.15 = bf16[96,1536]{1,0:T(8,128)(2,1)} collective-permute-done((bf16[96,1536]{1,0:T(8,128)(2,1)}, bf16[96,1536]{1,0:T(8,128)(2,1)}, u32[]{:S(2)}, u32[]{:S(2)}) %collective-permute-start.15) | collective-permute-done | bytes 294944 | tf_op jit(solution)/shard_map/ppermute | solution.py:32
  63.1 8.0 %shard_map.206 = (bf16[1536,128]{1,0:T(8,128)(2,1)S(1)}, f32[192,1024]{1,0:T(8,128)S(1)}, f32[8,1024]{1,0:T(8,128)S(1)}) custom-call(s32[8]{0:T(128)S(1)} %concatenate.45.scal, bf16[1024,256]{1,0:T(8,128)(2,1)S(1)} %get-tuple-element.89.query.refs_0_, bf16[2048,256]{1,0:T(8,128)(2,1)S(1)} %get-tuple-element.90.key.refs_1_, ...), custom_call_target="tpu_custom_call" | custom-call | flops 50331648 | tf_op jit(solution)/shard_map/pallas_call | solution.py:112
  71.7 6.2 %collective-permute-done.12.refs_6_.refs_2_ = bf16[448,768]{1,0:T(8,128)(2,1)S(1)} collective-permute-done((bf16[448,768]{1,0:T(8,128)(2,1)S(1)}, bf16[448,768]{1,0:T(8,128)(2,1)S(1)}, u32[]{:S(2)}, u32[]{:S(2)}) %collective-permute-start.12) | collective-permute-done | bytes 688160 | tf_op jit(solution)/shard_map/ppermute | solution.py:32
  78.4 6.1 %collective-permute-done.9.refs_2_ = bf16[1536,128]{1,0:T(8,128)(2,1)S(1)} collective-permute-done((bf16[1536,128]{1,0:T(8,128)(2,1)S(1)}, bf16[1536,128]{1,0:T(8,128)(2,1)S(1)}, u32[]{:S(2)}, u32[]{:S(2)}) %collective-permute-start.9) | collective-permute-done | bytes 393248 | tf_op jit(solution)/shard_map/ppermute | solution.py:32
  84.5 4.8 %collective-permute-done.17.refs_1_ = bf16[4,96,1536]{2,1,0:T(8,128)(2,1)S(1)} collective-permute-done((bf16[4,96,1536]{2,1,0:T(8,128)(2,1)S(1)}, bf16[4,96,1536]{2,1,0:T(8,128)(2,1)S(1)}, u32[]{:S(2)}, u32[]{:S(2)}) %collective-permute-start.17) | collective-permute-done | bytes 1179680 | tf_op jit(solution)/shard_map/ppermute | solution.py:32
  90.0 8.6 %shard_map.208 = (bf16[1024,768]{1,0:T(8,128)(2,1)S(1)}, bf16[1024,768]{1,0:T(8,128)(2,1)S(1)}, bf16[1024,768]{1,0:T(8,128)(2,1)S(1)}, f32[512,768]{1,0:T(8,128)...) custom-call(s32[8]{0:T(128)S(1)} %concatenate.45.scal, bf16[1536,128]{1,0:T(8,128)(2,1)S(1)} %get-tuple-element.92.refs_0_, ...), custom_call_target="tpu_custom_call" | custom-call | flops 301989888 | tf_op jit(solution)/shard_map/pallas_call | solution.py:112
  98.7 2.0 shard_map.209.refs_4_
  101.8 4.6 %shard_map.210 = (f32[512,768]{1,0:T(8,128)S(1)}, bf16[512,768]{1,0:T(8,128)(2,1)}, bf16[4,96,1536]{2,1,0:T(8,128)(2,1)S(1)}, bf16[4,96,1536]{2,1,0:T(8,128)(2,1)}) custom-call(s32[8]{0:T(128)S(1)} %concatenate.45.scal, bf16[1024,768]{1,0:T(8,128)(2,1)S(1)} %get-tuple-element.109.refs_0_, bf16[1024,768]{1,0:T(8,128)(2,1)S(1)} %get-tuple-element.107.refs_4_.refs_1_, ...), custom_call_target="tpu_custom_call" | custom-call | flops 150994944 | tf_op jit(solution)/shard_map/pallas_call | solution.py:112
  107.8 4.6 %collective-permute-done.19.got = bf16[256,768]{1,0:T(8,128)(2,1)S(1)} collective-permute-done((bf16[256,768]{1,0:T(8,128)(2,1)S(1)}, bf16[256,768]{1,0:T(8,128)(2,1)S(1)}, u32[]{:S(2)}, u32[]{:S(2)}) %collective-permute-start.19) | collective-permute-done | bytes 393248 | tf_op jit(solution)/shard_map/ppermute | solution.py:32
  116.3 9.8 %collective-permute-done.22.refs_2_ = bf16[256,768]{1,0:T(8,128)(2,1)} collective-permute-done((bf16[256,768]{1,0:T(8,128)(2,1)}, bf16[256,768]{1,0:T(8,128)(2,1)}, u32[]{:S(2)}, u32[]{:S(2)}) %collective-permute-start.22) | collective-permute-done | bytes 393248 | tf_op jit(solution)/shard_map/ppermute | solution.py:32
  126.1 2.1 collective-permute-done.23.refs_3_
  129.3 2.8 %shard_map.212 = (bf16[1024,256]{1,0:T(8,128)(2,1)S(1)}, f32[8,1024]{1,0:T(8,128)S(1)}, f32[4,96,192]{2,1,0:T(8,128)S(1)}, bf16[4,96,192]{2,1,0:T(8,128)(2,1)S(1)}) custom-call(s32[8]{0:T(128)S(1)} %concatenate.45.scal, bf16[256,768]{1,0:T(8,128)(2,1)} %get-tuple-element.115.refs_0_, bf16[256,768]{1,0:T(8,128)(2,1)} %collective-permute-done.21.refs_1_, ...), custom_call_target="tpu_custom_call" | custom-call | flops 37748736 | tf_op jit(solution)/shard_map/pallas_call | solution.py:112
  133.7 2.2 %shard_map.213 = (bf16[1024,384]{1,0:T(8,128)(2,1)S(1)}, f32[192,1024]{1,0:T(8,128)S(1)}, bf16[192,2048]{1,0:T(8,128)(2,1)S(1)}) custom-call(s32[8]{0:T(128)S(1)} %concatenate.45.scal, bf16[1024,256]{1,0:T(8,128)(2,1)S(1)} %get-tuple-element.89.query.refs_0_, bf16[2048,256]{1,0:T(8,128)(2,1)S(1)} %get-tuple-element.90.key.refs_1_, ...), custom_call_target="tpu_custom_call" | custom-call | flops 125829120 | tf_op jit(solution)/shard_map/pallas_call | solution.py:112
  139.0 9.3 %shard_map.214 = (bf16[1024,256]{1,0:T(8,128)(2,1)S(1)}, bf16[1024,256]{1,0:T(8,128)(2,1)S(1)}, bf16[1024,256]{1,0:T(8,128)(2,1)S(1)}, f32[8,768]{1,0:T(8,128)S(1)}) custom-call(s32[8]{0:T(128)S(1)} %concatenate.45.scal, bf16[1024,256]{1,0:T(8,128)(2,1)S(1)} %get-tuple-element.89.query.refs_0_, bf16[2048,256]{1,0:T(8,128)(2,1)S(1)} %get-tuple-element.90.key.refs_1_, ...), custom_call_target="tpu_custom_call" | custom-call | flops 125829120 | tf_op jit(solution)/shard_map/pallas_call | solution.py:112
  150.0 3.3 %collective-permute-start.28 = (bf16[4,96,192]{2,1,0:T(8,128)(2,1)S(1)}, bf16[4,96,192]{2,1,0:T(8,128)(2,1)S(1)}, u32[]{:S(2)}, u32[]{:S(2)}) collective-permute-start(bf16[4,96,192]{2,1,0:T(8,128)(2,1)S(1)} %get-tuple-element.137), channel_id=1, source_target_pairs={{0,1},{1,0},{2,3},{3,2},{4,5},{5,4},{6,7},{7,6},{8,9},{9,8},{10,11... | collective-permute-start | bytes 442376 | tf_op jit(solution)/shard_map/ppermute | solution.py:32
  153.3 10.1 %collective-permute-start.39 = (bf16[96,1536]{1,0:T(8,128)(2,1)S(1)}, bf16[96,1536]{1,0:T(8,128)(2,1)S(1)}, u32[]{:S(2)}, u32[]{:S(2)}) collective-permute-start(bf16[96,1536]{1,0:T(8,128)(2,1)S(1)} %get-tuple-element.196), channel_id=1, source_target_pairs={{0,24},{8,16},{16,8},{24,0},{1,25},{9,17},{17,9},{25,1},{2,26},{10... | collective-permute-start | bytes 884744 | tf_op jit(solution)/shard_map/ppermute | solution.py:32
  163.5 5.3 %collective-permute-start.38 = (bf16[96,1536]{1,0:T(8,128)(2,1)S(1)}, bf16[96,1536]{1,0:T(8,128)(2,1)S(1)}, u32[]{:S(2)}, u32[]{:S(2)}) collective-permute-start(bf16[96,1536]{1,0:T(8,128)(2,1)S(1)} %get-tuple-element.197), channel_id=1, source_target_pairs={{0,16},{8,24},{16,0},{24,8},{1,17},{9,25},{17,1},{25,9},{2,18},{10... | collective-permute-start | bytes 884744 | tf_op jit(solution)/shard_map/ppermute | solution.py:32
  170.0 5.4 %shard_map.215 = (bf16[1024,768]{1,0:T(8,128)(2,1)S(1)}, f32[4,96,640]{2,1,0:T(8,128)S(1)}, bf16[4,96,640]{2,1,0:T(8,128)(2,1)S(1)}, f32[8,768]{1,0:T(8,128)S(1)}) custom-call(s32[8]{0:T(128)S(1)} %concatenate.45.scal, bf16[1024,256]{1,0:T(8,128)(2,1)S(1)} %get-tuple-element.130.refs_0_, bf16[1024,256]{1,0:T(8,128)(2,1)S(1)} %get-tuple-element.132.refs_1_, ...), custom_call_target="tpu_custom_call" | custom-call | flops 56623104 | tf_op jit(solution)/shard_map/pallas_call | solution.py:112
  175.6 2.1 shard_map.216
  179.7 6.8 %collective-permute-done.32 = bf16[4,96,640]{2,1,0:T(8,128)(2,1)S(1)} collective-permute-done((bf16[4,96,640]{2,1,0:T(8,128)(2,1)S(1)}, bf16[4,96,640]{2,1,0:T(8,128)(2,1)S(1)}, u32[]{:S(2)}, u32[]{:S(2)}) %collective-permute-start.32) | collective-permute-done | bytes 491552 | tf_op jit(solution)/shard_map/ppermute | solution.py:32
  191.8 4.5 %collective-permute-start.34 = (bf16[112,832]{1,0:T(8,128)(2,1)S(1)}, bf16[112,832]{1,0:T(8,128)(2,1)S(1)}, u32[]{:S(2)}, u32[]{:S(2)}) collective-permute-start(bf16[112,832]{1,0:T(8,128)(2,1)S(1)} %get-tuple-element.217), channel_id=1, source_target_pairs={{0,16},{8,24},{16,0},{24,8},{1,17},{9,25},{17,1},{25,9},{2,18},{10... | collective-permute-start | bytes 559112 | tf_op jit(solution)/shard_map/ppermute | solution.py:32
  198.1 10.8 %collective-permute-done.34 = bf16[112,832]{1,0:T(8,128)(2,1)S(1)} collective-permute-done((bf16[112,832]{1,0:T(8,128)(2,1)S(1)}, bf16[112,832]{1,0:T(8,128)(2,1)S(1)}, u32[]{:S(2)}, u32[]{:S(2)}) %collective-permute-start.34) | collective-permute-done | bytes 186400 | tf_op jit(solution)/shard_map/ppermute | solution.py:32
  213.6 2.2 %shard_map.217 = (f32[256,768]{1,0:T(8,128)}, bf16[256,768]{1,0:T(8,128)(2,1)}, f32[8,768]{1,0:T(8,128)}) custom-call(s32[8]{0:T(128)S(1)} %concatenate.45.scal, f32[256,768]{1,0:T(8,128)S(1)} %get-tuple-element.191.part, bf16[256,768]{1,0:T(8,128)(2,1)S(1)} %collective-permute-done.30.got, bf16[256,768]{1,0:T(8,128)(2,1)S(1)} %bitcast.83, ...), custom_call_target="tpu_custom_call" | custom-call | tf_op jit(solution)/shard_map/pallas_call | solution.py:112
  (180 shorter events, 48.1 us)
Async XLA Ops:
  0.7 19.3 %collective-permute-start.2 = (bf16[256,768]{1,0:T(8,128)(2,1)}, bf16[256,768]{1,0:T(8,128)(2,1)S(1)}, u32[]{:S(2)}, u32[]{:S(2)}) collective-permute-start(bf16[256,768]{1,0:T(8,128)(2,1)} %bitcast.79), channel_id=1, source_target_pairs={{0,5},{1,4},{2,7},{3,6},{4,1},{5,0},{6,3},{7,2},{8,13},{9,12},{10,... | collective-permute-start | bytes 1179656 | tf_op jit(solution)/shard_map/ppermute | solution.py:728
  4.6 18.0 %collective-permute-start.1 = (bf16[256,768]{1,0:T(8,128)(2,1)}, bf16[256,768]{1,0:T(8,128)(2,1)S(1)}, u32[]{:S(2)}, u32[]{:S(2)}) collective-permute-start(bf16[256,768]{1,0:T(8,128)(2,1)} %bitcast.80), channel_id=1, source_target_pairs={{0,4},{2,6},{4,0},{6,2},{1,5},{3,7},{5,1},{7,3},{8,12},{10,14},{12... | collective-permute-start | bytes 1179656 | tf_op jit(solution)/shard_map/ppermute | solution.py:32
  5.2 17.5 %collective-permute-start = (bf16[256,768]{1,0:T(8,128)(2,1)}, bf16[256,768]{1,0:T(8,128)(2,1)S(1)}, u32[]{:S(2)}, u32[]{:S(2)}) collective-permute-start(bf16[256,768]{1,0:T(8,128)(2,1)} %bitcast.81), channel_id=1, source_target_pairs={{0,1},{1,0},{2,3},{3,2},{4,5},{5,4},{6,7},{7,6},{8,9},{9,8},{10,11... | collective-permute-start | bytes 1179656 | tf_op jit(solution)/shard_map/ppermute | solution.py:32
  8.9 10.3 %collective-permute-start.3 = (bf16[96,896]{1,0:T(8,128)(2,1)S(1)}, bf16[96,896]{1,0:T(8,128)(2,1)S(1)}, u32[]{:S(2)}, u32[]{:S(2)}) collective-permute-start(bf16[96,896]{1,0:T(8,128)(2,1)S(1)} %shard_map.203), channel_id=1, source_target_pairs={{0,16},{8,24},{16,0},{24,8},{1,17},{9,25},{17,1},{25,9},{2,18},{10... | collective-permute-start | bytes 516104 | tf_op jit(solution)/shard_map/ppermute | solution.py:32
  24.2 11.0 %collective-permute-start.5 = (bf16[512,768]{1,0:T(8,128)(2,1)}, bf16[512,768]{1,0:T(8,128)(2,1)}, u32[]{:S(2)}, u32[]{:S(2)}) collective-permute-start(bf16[512,768]{1,0:T(8,128)(2,1)} %constant_dynamic-update-slice_fusion.refs_2_), channel_id=1, source_target_pairs={{0,2},{2,0},{4,6},{6,4},{1,3},{3,1},{5,7},{7,5},{8,10},{10,8},{12,... | collective-permute-start | bytes 2359304 | tf_op jit(solution)/shard_map/ppermute | solution.py:32
  24.3 11.7 %collective-permute-start.4 = (bf16[512,768]{1,0:T(8,128)(2,1)S(1)}, bf16[512,768]{1,0:T(8,128)(2,1)S(1)}, u32[]{:S(2)}, u32[]{:S(2)}) collective-permute-start(bf16[512,768]{1,0:T(8,128)(2,1)S(1)} %pad_maximum_fusion.2.refs_0_.refs_8_), channel_id=1, source_target_pairs={{0,2},{2,0},{4,6},{6,4},{1,3},{3,1},{5,7},{7,5},{8,10},{10,8},{12,... | collective-permute-start | bytes 2359304 | tf_op jit(solution)/shard_map/ppermute | solution.py:32
  28.3 15.9 %collective-permute-start.7 = (bf16[4,96,896]{2,1,0:T(8,128)(2,1)S(1)}, bf16[4,96,896]{2,1,0:T(8,128)(2,1)}, u32[]{:S(2)}, u32[]{:S(2)}) collective-permute-start(bf16[4,96,896]{2,1,0:T(8,128)(2,1)S(1)} %pad_maximum_fusion.3.refs_1_), channel_id=1, source_target_pairs={{0,1},{1,0},{2,3},{3,2},{4,5},{5,4},{6,7},{7,6},{8,9},{9,8},{10,11... | collective-permute-start | bytes 2064392 | tf_op jit(solution)/shard_map/ppermute | solution.py:32
  30.8 24.5 %collective-permute-start.16 = (bf16[96,1536]{1,0:T(8,128)(2,1)}, bf16[96,1536]{1,0:T(8,128)(2,1)}, u32[]{:S(2)}, u32[]{:S(2)}) collective-permute-start(bf16[96,1536]{1,0:T(8,128)(2,1)} %pad_maximum_fusion.5), channel_id=1, source_target_pairs={{0,24},{8,16},{16,8},{24,0},{1,25},{9,17},{17,9},{25,1},{2,26},{10... | collective-permute-start | bytes 884744 | tf_op jit(solution)/shard_map/ppermute | solution.py:32
  35.2 24.4 %collective-permute-start.15 = (bf16[96,1536]{1,0:T(8,128)(2,1)}, bf16[96,1536]{1,0:T(8,128)(2,1)}, u32[]{:S(2)}, u32[]{:S(2)}) collective-permute-start(bf16[96,1536]{1,0:T(8,128)(2,1)} %pad_maximum_fusion.5), channel_id=1, source_target_pairs={{0,16},{8,24},{16,0},{24,8},{1,17},{9,25},{17,1},{25,9},{2,18},{10... | collective-permute-start | bytes 884744 | tf_op jit(solution)/shard_map/ppermute | solution.py:32
  35.2 24.4 %collective-permute-start.14 = (bf16[96,1536]{1,0:T(8,128)(2,1)}, bf16[96,1536]{1,0:T(8,128)(2,1)}, u32[]{:S(2)}, u32[]{:S(2)}) collective-permute-start(bf16[96,1536]{1,0:T(8,128)(2,1)} %pad_maximum_fusion.5), channel_id=1, source_target_pairs={{0,8},{8,0},{16,24},{24,16},{1,9},{9,1},{17,25},{25,17},{2,10},{10... | collective-permute-start | bytes 884744 | tf_op jit(solution)/shard_map/ppermute | solution.py:32
  59.6 18.3 %collective-permute-start.12 = (bf16[448,768]{1,0:T(8,128)(2,1)S(1)}, bf16[448,768]{1,0:T(8,128)(2,1)S(1)}, u32[]{:S(2)}, u32[]{:S(2)}) collective-permute-start(bf16[448,768]{1,0:T(8,128)(2,1)S(1)} %get-tuple-element.93.refs_4_.refs_0_), channel_id=1, source_target_pairs={{0,4},{2,6},{4,0},{6,2},{1,5},{3,7},{5,1},{7,3},{8,12},{10,14},{12... | collective-permute-start | bytes 2064392 | tf_op jit(solution)/shard_map/ppermute | solution.py:32
  62.5 26.8 %collective-permute-start.17 = (bf16[4,96,1536]{2,1,0:T(8,128)(2,1)S(1)}, bf16[4,96,1536]{2,1,0:T(8,128)(2,1)S(1)}, u32[]{:S(2)}, u32[]{:S(2)}) collective-permute-start(bf16[4,96,1536]{2,1,0:T(8,128)(2,1)S(1)} %pad_maximum_fusion.1.refs_0_), channel_id=1, source_target_pairs={{0,1},{1,0},{2,3},{3,2},{4,5},{5,4},{6,7},{7,6},{8,9},{9,8},{10,11... | collective-permute-start | bytes 3538952 | tf_op jit(solution)/shard_map/ppermute | solution.py:32
  71.1 13.4 %collective-permute-start.9 = (bf16[1536,128]{1,0:T(8,128)(2,1)S(1)}, bf16[1536,128]{1,0:T(8,128)(2,1)S(1)}, u32[]{:S(2)}, u32[]{:S(2)}) collective-permute-start(bf16[1536,128]{1,0:T(8,128)(2,1)S(1)} %get-tuple-element.92.refs_0_), channel_id=1, source_target_pairs={{0,4},{2,6},{4,0},{6,2},{1,5},{3,7},{5,1},{7,3},{8,12},{10,14},{12... | collective-permute-start | bytes 1179656 | tf_op jit(solution)/shard_map/ppermute | solution.py:32
  71.7 18.3 %collective-permute-start.11 = (bf16[448,768]{1,0:T(8,128)(2,1)S(1)}, bf16[448,768]{1,0:T(8,128)(2,1)S(1)}, u32[]{:S(2)}, u32[]{:S(2)}) collective-permute-start(bf16[448,768]{1,0:T(8,128)(2,1)S(1)} %get-tuple-element.93.refs_4_.refs_0_), channel_id=1, source_target_pairs={{0,2},{2,0},{4,6},{6,4},{1,3},{3,1},{5,7},{7,5},{8,10},{10,8},{12,... | collective-permute-start | bytes 2064392 | tf_op jit(solution)/shard_map/ppermute | solution.py:32
  77.9 12.1 %collective-permute-start.13 = (bf16[448,768]{1,0:T(8,128)(2,1)S(1)}, bf16[448,768]{1,0:T(8,128)(2,1)S(1)}, u32[]{:S(2)}, u32[]{:S(2)}) collective-permute-start(bf16[448,768]{1,0:T(8,128)(2,1)S(1)} %collective-permute-done.12.refs_6_.refs_2_), channel_id=1, source_target_pairs={{0,2},{2,0},{4,6},{6,4},{1,3},{3,1},{5,7},{7,5},{8,10},{10,8},{12,... | collective-permute-start | bytes 2064392 | tf_op jit(solution)/shard_map/ppermute | solution.py:32
  77.9 12.0 %collective-permute-start.8 = (bf16[1536,128]{1,0:T(8,128)(2,1)S(1)}, bf16[1536,128]{1,0:T(8,128)(2,1)S(1)}, u32[]{:S(2)}, u32[]{:S(2)}) collective-permute-start(bf16[1536,128]{1,0:T(8,128)(2,1)S(1)} %get-tuple-element.92.refs_0_), channel_id=1, source_target_pairs={{0,2},{2,0},{4,6},{6,4},{1,3},{3,1},{5,7},{7,5},{8,10},{10,8},{12,... | collective-permute-start | bytes 1179656 | tf_op jit(solution)/shard_map/ppermute | solution.py:32
  101.2 11.3 %collective-permute-start.19 = (bf16[256,768]{1,0:T(8,128)(2,1)S(1)}, bf16[256,768]{1,0:T(8,128)(2,1)S(1)}, u32[]{:S(2)}, u32[]{:S(2)}) collective-permute-start(bf16[256,768]{1,0:T(8,128)(2,1)S(1)} %get-tuple-element.194), channel_id=1, source_target_pairs={{0,4},{2,6},{4,0},{6,2},{1,5},{3,7},{5,1},{7,3},{8,12},{10,14},{12... | collective-permute-start | bytes 1179656 | tf_op jit(solution)/shard_map/ppermute | solution.py:32
  107.3 29.9 %collective-permute-start.25 = (bf16[4,96,1536]{2,1,0:T(8,128)(2,1)}, bf16[4,96,1536]{2,1,0:T(8,128)(2,1)}, u32[]{:S(2)}, u32[]{:S(2)}) collective-permute-start(bf16[4,96,1536]{2,1,0:T(8,128)(2,1)} %get-tuple-element.125), channel_id=1, source_target_pairs={{0,1},{1,0},{2,3},{3,2},{4,5},{5,4},{6,7},{7,6},{8,9},{9,8},{10,11... | collective-permute-start | bytes 3538952 | tf_op jit(solution)/shard_map/ppermute | solution.py:32
  115.3 10.8 %collective-permute-start.22 = (bf16[256,768]{1,0:T(8,128)(2,1)}, bf16[256,768]{1,0:T(8,128)(2,1)}, u32[]{:S(2)}, u32[]{:S(2)}) collective-permute-start(bf16[256,768]{1,0:T(8,128)(2,1)} %get-tuple-element.115.refs_0_), channel_id=1, source_target_pairs={{0,4},{2,6},{4,0},{6,2},{1,5},{3,7},{5,1},{7,3},{8,12},{10,14},{12... | collective-permute-start | bytes 1179656 | tf_op jit(solution)/shard_map/ppermute | solution.py:32
  115.8 16.3 %collective-permute-start.20 = (bf16[512,768]{1,0:T(8,128)(2,1)}, bf16[512,768]{1,0:T(8,128)(2,1)}, u32[]{:S(2)}, u32[]{:S(2)}) collective-permute-start(bf16[512,768]{1,0:T(8,128)(2,1)} %get-tuple-element.116), channel_id=1, source_target_pairs={{0,2},{2,0},{4,6},{6,4},{1,3},{3,1},{5,7},{7,5},{8,10},{10,8},{12,... | collective-permute-start | bytes 2359304 | tf_op jit(solution)/shard_map/ppermute | solution.py:32
  115.8 10.3 %collective-permute-start.21 = (bf16[256,768]{1,0:T(8,128)(2,1)}, bf16[256,768]{1,0:T(8,128)(2,1)}, u32[]{:S(2)}, u32[]{:S(2)}) collective-permute-start(bf16[256,768]{1,0:T(8,128)(2,1)} %get-tuple-element.115.refs_0_), channel_id=1, source_target_pairs={{0,2},{2,0},{4,6},{6,4},{1,3},{3,1},{5,7},{7,5},{8,10},{10,8},{12,... | collective-permute-start | bytes 1179656 | tf_op jit(solution)/shard_map/ppermute | solution.py:32
  133.2 42.3 %collective-permute-start.24 = (bf16[256,768]{1,0:T(8,128)(2,1)S(1)}, bf16[256,768]{1,0:T(8,128)(2,1)S(1)}, u32[]{:S(2)}, u32[]{:S(2)}) collective-permute-start(bf16[256,768]{1,0:T(8,128)(2,1)S(1)} %add_convert_fusion.2), channel_id=1, source_target_pairs={{0,4},{2,6},{4,0},{6,2},{1,5},{3,7},{5,1},{7,3},{8,12},{10,14},{12... | collective-permute-start | bytes 1179656 | tf_op jit(solution)/shard_map/ppermute | solution.py:32
  136.0 34.0 %collective-permute-start.26 = (bf16[1024,384]{1,0:T(8,128)(2,1)S(1)}, bf16[1024,384]{1,0:T(8,128)(2,1)S(1)}, u32[]{:S(2)}, u32[]{:S(2)}) collective-permute-start(bf16[1024,384]{1,0:T(8,128)(2,1)S(1)} %get-tuple-element.126), channel_id=1, source_target_pairs={{1,0},{3,2},{5,4},{7,6},{9,8},{11,10},{13,12},{15,14},{17,16},{19,... | collective-permute-start | bytes 2359304 | tf_op jit(solution)/shard_map/ppermute | solution.py:827
  148.3 15.2 %collective-permute-start.27 = (f32[8,768]{1,0:T(8,128)S(1)}, f32[8,768]{1,0:T(8,128)S(1)}, u32[]{:S(2)}, u32[]{:S(2)}) collective-permute-start(f32[8,768]{1,0:T(8,128)S(1)} %get-tuple-element.135), channel_id=1, source_target_pairs={{1,0},{3,2},{5,4},{7,6},{9,8},{11,10},{13,12},{15,14},{17,16},{19,... | collective-permute-start | bytes 73736 | tf_op jit(solution)/shard_map/ppermute | solution.py:840
  150.0 18.8 %collective-permute-start.28 = (bf16[4,96,192]{2,1,0:T(8,128)(2,1)S(1)}, bf16[4,96,192]{2,1,0:T(8,128)(2,1)S(1)}, u32[]{:S(2)}, u32[]{:S(2)}) collective-permute-start(bf16[4,96,192]{2,1,0:T(8,128)(2,1)S(1)} %get-tuple-element.137), channel_id=1, source_target_pairs={{0,1},{1,0},{2,3},{3,2},{4,5},{5,4},{6,7},{7,6},{8,9},{9,8},{10,11... | collective-permute-start | bytes 442376 | tf_op jit(solution)/shard_map/ppermute | solution.py:32
  153.3 37.4 %collective-permute-start.39 = (bf16[96,1536]{1,0:T(8,128)(2,1)S(1)}, bf16[96,1536]{1,0:T(8,128)(2,1)S(1)}, u32[]{:S(2)}, u32[]{:S(2)}) collective-permute-start(bf16[96,1536]{1,0:T(8,128)(2,1)S(1)} %get-tuple-element.196), channel_id=1, source_target_pairs={{0,24},{8,16},{16,8},{24,0},{1,25},{9,17},{17,9},{25,1},{2,26},{10... | collective-permute-start | bytes 884744 | tf_op jit(solution)/shard_map/ppermute | solution.py:32
  163.5 27.3 %collective-permute-start.38 = (bf16[96,1536]{1,0:T(8,128)(2,1)S(1)}, bf16[96,1536]{1,0:T(8,128)(2,1)S(1)}, u32[]{:S(2)}, u32[]{:S(2)}) collective-permute-start(bf16[96,1536]{1,0:T(8,128)(2,1)S(1)} %get-tuple-element.197), channel_id=1, source_target_pairs={{0,16},{8,24},{16,0},{24,8},{1,17},{9,25},{17,1},{25,9},{2,18},{10... | collective-permute-start | bytes 884744 | tf_op jit(solution)/shard_map/ppermute | solution.py:32
  168.8 21.9 %collective-permute-start.37 = (bf16[96,1536]{1,0:T(8,128)(2,1)S(1)}, bf16[96,1536]{1,0:T(8,128)(2,1)S(1)}, u32[]{:S(2)}, u32[]{:S(2)}) collective-permute-start(bf16[96,1536]{1,0:T(8,128)(2,1)S(1)} %get-tuple-element.198), channel_id=1, source_target_pairs={{0,8},{8,0},{16,24},{24,16},{1,9},{9,1},{17,25},{25,17},{2,10},{10... | collective-permute-start | bytes 884744 | tf_op jit(solution)/shard_map/ppermute | solution.py:32
  175.4 11.1 %collective-permute-start.32 = (bf16[4,96,640]{2,1,0:T(8,128)(2,1)S(1)}, bf16[4,96,640]{2,1,0:T(8,128)(2,1)S(1)}, u32[]{:S(2)}, u32[]{:S(2)}) collective-permute-start(bf16[4,96,640]{2,1,0:T(8,128)(2,1)S(1)} %get-tuple-element.152), channel_id=1, source_target_pairs={{0,1},{1,0},{2,3},{3,2},{4,5},{5,4},{6,7},{7,6},{8,9},{9,8},{10,11... | collective-permute-start | bytes 1474568 | tf_op jit(solution)/shard_map/ppermute | solution.py:32
  188.1 25.5 %collective-permute-start.30 = (bf16[256,768]{1,0:T(8,128)(2,1)}, bf16[256,768]{1,0:T(8,128)(2,1)S(1)}, u32[]{:S(2)}, u32[]{:S(2)}) collective-permute-start(bf16[256,768]{1,0:T(8,128)(2,1)} %get-tuple-element.190), channel_id=1, source_target_pairs={{0,4},{2,6},{4,0},{6,2},{1,5},{3,7},{5,1},{7,3},{8,12},{10,14},{12... | collective-permute-start | bytes 1179656 | tf_op jit(solution)/shard_map/ppermute | solution.py:32
  191.8 17.1 %collective-permute-start.34 = (bf16[112,832]{1,0:T(8,128)(2,1)S(1)}, bf16[112,832]{1,0:T(8,128)(2,1)S(1)}, u32[]{:S(2)}, u32[]{:S(2)}) collective-permute-start(bf16[112,832]{1,0:T(8,128)(2,1)S(1)} %get-tuple-element.217), channel_id=1, source_target_pairs={{0,16},{8,24},{16,0},{24,8},{1,17},{9,25},{17,1},{25,9},{2,18},{10... | collective-permute-start | bytes 559112 | tf_op jit(solution)/shard_map/ppermute | solution.py:32
  196.3 12.6 %collective-permute-start.35 = (bf16[112,832]{1,0:T(8,128)(2,1)S(1)}, bf16[112,832]{1,0:T(8,128)(2,1)S(1)}, u32[]{:S(2)}, u32[]{:S(2)}) collective-permute-start(bf16[112,832]{1,0:T(8,128)(2,1)S(1)} %get-tuple-element.218), channel_id=1, source_target_pairs={{0,24},{8,16},{16,8},{24,0},{1,25},{9,17},{17,9},{25,1},{2,26},{10... | collective-permute-start | bytes 559112 | tf_op jit(solution)/shard_map/ppermute | solution.py:32
  (41 other events, 357.8 us)

commit v4 on v3

--- a/solution.py
+++ b/solution.py
@@ -22,6 +22,7 @@
 
 VMEM = pl.BlockSpec(memory_space=pltpu.VMEM)
 SMEM = pl.BlockSpec(memory_space=pltpu.SMEM)
+HBM = pl.BlockSpec(memory_space=pl.ANY)
 
 
 def after(value, *others):
@@ -107,13 +108,13 @@
     return here, swap(far, "heads", 2)
 
 
-def call(body, outs, *args, scratch=(), flops=0, limit=16, plain=False):
-    in_specs = [pl.BlockSpec(memory_space=pl.ANY)] * len(args) if plain else [SMEM] + [VMEM] * (len(args) - 1)
+def call(body, outs, *args, scratch=(), flops=0, limit=16, plain=False, away=()):
+    in_specs = [HBM] * len(args) if plain else [SMEM] + [VMEM] * (len(args) - 1)
     return pl.pallas_call(
         body,
         out_shape=[jax.ShapeDtypeStruct(*o) for o in outs],
         in_specs=in_specs,
-        out_specs=[VMEM] * len(outs),
+        out_specs=[HBM if index in away else VMEM for index in range(len(outs))],
         scratch_shapes=list(scratch),
         compiler_params=pltpu.CompilerParams(vmem_limit_bytes=limit << 20),
         cost_estimate=pl.CostEstimate(flops=flops // 16, transcendentals=0, bytes_accessed=0),
@@ -210,7 +211,7 @@
 
 
 def norm_body(half, quarter, scal, *refs):
-    pieces, hats, form = refs[:4], refs[4], refs[5]
+    pieces, hats, form_out, form, sem = refs[:4], *refs[4:]
     head = scal[0]
     for side in range(2):
         for rel in range(4):
@@ -222,6 +223,10 @@
                 form[ds(base, quarter), :] = hat.astype(b16)
             else:
                 hats[ds(base, quarter), :] = hat
+        if side == 0:
+            copy = pltpu.make_async_copy(form, form_out, sem)
+            copy.start()
+    copy.wait()
 
 
 def front_body(half, quarter, heads, paired, scal, *refs):
@@ -231,7 +236,8 @@
     if not paired:
         norms_in, taps_in, refs = refs[0], refs[1], refs[2:]
     normed, projected, wpad, query, key, value, extra, norms, taps = refs[:9]
-    proj, columns, features, wo = refs[9:]
+    normed_out, projected_out, wpad_out = normed, projected, wpad
+    proj, columns, features, wo, normed, wpad, sems = refs[9:]
     if paired:
         small_rows(scal, (w_own, w_other), heads, norms, taps, columns, features)
     else:
@@ -273,7 +279,13 @@
     def _(block):
         project(block, True)
 
-    projected[...] = proj[half : 2 * half + 16, :]
+    copies = [
+        pltpu.make_async_copy(wpad, wpad_out, sems.at[0]),
+        pltpu.make_async_copy(normed, normed_out, sems.at[1]),
+        pltpu.make_async_copy(proj.at[half : 2 * half + 16, :], projected_out, sems.at[2]),
+    ]
+    for copy in copies:
+        copy.start()
     bounds = edges(scal)
 
     def convolve(block, own):
@@ -302,6 +314,9 @@
     @pl.loop(4, 8)
     def _(block):
         convolve(block, True)
+
+    for copy in copies:
+        copy.wait()
 
 
 def masked_queries(query, slots, heads):
@@ -732,7 +747,8 @@
     hats, form_one = call(
         functools.partial(norm_body, half, quarter),
         [((2 * half, model), f32), ((half, model), b16)],
-        scal, *x_pieces, *y_pieces, flops=2 * half * model, limit=6,
+        scal, *x_pieces, *y_pieces, flops=2 * half * model, limit=8, away=(1,),
+        scratch=[pltpu.VMEM((half, model), b16), pltpu.SemaphoreType.DMA],
     )
     w_own, w_other = gather_seq(shards)
     w_other = after(w_other, hats)
@@ -750,8 +766,9 @@
         scratch=[
             pltpu.VMEM((2 * half + 16, 3 * PADW), b16),
             pltpu.VMEM((model, 128), f32), pltpu.VMEM((KERNEL * HEAD_DIM, 128), f32), pltpu.VMEM((model, PADW), f32),
+            pltpu.VMEM((half, model), b16), pltpu.VMEM((model, 3 * PADW), b16), pltpu.SemaphoreType.DMA((3,)),
         ],
-        flops=4 * half * model * 3 * width, limit=12,
+        flops=4 * half * model * 3 * width, limit=14, away=(0, 1, 2),
     )
 
     feed_own, feed_other = gather_seq(after(feed_shards, query))
@@ -813,6 +830,7 @@
         scratch=[pltpu.VMEM((width, model), f32), pltpu.VMEM((model, width), f32)],
         flops=4 * half * model * width, limit=6,
     )
+    pj_got = scatter_seq(pj_send)
     out_here, out_far = scatter_far(out_keep, after(out_got, dout), quarter)
     remote, query_t, kt = call(
         functools.partial(remote_back_body, half, heads),
@@ -825,12 +843,13 @@
         flops=10 * half * half * width, limit=8,
     )
     remote_in = lax.ppermute(remote, "seq", [(1, 0)])
-    ff_own, ff_rest = join_seq((ff_keep, after(ff_got, remote)))
+    ff_got, pj_got = after((ff_got, pj_got), remote)
+    ff_own, ff_rest = join_seq((ff_keep, ff_got))
 
     dq, dk, dv, front = call(
         functools.partial(local_back_body, half, heads),
         [((half, PADW), b16), ((half, PADW), b16), ((half, PADW), b16), ((8, 3 * PADW), f32)],
-        scal, query, key, value, dout, lse, row_dot, kt, after(query_t, ff_rest), taps,
+        scal, query, key, value, dout, lse, row_dot, kt, after(query_t, ff_rest, pj_got), taps,
         scratch=[
             pltpu.VMEM((heads, half, PADW), b16), pltpu.VMEM((heads, half, PADW), b16),
             pltpu.VMEM((KB, PADW), f32), pltpu.VMEM((KB, PADW), f32), pltpu.VMEM((width, half), f32),
@@ -838,9 +857,7 @@
         flops=10 * half * half * width, limit=8,
     )
     front_in = lax.ppermute(front, "seq", [(1, 0)])
-    pj_got = scatter_seq(after(pj_send, ff_rest))
     remote_in = after(remote_in, dq)
-    front_in = after(front_in, pj_got)
     block_output = (middle_own + out_here + after(out_far, dq).astype(f32)).astype(b16)
 
     proj_grad, w_keep, w_send, sums_taps = call(
@@ -865,17 +882,19 @@
     small = jnp.concatenate([small[0:4], sums_taps[4:8]])
     small = small + swap(small, "seq", 1)
     ff_out, _ = scatter_batch(ff_own, ff_rest, None, small)
+    small = jnp.concatenate([small[0:4] + swap(small[0:4], "heads", 2), small[4:8]])
+    qkv_own, qkv_rest = join_seq((w_keep, after(w_got, small)), (pj_keep, pj_got))
     cut = small.shape[1] // 2
     small = jnp.concatenate([small[:, :cut], small[:, cut:]])
-    qkv_own, qkv_rest = join_seq((w_keep, w_got), (pj_keep, pj_got))
-    qkv_out, small = scatter_batch(qkv_own, qkv_rest, small)
-    pj_out = qkv_out[:, 640:]
-    small = jnp.concatenate([small[:8], small[8:]], axis=1)
     input_grad, _, _ = call(
         functools.partial(norm_back_body, 0),
         [((quarter, model), f32), ((quarter, model), b16), ((8, model), f32)],
         scal, dn_here, dn_far, x_own, middle_grad, norms, limit=6,
     )
+    qkv_out, small = scatter_batch(qkv_own, qkv_rest, small, input_grad)
+    pj_out = qkv_out[:, 640:]
+    small = jnp.concatenate([small[:8], small[8:]], axis=1)
+
     qkv_out = jnp.stack(
         [
             jnp.concatenate([qkv_out[:, 0:128], qkv_out[:, 384:448]], axis=1),
@@ -885,7 +904,6 @@
         axis=1,
     )
     gains = lax.dynamic_slice_in_dim(small[0:4], own * group, group, 1)
-    gains = gains + swap(gains, "heads", 2)
     kernel_out = small[4 : 4 + KERNEL].reshape(KERNEL, 3, PADW)[:, :, :width].reshape(KERNEL, 3, heads, HEAD_DIM)
     kernel_out = kernel_out.transpose(1, 2, 3, 0).reshape(3, heads, HEAD_DIM * KERNEL)
     kernel_out = lax.dynamic_slice_in_dim(kernel_out, own * share, share, 2)

time: 217 us -> 216 us (level)
  starting transfers between devices: 53.5 us -> 40.8 us
  waiting for transfers between devices: 74.1 us -> 86.2 us
    ppermute x37, starting transfers between devices: 46.6 us -> 34 us  [swap(): lax.ppermute(shard, axis, [(i, i ^ by) for i in range(lax.axis_size(axis))])]
    ppermute x1, waiting for transfers between devices: 0.01 us -> 7.93 us  [on_device(): remote_in = lax.ppermute(remote, 'seq', [(1, 0)])]
    ppermute x37, waiting for transfers between devices: 74.1 us -> 78.3 us  [swap(): lax.ppermute(shard, axis, [(i, i ^ by) for i in range(lax.axis_size(axis))])]
  transfers between devices with their start and end apart: 40 -> 40, of which waited for: 16 -> 20; matrix products, arithmetic and copies ran while one was open for 7% -> 5% of each run, Pallas kernels for 24% -> 25%
where the time goes in v4:
time: 216 us; the launch traced here: 215 us
  waiting for transfers between devices  86.2 us (40%)
  Pallas kernels  63.2 us (29%)
  starting transfers between devices  40.8 us (19%)
  local copies, waits for them, and re-layouts  13.9 us (6%)
  other arithmetic  9.65 us (4%)
    ppermute x37, waiting for transfers between devices, swap(): lax.ppermute(shard, axis, [(i, i ^ by) for i in range(lax.axis_size(axis))])  78.3 us
    pallas_call x15, Pallas kernels, call(): pl.pallas_call(body, out_shape=[jax.ShapeDtypeStruct(*o) for o in outs],...  63.2 us
    ppermute x37, starting transfers between devices, swap(): lax.ppermute(shard, axis, [(i, i ^ by) for i in range(lax.axis_size(axis))])  34 us
    unnamed x68, local copies, waits for them, and re-layouts  10.4 us
    ppermute x1, waiting for transfers between devices, on_device(): remote_in = lax.ppermute(remote, 'seq', [(1, 0)])  7.93 us
  transfers between devices with their start and end apart: 40, of which 20 were waited for; matrix products, arithmetic and copies ran while one was open for 5% of the time, Pallas kernels for 25%

profile of v4, /device:TPU:0, one launch (start us, length us, event | category | flops | bytes accessed | tf_op | source)
XLA Modules:
  0.0 215.1 jit_solution(12919286304800134578)
XLA Ops:
  0.7 4.0 %collective-permute-start.2 = (bf16[256,768]{1,0:T(8,128)(2,1)}, bf16[256,768]{1,0:T(8,128)(2,1)S(1)}, u32[]{:S(2)}, u32[]{:S(2)}) collective-permute-start(bf16[256,768]{1,0:T(8,128)(2,1)} %bitcast.79), channel_id=1, source_target_pairs={{0,5},{1,4},{2,7},{3,6},{4,1},{5,0},{6,3},{7,2},{8,13},{9,12},{10,... | collective-permute-start | bytes 1179656 | tf_op jit(solution)/shard_map/ppermute | solution.py:743
  8.9 3.1 %collective-permute-start.3 = (bf16[96,896]{1,0:T(8,128)(2,1)S(1)}, bf16[96,896]{1,0:T(8,128)(2,1)S(1)}, u32[]{:S(2)}, u32[]{:S(2)}) collective-permute-start(bf16[96,896]{1,0:T(8,128)(2,1)S(1)} %shard_map.203), channel_id=1, source_target_pairs={{0,16},{8,24},{16,0},{24,8},{1,17},{9,25},{17,1},{25,9},{2,18},{10... | collective-permute-start | bytes 516104 | tf_op jit(solution)/shard_map/ppermute | solution.py:33
  11.9 7.2 %collective-permute-done.3 = bf16[96,896]{1,0:T(8,128)(2,1)S(1)} collective-permute-done((bf16[96,896]{1,0:T(8,128)(2,1)S(1)}, bf16[96,896]{1,0:T(8,128)(2,1)S(1)}, u32[]{:S(2)}, u32[]{:S(2)}) %collective-permute-start.3) | collective-permute-done | bytes 172064 | tf_op jit(solution)/shard_map/ppermute | solution.py:33
  20.0 2.7 %collective-permute-done.1 = bf16[256,768]{1,0:T(8,128)(2,1)S(1)} collective-permute-done((bf16[256,768]{1,0:T(8,128)(2,1)}, bf16[256,768]{1,0:T(8,128)(2,1)S(1)}, u32[]{:S(2)}, u32[]{:S(2)}) %collective-permute-start.1) | collective-permute-done | bytes 393248 | tf_op jit(solution)/shard_map/ppermute | solution.py:33
  24.9 3.3 %collective-permute-done.6 = bf16[192,896]{1,0:T(8,128)(2,1)S(1)} collective-permute-done((bf16[192,896]{1,0:T(8,128)(2,1)S(1)}, bf16[192,896]{1,0:T(8,128)(2,1)S(1)}, u32[]{:S(2)}, u32[]{:S(2)}) %collective-permute-start.6) | collective-permute-done | bytes 344096 | tf_op jit(solution)/shard_map/ppermute | solution.py:33
  30.8 4.5 %collective-permute-start.16 = (bf16[96,1536]{1,0:T(8,128)(2,1)}, bf16[96,1536]{1,0:T(8,128)(2,1)}, u32[]{:S(2)}, u32[]{:S(2)}) collective-permute-start(bf16[96,1536]{1,0:T(8,128)(2,1)} %pad_maximum_fusion.5), channel_id=1, source_target_pairs={{0,24},{8,16},{16,8},{24,0},{1,25},{9,17},{17,9},{25,1},{2,26},{10... | collective-permute-start | bytes 884744 | tf_op jit(solution)/shard_map/ppermute | solution.py:33
  36.0 3.7 %shard_map.204 = (f32[2048,768]{1,0:T(8,128)S(1)}, bf16[1024,768]{1,0:T(8,128)(2,1)S(1)}) custom-call(s32[8]{0:T(128)S(1)} %concatenate.48.scal, bf16[512,768]{1,0:T(8,128)(2,1)S(1)} %pad_maximum_fusion.2.refs_0_.refs_8_, bf16[512,768]{1,0:T(8,128)(2,1)S(1)} %collective-permute-done.4.refs_1_.refs_9_, ...), custom_call_target="tpu_custom_call" | custom-call | flops 98304 | tf_op jit(solution)/shard_map/pallas_call | solution.py:113
  40.9 3.3 %collective-permute-done.7.refs_2_ = bf16[4,96,896]{2,1,0:T(8,128)(2,1)} collective-permute-done((bf16[4,96,896]{2,1,0:T(8,128)(2,1)S(1)}, bf16[4,96,896]{2,1,0:T(8,128)(2,1)}, u32[]{:S(2)}, u32[]{:S(2)}) %collective-permute-start.7) | collective-permute-done | bytes 688160 | tf_op jit(solution)/shard_map/ppermute | solution.py:33
  45.3 9.2 %shard_map.205 = (bf16[1024,768]{1,0:T(8,128)(2,1)S(1)}, bf16[1040,768]{1,0:T(8,128)(2,1)S(1)}, bf16[768,768]{1,0:T(8,128)(2,1)S(1)}, bf16[1024,256]{1,0:T(8,128...) custom-call(s32[8]{0:T(128)S(1)} %concatenate.48.scal, ...), custom_call_target="tpu_custom_call" | custom-call | flops 113246208 | tf_op jit(solution)/shard_map/pallas_call | solution.py:113
  55.7 3.9 %collective-permute-done.15 = bf16[96,1536]{1,0:T(8,128)(2,1)} collective-permute-done((bf16[96,1536]{1,0:T(8,128)(2,1)}, bf16[96,1536]{1,0:T(8,128)(2,1)}, u32[]{:S(2)}, u32[]{:S(2)}) %collective-permute-start.15) | collective-permute-done | bytes 294944 | tf_op jit(solution)/shard_map/ppermute | solution.py:33
  63.1 8.0 %shard_map.206 = (bf16[1536,128]{1,0:T(8,128)(2,1)S(1)}, f32[192,1024]{1,0:T(8,128)S(1)}, f32[8,1024]{1,0:T(8,128)S(1)}) custom-call(s32[8]{0:T(128)S(1)} %concatenate.48.scal, bf16[1024,256]{1,0:T(8,128)(2,1)S(1)} %get-tuple-element.92.query.refs_0_, bf16[2048,256]{1,0:T(8,128)(2,1)S(1)} %get-tuple-element.93.key.refs_1_, ...), custom_call_target="tpu_custom_call" | custom-call | flops 50331648 | tf_op jit(solution)/shard_map/pallas_call | solution.py:113
  71.7 6.2 %collective-permute-done.12.refs_6_.refs_2_ = bf16[448,768]{1,0:T(8,128)(2,1)S(1)} collective-permute-done((bf16[448,768]{1,0:T(8,128)(2,1)S(1)}, bf16[448,768]{1,0:T(8,128)(2,1)S(1)}, u32[]{:S(2)}, u32[]{:S(2)}) %collective-permute-start.12) | collective-permute-done | bytes 688160 | tf_op jit(solution)/shard_map/ppermute | solution.py:33
  78.4 6.1 %collective-permute-done.9.refs_2_ = bf16[1536,128]{1,0:T(8,128)(2,1)S(1)} collective-permute-done((bf16[1536,128]{1,0:T(8,128)(2,1)S(1)}, bf16[1536,128]{1,0:T(8,128)(2,1)S(1)}, u32[]{:S(2)}, u32[]{:S(2)}) %collective-permute-start.9) | collective-permute-done | bytes 393248 | tf_op jit(solution)/shard_map/ppermute | solution.py:33
  84.5 4.8 %collective-permute-done.17.refs_1_ = bf16[4,96,1536]{2,1,0:T(8,128)(2,1)S(1)} collective-permute-done((bf16[4,96,1536]{2,1,0:T(8,128)(2,1)S(1)}, bf16[4,96,1536]{2,1,0:T(8,128)(2,1)S(1)}, u32[]{:S(2)}, u32[]{:S(2)}) %collective-permute-start.17) | collective-permute-done | bytes 1179680 | tf_op jit(solution)/shard_map/ppermute | solution.py:33
  90.0 8.6 %shard_map.208 = (bf16[1024,768]{1,0:T(8,128)(2,1)S(1)}, bf16[1024,768]{1,0:T(8,128)(2,1)S(1)}, bf16[1024,768]{1,0:T(8,128)(2,1)S(1)}, f32[512,768]{1,0:T(8,128)...) custom-call(s32[8]{0:T(128)S(1)} %concatenate.48.scal, bf16[1536,128]{1,0:T(8,128)(2,1)S(1)} %get-tuple-element.95.refs_0_, ...), custom_call_target="tpu_custom_call" | custom-call | flops 301989888 | tf_op jit(solution)/shard_map/pallas_call | solution.py:113
  101.7 4.6 %shard_map.210 = (f32[512,768]{1,0:T(8,128)S(1)}, bf16[512,768]{1,0:T(8,128)(2,1)}, bf16[4,96,1536]{2,1,0:T(8,128)(2,1)S(1)}, bf16[4,96,1536]{2,1,0:T(8,128)(2,1)}) custom-call(s32[8]{0:T(128)S(1)} %concatenate.48.scal, bf16[1024,768]{1,0:T(8,128)(2,1)S(1)} %get-tuple-element.112.refs_0_, bf16[1024,768]{1,0:T(8,128)(2,1)S(1)} %get-tuple-element.110.refs_4_.refs_1_, ...), custom_call_target="tpu_custom_call" | custom-call | flops 150994944 | tf_op jit(solution)/shard_map/pallas_call | solution.py:113
  107.8 4.6 %collective-permute-done.19.got = bf16[256,768]{1,0:T(8,128)(2,1)S(1)} collective-permute-done((bf16[256,768]{1,0:T(8,128)(2,1)S(1)}, bf16[256,768]{1,0:T(8,128)(2,1)S(1)}, u32[]{:S(2)}, u32[]{:S(2)}) %collective-permute-start.19) | collective-permute-done | bytes 393248 | tf_op jit(solution)/shard_map/ppermute | solution.py:33
  116.3 9.8 %collective-permute-done.22.refs_2_ = bf16[256,768]{1,0:T(8,128)(2,1)} collective-permute-done((bf16[256,768]{1,0:T(8,128)(2,1)}, bf16[256,768]{1,0:T(8,128)(2,1)}, u32[]{:S(2)}, u32[]{:S(2)}) %collective-permute-start.22) | collective-permute-done | bytes 393248 | tf_op jit(solution)/shard_map/ppermute | solution.py:33
  126.1 2.1 collective-permute-done.23.refs_3_
  129.3 2.8 %shard_map.212 = (bf16[1024,256]{1,0:T(8,128)(2,1)S(1)}, f32[8,1024]{1,0:T(8,128)S(1)}, f32[4,96,192]{2,1,0:T(8,128)S(1)}, bf16[4,96,192]{2,1,0:T(8,128)(2,1)S(1)}) custom-call(s32[8]{0:T(128)S(1)} %concatenate.48.scal, bf16[256,768]{1,0:T(8,128)(2,1)} %get-tuple-element.118.refs_0_, bf16[256,768]{1,0:T(8,128)(2,1)} %collective-permute-done.21.refs_1_, ...), custom_call_target="tpu_custom_call" | custom-call | flops 37748736 | tf_op jit(solution)/shard_map/pallas_call | solution.py:113
  134.3 2.2 %shard_map.213 = (bf16[1024,384]{1,0:T(8,128)(2,1)S(1)}, f32[192,1024]{1,0:T(8,128)S(1)}, bf16[192,2048]{1,0:T(8,128)(2,1)S(1)}) custom-call(s32[8]{0:T(128)S(1)} %concatenate.48.scal, bf16[1024,256]{1,0:T(8,128)(2,1)S(1)} %get-tuple-element.92.query.refs_0_, bf16[2048,256]{1,0:T(8,128)(2,1)S(1)} %get-tuple-element.93.key.refs_1_, ...), custom_call_target="tpu_custom_call" | custom-call | flops 125829120 | tf_op jit(solution)/shard_map/pallas_call | solution.py:113
  139.6 9.3 %shard_map.214 = (bf16[1024,256]{1,0:T(8,128)(2,1)S(1)}, bf16[1024,256]{1,0:T(8,128)(2,1)S(1)}, bf16[1024,256]{1,0:T(8,128)(2,1)S(1)}, f32[8,768]{1,0:T(8,128)S(1)}) custom-call(s32[8]{0:T(128)S(1)} %concatenate.48.scal, bf16[1024,256]{1,0:T(8,128)(2,1)S(1)} %get-tuple-element.92.query.refs_0_, bf16[2048,256]{1,0:T(8,128)(2,1)S(1)} %get-tuple-element.93.key.refs_1_, ...), custom_call_target="tpu_custom_call" | custom-call | flops 125829120 | tf_op jit(solution)/shard_map/pallas_call | solution.py:113
  154.2 7.9 %collective-permute-done.27.refs_3_ = bf16[1024,384]{1,0:T(8,128)(2,1)S(1)} collective-permute-done((bf16[1024,384]{1,0:T(8,128)(2,1)S(1)}, bf16[1024,384]{1,0:T(8,128)(2,1)S(1)}, u32[]{:S(2)}, u32[]{:S(2)}) %collective-permute-start.27) | collective-permute-done | bytes 786464 | tf_op jit(solution)/shard_map/ppermute | solution.py:845
  163.8 5.4 %shard_map.215 = (bf16[1024,768]{1,0:T(8,128)(2,1)S(1)}, f32[4,96,640]{2,1,0:T(8,128)S(1)}, bf16[4,96,640]{2,1,0:T(8,128)(2,1)S(1)}, f32[8,768]{1,0:T(8,128)S(1)}) custom-call(s32[8]{0:T(128)S(1)} %concatenate.48.scal, bf16[1024,256]{1,0:T(8,128)(2,1)S(1)} %get-tuple-element.133.refs_0_, bf16[1024,256]{1,0:T(8,128)(2,1)S(1)} %get-tuple-element.135.refs_1_, ...), custom_call_target="tpu_custom_call" | custom-call | flops 56623104 | tf_op jit(solution)/shard_map/pallas_call | solution.py:113
  170.9 2.1 shard_map.216
  175.0 6.2 %collective-permute-done.33 = bf16[4,96,640]{2,1,0:T(8,128)(2,1)S(1)} collective-permute-done((bf16[4,96,640]{2,1,0:T(8,128)(2,1)S(1)}, bf16[4,96,640]{2,1,0:T(8,128)(2,1)S(1)}, u32[]{:S(2)}, u32[]{:S(2)}) %collective-permute-start.33) | collective-permute-done | bytes 491552 | tf_op jit(solution)/shard_map/ppermute | solution.py:33
  187.3 5.4 %collective-permute-done.32 = f32[4,768]{1,0:T(4,128)S(1)} collective-permute-done((f32[4,768]{1,0:T(4,128)S(1)}, f32[4,768]{1,0:T(4,128)S(1)}, u32[]{:S(2)}, u32[]{:S(2)}) %collective-permute-start.32) | collective-permute-done | bytes 12320 | tf_op jit(solution)/shard_map/ppermute | solution.py:33
  192.8 4.8 %collective-permute-start.36 = (bf16[112,832]{1,0:T(8,128)(2,1)S(1)}, bf16[112,832]{1,0:T(8,128)(2,1)S(1)}, u32[]{:S(2)}, u32[]{:S(2)}) collective-permute-start(bf16[112,832]{1,0:T(8,128)(2,1)S(1)} %get-tuple-element.224), channel_id=1, source_target_pairs={{0,24},{8,16},{16,8},{24,0},{1,25},{9,17},{17,9},{25,1},{2,26},{10... | collective-permute-start | bytes 559112 | tf_op jit(solution)/shard_map/ppermute | solution.py:33
  199.1 2.2 %shard_map.217 = (f32[256,768]{1,0:T(8,128)}, bf16[256,768]{1,0:T(8,128)(2,1)}, f32[8,768]{1,0:T(8,128)}) custom-call(s32[8]{0:T(128)S(1)} %concatenate.48.scal, f32[256,768]{1,0:T(8,128)S(1)} %get-tuple-element.197.part, bf16[256,768]{1,0:T(8,128)(2,1)S(1)} %collective-permute-done.30.got, bf16[256,768]{1,0:T(8,128)(2,1)S(1)} %bitcast.83, ...), custom_call_target="tpu_custom_call" | custom-call | tf_op jit(solution)/shard_map/pallas_call | solution.py:113
  201.3 2.2 %collective-permute-done.36 = bf16[112,832]{1,0:T(8,128)(2,1)S(1)} collective-permute-done((bf16[112,832]{1,0:T(8,128)(2,1)S(1)}, bf16[112,832]{1,0:T(8,128)(2,1)S(1)}, u32[]{:S(2)}, u32[]{:S(2)}) %collective-permute-start.36) | collective-permute-done | bytes 186400 | tf_op jit(solution)/shard_map/ppermute | solution.py:33
  203.5 2.3 %collective-permute-done.34 = bf16[112,832]{1,0:T(8,128)(2,1)S(1)} collective-permute-done((bf16[112,832]{1,0:T(8,128)(2,1)S(1)}, bf16[112,832]{1,0:T(8,128)(2,1)S(1)}, u32[]{:S(2)}, u32[]{:S(2)}) %collective-permute-start.34) | collective-permute-done | bytes 186400 | tf_op jit(solution)/shard_map/ppermute | solution.py:33
  205.9 5.8 %collective-permute-done.35 = bf16[112,832]{1,0:T(8,128)(2,1)S(1)} collective-permute-done((bf16[112,832]{1,0:T(8,128)(2,1)S(1)}, bf16[112,832]{1,0:T(8,128)(2,1)S(1)}, u32[]{:S(2)}, u32[]{:S(2)}) %collective-permute-start.35) | collective-permute-done | bytes 186400 | tf_op jit(solution)/shard_map/ppermute | solution.py:33
  (181 shorter events, 55.6 us)
Async XLA Ops:
  0.7 19.3 %collective-permute-start.2 = (bf16[256,768]{1,0:T(8,128)(2,1)}, bf16[256,768]{1,0:T(8,128)(2,1)S(1)}, u32[]{:S(2)}, u32[]{:S(2)}) collective-permute-start(bf16[256,768]{1,0:T(8,128)(2,1)} %bitcast.79), channel_id=1, source_target_pairs={{0,5},{1,4},{2,7},{3,6},{4,1},{5,0},{6,3},{7,2},{8,13},{9,12},{10,... | collective-permute-start | bytes 1179656 | tf_op jit(solution)/shard_map/ppermute | solution.py:743
  4.6 18.0 %collective-permute-start.1 = (bf16[256,768]{1,0:T(8,128)(2,1)}, bf16[256,768]{1,0:T(8,128)(2,1)S(1)}, u32[]{:S(2)}, u32[]{:S(2)}) collective-permute-start(bf16[256,768]{1,0:T(8,128)(2,1)} %bitcast.80), channel_id=1, source_target_pairs={{0,4},{2,6},{4,0},{6,2},{1,5},{3,7},{5,1},{7,3},{8,12},{10,14},{12... | collective-permute-start | bytes 1179656 | tf_op jit(solution)/shard_map/ppermute | solution.py:33
  5.2 17.5 %collective-permute-start = (bf16[256,768]{1,0:T(8,128)(2,1)}, bf16[256,768]{1,0:T(8,128)(2,1)S(1)}, u32[]{:S(2)}, u32[]{:S(2)}) collective-permute-start(bf16[256,768]{1,0:T(8,128)(2,1)} %bitcast.81), channel_id=1, source_target_pairs={{0,1},{1,0},{2,3},{3,2},{4,5},{5,4},{6,7},{7,6},{8,9},{9,8},{10,11... | collective-permute-start | bytes 1179656 | tf_op jit(solution)/shard_map/ppermute | solution.py:33
  8.9 10.3 %collective-permute-start.3 = (bf16[96,896]{1,0:T(8,128)(2,1)S(1)}, bf16[96,896]{1,0:T(8,128)(2,1)S(1)}, u32[]{:S(2)}, u32[]{:S(2)}) collective-permute-start(bf16[96,896]{1,0:T(8,128)(2,1)S(1)} %shard_map.203), channel_id=1, source_target_pairs={{0,16},{8,24},{16,0},{24,8},{1,17},{9,25},{17,1},{25,9},{2,18},{10... | collective-permute-start | bytes 516104 | tf_op jit(solution)/shard_map/ppermute | solution.py:33
  19.2 9.0 %collective-permute-start.6 = (bf16[192,896]{1,0:T(8,128)(2,1)S(1)}, bf16[192,896]{1,0:T(8,128)(2,1)S(1)}, u32[]{:S(2)}, u32[]{:S(2)}) collective-permute-start(bf16[192,896]{1,0:T(8,128)(2,1)S(1)} %pad_maximum_fusion.4), channel_id=1, source_target_pairs={{0,8},{8,0},{16,24},{24,16},{1,9},{9,1},{17,25},{25,17},{2,10},{10... | collective-permute-start | bytes 1032200 | tf_op jit(solution)/shard_map/ppermute | solution.py:33
  24.2 11.0 %collective-permute-start.5 = (bf16[512,768]{1,0:T(8,128)(2,1)}, bf16[512,768]{1,0:T(8,128)(2,1)}, u32[]{:S(2)}, u32[]{:S(2)}) collective-permute-start(bf16[512,768]{1,0:T(8,128)(2,1)} %constant_dynamic-update-slice_fusion.refs_2_), channel_id=1, source_target_pairs={{0,2},{2,0},{4,6},{6,4},{1,3},{3,1},{5,7},{7,5},{8,10},{10,8},{12,... | collective-permute-start | bytes 2359304 | tf_op jit(solution)/shard_map/ppermute | solution.py:33
  24.3 11.7 %collective-permute-start.4 = (bf16[512,768]{1,0:T(8,128)(2,1)S(1)}, bf16[512,768]{1,0:T(8,128)(2,1)S(1)}, u32[]{:S(2)}, u32[]{:S(2)}) collective-permute-start(bf16[512,768]{1,0:T(8,128)(2,1)S(1)} %pad_maximum_fusion.2.refs_0_.refs_8_), channel_id=1, source_target_pairs={{0,2},{2,0},{4,6},{6,4},{1,3},{3,1},{5,7},{7,5},{8,10},{10,8},{12,... | collective-permute-start | bytes 2359304 | tf_op jit(solution)/shard_map/ppermute | solution.py:33
  28.3 15.9 %collective-permute-start.7 = (bf16[4,96,896]{2,1,0:T(8,128)(2,1)S(1)}, bf16[4,96,896]{2,1,0:T(8,128)(2,1)}, u32[]{:S(2)}, u32[]{:S(2)}) collective-permute-start(bf16[4,96,896]{2,1,0:T(8,128)(2,1)S(1)} %pad_maximum_fusion.3.refs_1_), channel_id=1, source_target_pairs={{0,1},{1,0},{2,3},{3,2},{4,5},{5,4},{6,7},{7,6},{8,9},{9,8},{10,11... | collective-permute-start | bytes 2064392 | tf_op jit(solution)/shard_map/ppermute | solution.py:33
  30.8 24.9 %collective-permute-start.16 = (bf16[96,1536]{1,0:T(8,128)(2,1)}, bf16[96,1536]{1,0:T(8,128)(2,1)}, u32[]{:S(2)}, u32[]{:S(2)}) collective-permute-start(bf16[96,1536]{1,0:T(8,128)(2,1)} %pad_maximum_fusion.5), channel_id=1, source_target_pairs={{0,24},{8,16},{16,8},{24,0},{1,25},{9,17},{17,9},{25,1},{2,26},{10... | collective-permute-start | bytes 884744 | tf_op jit(solution)/shard_map/ppermute | solution.py:33
  35.2 24.4 %collective-permute-start.15 = (bf16[96,1536]{1,0:T(8,128)(2,1)}, bf16[96,1536]{1,0:T(8,128)(2,1)}, u32[]{:S(2)}, u32[]{:S(2)}) collective-permute-start(bf16[96,1536]{1,0:T(8,128)(2,1)} %pad_maximum_fusion.5), channel_id=1, source_target_pairs={{0,16},{8,24},{16,0},{24,8},{1,17},{9,25},{17,1},{25,9},{2,18},{10... | collective-permute-start | bytes 884744 | tf_op jit(solution)/shard_map/ppermute | solution.py:33
  35.2 24.4 %collective-permute-start.14 = (bf16[96,1536]{1,0:T(8,128)(2,1)}, bf16[96,1536]{1,0:T(8,128)(2,1)}, u32[]{:S(2)}, u32[]{:S(2)}) collective-permute-start(bf16[96,1536]{1,0:T(8,128)(2,1)} %pad_maximum_fusion.5), channel_id=1, source_target_pairs={{0,8},{8,0},{16,24},{24,16},{1,9},{9,1},{17,25},{25,17},{2,10},{10... | collective-permute-start | bytes 884744 | tf_op jit(solution)/shard_map/ppermute | solution.py:33
  59.6 18.3 %collective-permute-start.12 = (bf16[448,768]{1,0:T(8,128)(2,1)S(1)}, bf16[448,768]{1,0:T(8,128)(2,1)S(1)}, u32[]{:S(2)}, u32[]{:S(2)}) collective-permute-start(bf16[448,768]{1,0:T(8,128)(2,1)S(1)} %get-tuple-element.96.refs_4_.refs_0_), channel_id=1, source_target_pairs={{0,4},{2,6},{4,0},{6,2},{1,5},{3,7},{5,1},{7,3},{8,12},{10,14},{12... | collective-permute-start | bytes 2064392 | tf_op jit(solution)/shard_map/ppermute | solution.py:33
  62.5 26.8 %collective-permute-start.17 = (bf16[4,96,1536]{2,1,0:T(8,128)(2,1)S(1)}, bf16[4,96,1536]{2,1,0:T(8,128)(2,1)S(1)}, u32[]{:S(2)}, u32[]{:S(2)}) collective-permute-start(bf16[4,96,1536]{2,1,0:T(8,128)(2,1)S(1)} %pad_maximum_fusion.1.refs_0_), channel_id=1, source_target_pairs={{0,1},{1,0},{2,3},{3,2},{4,5},{5,4},{6,7},{7,6},{8,9},{9,8},{10,11... | collective-permute-start | bytes 3538952 | tf_op jit(solution)/shard_map/ppermute | solution.py:33
  71.1 13.4 %collective-permute-start.9 = (bf16[1536,128]{1,0:T(8,128)(2,1)S(1)}, bf16[1536,128]{1,0:T(8,128)(2,1)S(1)}, u32[]{:S(2)}, u32[]{:S(2)}) collective-permute-start(bf16[1536,128]{1,0:T(8,128)(2,1)S(1)} %get-tuple-element.95.refs_0_), channel_id=1, source_target_pairs={{0,4},{2,6},{4,0},{6,2},{1,5},{3,7},{5,1},{7,3},{8,12},{10,14},{12... | collective-permute-start | bytes 1179656 | tf_op jit(solution)/shard_map/ppermute | solution.py:33
  71.7 18.3 %collective-permute-start.11 = (bf16[448,768]{1,0:T(8,128)(2,1)S(1)}, bf16[448,768]{1,0:T(8,128)(2,1)S(1)}, u32[]{:S(2)}, u32[]{:S(2)}) collective-permute-start(bf16[448,768]{1,0:T(8,128)(2,1)S(1)} %get-tuple-element.96.refs_4_.refs_0_), channel_id=1, source_target_pairs={{0,2},{2,0},{4,6},{6,4},{1,3},{3,1},{5,7},{7,5},{8,10},{10,8},{12,... | collective-permute-start | bytes 2064392 | tf_op jit(solution)/shard_map/ppermute | solution.py:33
  77.9 12.1 %collective-permute-start.13 = (bf16[448,768]{1,0:T(8,128)(2,1)S(1)}, bf16[448,768]{1,0:T(8,128)(2,1)S(1)}, u32[]{:S(2)}, u32[]{:S(2)}) collective-permute-start(bf16[448,768]{1,0:T(8,128)(2,1)S(1)} %collective-permute-done.12.refs_6_.refs_2_), channel_id=1, source_target_pairs={{0,2},{2,0},{4,6},{6,4},{1,3},{3,1},{5,7},{7,5},{8,10},{10,8},{12,... | collective-permute-start | bytes 2064392 | tf_op jit(solution)/shard_map/ppermute | solution.py:33
  77.9 12.0 %collective-permute-start.8 = (bf16[1536,128]{1,0:T(8,128)(2,1)S(1)}, bf16[1536,128]{1,0:T(8,128)(2,1)S(1)}, u32[]{:S(2)}, u32[]{:S(2)}) collective-permute-start(bf16[1536,128]{1,0:T(8,128)(2,1)S(1)} %get-tuple-element.95.refs_0_), channel_id=1, source_target_pairs={{0,2},{2,0},{4,6},{6,4},{1,3},{3,1},{5,7},{7,5},{8,10},{10,8},{12,... | collective-permute-start | bytes 1179656 | tf_op jit(solution)/shard_map/ppermute | solution.py:33
  101.1 11.3 %collective-permute-start.19 = (bf16[256,768]{1,0:T(8,128)(2,1)S(1)}, bf16[256,768]{1,0:T(8,128)(2,1)S(1)}, u32[]{:S(2)}, u32[]{:S(2)}) collective-permute-start(bf16[256,768]{1,0:T(8,128)(2,1)S(1)} %get-tuple-element.200), channel_id=1, source_target_pairs={{0,4},{2,6},{4,0},{6,2},{1,5},{3,7},{5,1},{7,3},{8,12},{10,14},{12... | collective-permute-start | bytes 1179656 | tf_op jit(solution)/shard_map/ppermute | solution.py:33
  107.3 30.5 %collective-permute-start.25 = (bf16[4,96,1536]{2,1,0:T(8,128)(2,1)}, bf16[4,96,1536]{2,1,0:T(8,128)(2,1)}, u32[]{:S(2)}, u32[]{:S(2)}) collective-permute-start(bf16[4,96,1536]{2,1,0:T(8,128)(2,1)} %get-tuple-element.127), channel_id=1, source_target_pairs={{0,1},{1,0},{2,3},{3,2},{4,5},{5,4},{6,7},{7,6},{8,9},{9,8},{10,11... | collective-permute-start | bytes 3538952 | tf_op jit(solution)/shard_map/ppermute | solution.py:33
  115.3 10.8 %collective-permute-start.22 = (bf16[256,768]{1,0:T(8,128)(2,1)}, bf16[256,768]{1,0:T(8,128)(2,1)}, u32[]{:S(2)}, u32[]{:S(2)}) collective-permute-start(bf16[256,768]{1,0:T(8,128)(2,1)} %get-tuple-element.118.refs_0_), channel_id=1, source_target_pairs={{0,4},{2,6},{4,0},{6,2},{1,5},{3,7},{5,1},{7,3},{8,12},{10,14},{12... | collective-permute-start | bytes 1179656 | tf_op jit(solution)/shard_map/ppermute | solution.py:33
  115.8 16.9 %collective-permute-start.20 = (bf16[512,768]{1,0:T(8,128)(2,1)}, bf16[512,768]{1,0:T(8,128)(2,1)}, u32[]{:S(2)}, u32[]{:S(2)}) collective-permute-start(bf16[512,768]{1,0:T(8,128)(2,1)} %get-tuple-element.119), channel_id=1, source_target_pairs={{0,2},{2,0},{4,6},{6,4},{1,3},{3,1},{5,7},{7,5},{8,10},{10,8},{12,... | collective-permute-start | bytes 2359304 | tf_op jit(solution)/shard_map/ppermute | solution.py:33
  115.8 10.3 %collective-permute-start.21 = (bf16[256,768]{1,0:T(8,128)(2,1)}, bf16[256,768]{1,0:T(8,128)(2,1)}, u32[]{:S(2)}, u32[]{:S(2)}) collective-permute-start(bf16[256,768]{1,0:T(8,128)(2,1)} %get-tuple-element.118.refs_0_), channel_id=1, source_target_pairs={{0,2},{2,0},{4,6},{6,4},{1,3},{3,1},{5,7},{7,5},{8,10},{10,8},{12,... | collective-permute-start | bytes 1179656 | tf_op jit(solution)/shard_map/ppermute | solution.py:33
  133.8 37.1 %collective-permute-start.24 = (bf16[256,768]{1,0:T(8,128)(2,1)S(1)}, bf16[256,768]{1,0:T(8,128)(2,1)S(1)}, u32[]{:S(2)}, u32[]{:S(2)}) collective-permute-start(bf16[256,768]{1,0:T(8,128)(2,1)S(1)} %add_convert_fusion.2), channel_id=1, source_target_pairs={{0,4},{2,6},{4,0},{6,2},{1,5},{3,7},{5,1},{7,3},{8,12},{10,14},{12... | collective-permute-start | bytes 1179656 | tf_op jit(solution)/shard_map/ppermute | solution.py:33
  136.5 25.7 %collective-permute-start.27 = (bf16[1024,384]{1,0:T(8,128)(2,1)S(1)}, bf16[1024,384]{1,0:T(8,128)(2,1)S(1)}, u32[]{:S(2)}, u32[]{:S(2)}) collective-permute-start(bf16[1024,384]{1,0:T(8,128)(2,1)S(1)} %get-tuple-element.129), channel_id=1, source_target_pairs={{1,0},{3,2},{5,4},{7,6},{9,8},{11,10},{13,12},{15,14},{17,16},{19,... | collective-permute-start | bytes 2359304 | tf_op jit(solution)/shard_map/ppermute | solution.py:845
  148.9 14.9 %collective-permute-start.28 = (f32[8,768]{1,0:T(8,128)S(1)}, f32[8,768]{1,0:T(8,128)S(1)}, u32[]{:S(2)}, u32[]{:S(2)}) collective-permute-start(f32[8,768]{1,0:T(8,128)S(1)} %get-tuple-element.138), channel_id=1, source_target_pairs={{1,0},{3,2},{5,4},{7,6},{9,8},{11,10},{13,12},{15,14},{17,16},{19,... | collective-permute-start | bytes 73736 | tf_op jit(solution)/shard_map/ppermute | solution.py:859
  152.4 34.8 %collective-permute-start.39 = (bf16[96,1536]{1,0:T(8,128)(2,1)S(1)}, bf16[96,1536]{1,0:T(8,128)(2,1)S(1)}, u32[]{:S(2)}, u32[]{:S(2)}) collective-permute-start(bf16[96,1536]{1,0:T(8,128)(2,1)S(1)} %get-tuple-element.202), channel_id=1, source_target_pairs={{0,24},{8,16},{16,8},{24,0},{1,25},{9,17},{17,9},{25,1},{2,26},{10... | collective-permute-start | bytes 884744 | tf_op jit(solution)/shard_map/ppermute | solution.py:33
  154.2 32.9 %collective-permute-start.38 = (bf16[96,1536]{1,0:T(8,128)(2,1)S(1)}, bf16[96,1536]{1,0:T(8,128)(2,1)S(1)}, u32[]{:S(2)}, u32[]{:S(2)}) collective-permute-start(bf16[96,1536]{1,0:T(8,128)(2,1)S(1)} %get-tuple-element.203), channel_id=1, source_target_pairs={{0,16},{8,24},{16,0},{24,8},{1,17},{9,25},{17,1},{25,9},{2,18},{10... | collective-permute-start | bytes 884744 | tf_op jit(solution)/shard_map/ppermute | solution.py:33
  162.2 25.0 %collective-permute-start.37 = (bf16[96,1536]{1,0:T(8,128)(2,1)S(1)}, bf16[96,1536]{1,0:T(8,128)(2,1)S(1)}, u32[]{:S(2)}, u32[]{:S(2)}) collective-permute-start(bf16[96,1536]{1,0:T(8,128)(2,1)S(1)} %get-tuple-element.204), channel_id=1, source_target_pairs={{0,8},{8,0},{16,24},{24,16},{1,9},{9,1},{17,25},{25,17},{2,10},{10... | collective-permute-start | bytes 884744 | tf_op jit(solution)/shard_map/ppermute | solution.py:33
  169.2 12.0 %collective-permute-start.33 = (bf16[4,96,640]{2,1,0:T(8,128)(2,1)S(1)}, bf16[4,96,640]{2,1,0:T(8,128)(2,1)S(1)}, u32[]{:S(2)}, u32[]{:S(2)}) collective-permute-start(bf16[4,96,640]{2,1,0:T(8,128)(2,1)S(1)} %get-tuple-element.152), channel_id=1, source_target_pairs={{0,1},{1,0},{2,3},{3,2},{4,5},{5,4},{6,7},{7,6},{8,9},{9,8},{10,11... | collective-permute-start | bytes 1474568 | tf_op jit(solution)/shard_map/ppermute | solution.py:33
  183.5 15.6 %collective-permute-start.30 = (bf16[256,768]{1,0:T(8,128)(2,1)S(1)}, bf16[256,768]{1,0:T(8,128)(2,1)S(1)}, u32[]{:S(2)}, u32[]{:S(2)}) collective-permute-start(bf16[256,768]{1,0:T(8,128)(2,1)S(1)} %get-tuple-element.196), channel_id=1, source_target_pairs={{0,4},{2,6},{4,0},{6,2},{1,5},{3,7},{5,1},{7,3},{8,12},{10,14},{12... | collective-permute-start | bytes 1179656 | tf_op jit(solution)/shard_map/ppermute | solution.py:33
  192.8 10.7 %collective-permute-start.36 = (bf16[112,832]{1,0:T(8,128)(2,1)S(1)}, bf16[112,832]{1,0:T(8,128)(2,1)S(1)}, u32[]{:S(2)}, u32[]{:S(2)}) collective-permute-start(bf16[112,832]{1,0:T(8,128)(2,1)S(1)} %get-tuple-element.224), channel_id=1, source_target_pairs={{0,24},{8,16},{16,8},{24,0},{1,25},{9,17},{17,9},{25,1},{2,26},{10... | collective-permute-start | bytes 559112 | tf_op jit(solution)/shard_map/ppermute | solution.py:33
  197.6 14.0 %collective-permute-start.35 = (bf16[112,832]{1,0:T(8,128)(2,1)S(1)}, bf16[112,832]{1,0:T(8,128)(2,1)S(1)}, u32[]{:S(2)}, u32[]{:S(2)}) collective-permute-start(bf16[112,832]{1,0:T(8,128)(2,1)S(1)} %get-tuple-element.226), channel_id=1, source_target_pairs={{0,16},{8,24},{16,0},{24,8},{1,17},{9,25},{17,1},{25,9},{2,18},{10... | collective-permute-start | bytes 559112 | tf_op jit(solution)/shard_map/ppermute | solution.py:33
  (41 other events, 356.5 us)

commit v5 on v4

--- a/solution.py
+++ b/solution.py
@@ -883,7 +883,7 @@
     small = small + swap(small, "seq", 1)
     ff_out, _ = scatter_batch(ff_own, ff_rest, None, small)
     small = jnp.concatenate([small[0:4] + swap(small[0:4], "heads", 2), small[4:8]])
-    qkv_own, qkv_rest = join_seq((w_keep, after(w_got, small)), (pj_keep, pj_got))
+    qkv_own, qkv_rest = join_seq((w_keep[..., : 3 * width], after(w_got, small)[..., : 3 * width]), (pj_keep, pj_got))
     cut = small.shape[1] // 2
     small = jnp.concatenate([small[:, :cut], small[:, cut:]])
     input_grad, _, _ = call(
@@ -892,7 +892,7 @@
         scal, dn_here, dn_far, x_own, middle_grad, norms, limit=6,
     )
     qkv_out, small = scatter_batch(qkv_own, qkv_rest, small, input_grad)
-    pj_out = qkv_out[:, 640:]
+    pj_out = qkv_out[:, 3 * width :]
     small = jnp.concatenate([small[:8], small[8:]], axis=1)
 
     qkv_out = jnp.stack(

time: 216 us -> 212 us (0.981)
  starting transfers between devices: 40.8 us -> 36.7 us
    ppermute x37, starting transfers between devices: 34 us -> 29.9 us  [swap(): lax.ppermute(shard, axis, [(i, i ^ by) for i in range(lax.axis_size(axis))])]
  transfers between devices with their start and end apart: 40 -> 40, of which waited for: 20 -> 19; matrix products, arithmetic and copies ran while one was open for 5% -> 5% of each run, Pallas kernels for 25% -> 26%
where the time goes in v5:
time: 212 us; the launch traced here: 210 us
  waiting for transfers between devices  84.2 us (40%)
  Pallas kernels  63.2 us (30%)
  starting transfers between devices  36.7 us (17%)
  local copies, waits for them, and re-layouts  15.2 us (7%)
  other arithmetic  9.73 us (5%)
    ppermute x37, waiting for transfers between devices, swap(): lax.ppermute(shard, axis, [(i, i ^ by) for i in range(lax.axis_size(axis))])  76.6 us
    pallas_call x15, Pallas kernels, call(): pl.pallas_call(body, out_shape=[jax.ShapeDtypeStruct(*o) for o in outs],...  63.2 us
    ppermute x37, starting transfers between devices, swap(): lax.ppermute(shard, axis, [(i, i ^ by) for i in range(lax.axis_size(axis))])  29.9 us
    unnamed x68, local copies, waits for them, and re-layouts  11.5 us
    ppermute x1, waiting for transfers between devices, on_device(): remote_in = lax.ppermute(remote, 'seq', [(1, 0)])  7.52 us
  transfers between devices with their start and end apart: 40, of which 19 were waited for; matrix products, arithmetic and copies ran while one was open for 5% of the time, Pallas kernels for 26%

profile of v5, /device:TPU:0, one launch (start us, length us, event | category | flops | bytes accessed | tf_op | source)
XLA Modules:
  0.0 210.3 jit_solution(832137537602400586)
XLA Ops:
  0.6 4.0 %collective-permute-start.2 = (bf16[256,768]{1,0:T(8,128)(2,1)}, bf16[256,768]{1,0:T(8,128)(2,1)S(1)}, u32[]{:S(2)}, u32[]{:S(2)}) collective-permute-start(bf16[256,768]{1,0:T(8,128)(2,1)} %bitcast.79), channel_id=1, source_target_pairs={{0,5},{1,4},{2,7},{3,6},{4,1},{5,0},{6,3},{7,2},{8,13},{9,12},{10,... | collective-permute-start | bytes 1179656 | tf_op jit(solution)/shard_map/ppermute | solution.py:743
  8.9 3.1 %collective-permute-start.3 = (bf16[96,896]{1,0:T(8,128)(2,1)S(1)}, bf16[96,896]{1,0:T(8,128)(2,1)S(1)}, u32[]{:S(2)}, u32[]{:S(2)}) collective-permute-start(bf16[96,896]{1,0:T(8,128)(2,1)S(1)} %shard_map.203), channel_id=1, source_target_pairs={{0,16},{8,24},{16,0},{24,8},{1,17},{9,25},{17,1},{25,9},{2,18},{10... | collective-permute-start | bytes 516104 | tf_op jit(solution)/shard_map/ppermute | solution.py:33
  11.9 7.2 %collective-permute-done.3 = bf16[96,896]{1,0:T(8,128)(2,1)S(1)} collective-permute-done((bf16[96,896]{1,0:T(8,128)(2,1)S(1)}, bf16[96,896]{1,0:T(8,128)(2,1)S(1)}, u32[]{:S(2)}, u32[]{:S(2)}) %collective-permute-start.3) | collective-permute-done | bytes 172064 | tf_op jit(solution)/shard_map/ppermute | solution.py:33
  20.0 2.7 %collective-permute-done.1 = bf16[256,768]{1,0:T(8,128)(2,1)S(1)} collective-permute-done((bf16[256,768]{1,0:T(8,128)(2,1)}, bf16[256,768]{1,0:T(8,128)(2,1)S(1)}, u32[]{:S(2)}, u32[]{:S(2)}) %collective-permute-start.1) | collective-permute-done | bytes 393248 | tf_op jit(solution)/shard_map/ppermute | solution.py:33
  24.9 3.3 %collective-permute-done.6 = bf16[192,896]{1,0:T(8,128)(2,1)S(1)} collective-permute-done((bf16[192,896]{1,0:T(8,128)(2,1)S(1)}, bf16[192,896]{1,0:T(8,128)(2,1)S(1)}, u32[]{:S(2)}, u32[]{:S(2)}) %collective-permute-start.6) | collective-permute-done | bytes 344096 | tf_op jit(solution)/shard_map/ppermute | solution.py:33
  30.8 4.5 %collective-permute-start.16 = (bf16[96,1536]{1,0:T(8,128)(2,1)}, bf16[96,1536]{1,0:T(8,128)(2,1)}, u32[]{:S(2)}, u32[]{:S(2)}) collective-permute-start(bf16[96,1536]{1,0:T(8,128)(2,1)} %pad_maximum_fusion.5), channel_id=1, source_target_pairs={{0,24},{8,16},{16,8},{24,0},{1,25},{9,17},{17,9},{25,1},{2,26},{10... | collective-permute-start | bytes 884744 | tf_op jit(solution)/shard_map/ppermute | solution.py:33
  36.0 3.7 %shard_map.204 = (f32[2048,768]{1,0:T(8,128)S(1)}, bf16[1024,768]{1,0:T(8,128)(2,1)S(1)}) custom-call(s32[8]{0:T(128)S(1)} %concatenate.48.scal, bf16[512,768]{1,0:T(8,128)(2,1)S(1)} %pad_maximum_fusion.2.refs_0_.refs_8_, bf16[512,768]{1,0:T(8,128)(2,1)S(1)} %collective-permute-done.4.refs_1_.refs_9_, ...), custom_call_target="tpu_custom_call" | custom-call | flops 98304 | tf_op jit(solution)/shard_map/pallas_call | solution.py:113
  40.9 3.3 %collective-permute-done.7.refs_2_ = bf16[4,96,896]{2,1,0:T(8,128)(2,1)} collective-permute-done((bf16[4,96,896]{2,1,0:T(8,128)(2,1)S(1)}, bf16[4,96,896]{2,1,0:T(8,128)(2,1)}, u32[]{:S(2)}, u32[]{:S(2)}) %collective-permute-start.7) | collective-permute-done | bytes 688160 | tf_op jit(solution)/shard_map/ppermute | solution.py:33
  45.3 9.2 %shard_map.205 = (bf16[1024,768]{1,0:T(8,128)(2,1)S(1)}, bf16[1040,768]{1,0:T(8,128)(2,1)S(1)}, bf16[768,768]{1,0:T(8,128)(2,1)S(1)}, bf16[1024,256]{1,0:T(8,128...) custom-call(s32[8]{0:T(128)S(1)} %concatenate.48.scal, ...), custom_call_target="tpu_custom_call" | custom-call | flops 113246208 | tf_op jit(solution)/shard_map/pallas_call | solution.py:113
  56.8 2.8 %collective-permute-done.15 = bf16[96,1536]{1,0:T(8,128)(2,1)} collective-permute-done((bf16[96,1536]{1,0:T(8,128)(2,1)}, bf16[96,1536]{1,0:T(8,128)(2,1)}, u32[]{:S(2)}, u32[]{:S(2)}) %collective-permute-start.15) | collective-permute-done | bytes 294944 | tf_op jit(solution)/shard_map/ppermute | solution.py:33
  63.1 8.0 %shard_map.206 = (bf16[1536,128]{1,0:T(8,128)(2,1)S(1)}, f32[192,1024]{1,0:T(8,128)S(1)}, f32[8,1024]{1,0:T(8,128)S(1)}) custom-call(s32[8]{0:T(128)S(1)} %concatenate.48.scal, bf16[1024,256]{1,0:T(8,128)(2,1)S(1)} %get-tuple-element.92.query.refs_0_, bf16[2048,256]{1,0:T(8,128)(2,1)S(1)} %get-tuple-element.93.key.refs_1_, ...), custom_call_target="tpu_custom_call" | custom-call | flops 50331648 | tf_op jit(solution)/shard_map/pallas_call | solution.py:113
  71.7 6.2 %collective-permute-done.12.refs_6_.refs_2_ = bf16[448,768]{1,0:T(8,128)(2,1)S(1)} collective-permute-done((bf16[448,768]{1,0:T(8,128)(2,1)S(1)}, bf16[448,768]{1,0:T(8,128)(2,1)S(1)}, u32[]{:S(2)}, u32[]{:S(2)}) %collective-permute-start.12) | collective-permute-done | bytes 688160 | tf_op jit(solution)/shard_map/ppermute | solution.py:33
  78.4 6.1 %collective-permute-done.9.refs_2_ = bf16[1536,128]{1,0:T(8,128)(2,1)S(1)} collective-permute-done((bf16[1536,128]{1,0:T(8,128)(2,1)S(1)}, bf16[1536,128]{1,0:T(8,128)(2,1)S(1)}, u32[]{:S(2)}, u32[]{:S(2)}) %collective-permute-start.9) | collective-permute-done | bytes 393248 | tf_op jit(solution)/shard_map/ppermute | solution.py:33
  84.5 4.8 %collective-permute-done.17.refs_1_ = bf16[4,96,1536]{2,1,0:T(8,128)(2,1)S(1)} collective-permute-done((bf16[4,96,1536]{2,1,0:T(8,128)(2,1)S(1)}, bf16[4,96,1536]{2,1,0:T(8,128)(2,1)S(1)}, u32[]{:S(2)}, u32[]{:S(2)}) %collective-permute-start.17) | collective-permute-done | bytes 1179680 | tf_op jit(solution)/shard_map/ppermute | solution.py:33
  90.0 8.6 %shard_map.208 = (bf16[1024,768]{1,0:T(8,128)(2,1)S(1)}, bf16[1024,768]{1,0:T(8,128)(2,1)S(1)}, bf16[1024,768]{1,0:T(8,128)(2,1)S(1)}, f32[512,768]{1,0:T(8,128)...) custom-call(s32[8]{0:T(128)S(1)} %concatenate.48.scal, bf16[1536,128]{1,0:T(8,128)(2,1)S(1)} %get-tuple-element.95.refs_0_, ...), custom_call_target="tpu_custom_call" | custom-call | flops 301989888 | tf_op jit(solution)/shard_map/pallas_call | solution.py:113
  101.8 4.6 %shard_map.210 = (f32[512,768]{1,0:T(8,128)S(1)}, bf16[512,768]{1,0:T(8,128)(2,1)}, bf16[4,96,1536]{2,1,0:T(8,128)(2,1)S(1)}, bf16[4,96,1536]{2,1,0:T(8,128)(2,1)}) custom-call(s32[8]{0:T(128)S(1)} %concatenate.48.scal, bf16[1024,768]{1,0:T(8,128)(2,1)S(1)} %get-tuple-element.112.refs_0_, bf16[1024,768]{1,0:T(8,128)(2,1)S(1)} %get-tuple-element.110.refs_4_.refs_1_, ...), custom_call_target="tpu_custom_call" | custom-call | flops 150994944 | tf_op jit(solution)/shard_map/pallas_call | solution.py:113
  107.9 4.6 %collective-permute-done.19.got = bf16[256,768]{1,0:T(8,128)(2,1)S(1)} collective-permute-done((bf16[256,768]{1,0:T(8,128)(2,1)S(1)}, bf16[256,768]{1,0:T(8,128)(2,1)S(1)}, u32[]{:S(2)}, u32[]{:S(2)}) %collective-permute-start.19) | collective-permute-done | bytes 393248 | tf_op jit(solution)/shard_map/ppermute | solution.py:33
  116.3 9.8 %collective-permute-done.22.refs_2_ = bf16[256,768]{1,0:T(8,128)(2,1)} collective-permute-done((bf16[256,768]{1,0:T(8,128)(2,1)}, bf16[256,768]{1,0:T(8,128)(2,1)}, u32[]{:S(2)}, u32[]{:S(2)}) %collective-permute-start.22) | collective-permute-done | bytes 393248 | tf_op jit(solution)/shard_map/ppermute | solution.py:33
  129.3 2.8 %shard_map.212 = (bf16[1024,256]{1,0:T(8,128)(2,1)S(1)}, f32[8,1024]{1,0:T(8,128)S(1)}, f32[4,96,192]{2,1,0:T(8,128)S(1)}, bf16[4,96,192]{2,1,0:T(8,128)(2,1)S(1)}) custom-call(s32[8]{0:T(128)S(1)} %concatenate.48.scal, bf16[256,768]{1,0:T(8,128)(2,1)} %get-tuple-element.118.refs_0_, bf16[256,768]{1,0:T(8,128)(2,1)} %collective-permute-done.21.refs_1_, ...), custom_call_target="tpu_custom_call" | custom-call | flops 37748736 | tf_op jit(solution)/shard_map/pallas_call | solution.py:113
  134.3 2.2 %shard_map.213 = (bf16[1024,384]{1,0:T(8,128)(2,1)S(1)}, f32[192,1024]{1,0:T(8,128)S(1)}, bf16[192,2048]{1,0:T(8,128)(2,1)S(1)}) custom-call(s32[8]{0:T(128)S(1)} %concatenate.48.scal, bf16[1024,256]{1,0:T(8,128)(2,1)S(1)} %get-tuple-element.92.query.refs_0_, bf16[2048,256]{1,0:T(8,128)(2,1)S(1)} %get-tuple-element.93.key.refs_1_, ...), custom_call_target="tpu_custom_call" | custom-call | flops 125829120 | tf_op jit(solution)/shard_map/pallas_call | solution.py:113
  139.6 9.3 %shard_map.214 = (bf16[1024,256]{1,0:T(8,128)(2,1)S(1)}, bf16[1024,256]{1,0:T(8,128)(2,1)S(1)}, bf16[1024,256]{1,0:T(8,128)(2,1)S(1)}, f32[8,768]{1,0:T(8,128)S(1)}) custom-call(s32[8]{0:T(128)S(1)} %concatenate.48.scal, bf16[1024,256]{1,0:T(8,128)(2,1)S(1)} %get-tuple-element.92.query.refs_0_, bf16[2048,256]{1,0:T(8,128)(2,1)S(1)} %get-tuple-element.93.key.refs_1_, ...), custom_call_target="tpu_custom_call" | custom-call | flops 125829120 | tf_op jit(solution)/shard_map/pallas_call | solution.py:113
  152.4 2.3 %collective-permute-start.39 = (bf16[96,1536]{1,0:T(8,128)(2,1)S(1)}, bf16[96,1536]{1,0:T(8,128)(2,1)S(1)}, u32[]{:S(2)}, u32[]{:S(2)}) collective-permute-start(bf16[96,1536]{1,0:T(8,128)(2,1)S(1)} %get-tuple-element.202), channel_id=1, source_target_pairs={{0,24},{8,16},{16,8},{24,0},{1,25},{9,17},{17,9},{25,1},{2,26},{10... | collective-permute-start | bytes 884744 | tf_op jit(solution)/shard_map/ppermute | solution.py:33
  154.7 7.5 %collective-permute-done.27.refs_3_ = bf16[1024,384]{1,0:T(8,128)(2,1)S(1)} collective-permute-done((bf16[1024,384]{1,0:T(8,128)(2,1)S(1)}, bf16[1024,384]{1,0:T(8,128)(2,1)S(1)}, u32[]{:S(2)}, u32[]{:S(2)}) %collective-permute-start.27) | collective-permute-done | bytes 786464 | tf_op jit(solution)/shard_map/ppermute | solution.py:845
  162.2 2.2 %collective-permute-start.37 = (bf16[96,1536]{1,0:T(8,128)(2,1)S(1)}, bf16[96,1536]{1,0:T(8,128)(2,1)S(1)}, u32[]{:S(2)}, u32[]{:S(2)}) collective-permute-start(bf16[96,1536]{1,0:T(8,128)(2,1)S(1)} %get-tuple-element.204), channel_id=1, source_target_pairs={{0,8},{8,0},{16,24},{24,16},{1,9},{9,1},{17,25},{25,17},{2,10},{10... | collective-permute-start | bytes 884744 | tf_op jit(solution)/shard_map/ppermute | solution.py:33
  164.4 5.4 %shard_map.215 = (bf16[1024,768]{1,0:T(8,128)(2,1)S(1)}, f32[4,96,640]{2,1,0:T(8,128)S(1)}, bf16[4,96,640]{2,1,0:T(8,128)(2,1)S(1)}, f32[8,768]{1,0:T(8,128)S(1)}) custom-call(s32[8]{0:T(128)S(1)} %concatenate.48.scal, bf16[1024,256]{1,0:T(8,128)(2,1)S(1)} %get-tuple-element.133.refs_0_, bf16[1024,256]{1,0:T(8,128)(2,1)S(1)} %get-tuple-element.135.refs_1_, ...), custom_call_target="tpu_custom_call" | custom-call | flops 56623104 | tf_op jit(solution)/shard_map/pallas_call | solution.py:113
  170.0 2.1 shard_map.216
  174.1 7.4 %collective-permute-done.33 = bf16[4,96,640]{2,1,0:T(8,128)(2,1)S(1)} collective-permute-done((bf16[4,96,640]{2,1,0:T(8,128)(2,1)S(1)}, bf16[4,96,640]{2,1,0:T(8,128)(2,1)S(1)}, u32[]{:S(2)}, u32[]{:S(2)}) %collective-permute-start.33) | collective-permute-done | bytes 491552 | tf_op jit(solution)/shard_map/ppermute | solution.py:33
  183.4 2.2 %collective-permute-done.31 = f32[8,768]{1,0:T(8,128)S(1)} collective-permute-done((f32[8,768]{1,0:T(8,128)S(1)}, f32[8,768]{1,0:T(8,128)S(1)}, u32[]{:S(2)}, u32[]{:S(2)}) %collective-permute-start.31) | collective-permute-done | bytes 24608 | tf_op jit(solution)/shard_map/ppermute | solution.py:33
  187.0 4.2 %collective-permute-done.32 = f32[4,768]{1,0:T(4,128)S(1)} collective-permute-done((f32[4,768]{1,0:T(4,128)S(1)}, f32[4,768]{1,0:T(4,128)S(1)}, u32[]{:S(2)}, u32[]{:S(2)}) %collective-permute-start.32) | collective-permute-done | bytes 12320 | tf_op jit(solution)/shard_map/ppermute | solution.py:33
  192.8 3.0 %collective-permute-start.35 = (bf16[112,768]{1,0:T(8,128)(2,1)S(1)}, bf16[112,768]{1,0:T(8,128)(2,1)S(1)}, u32[]{:S(2)}, u32[]{:S(2)}) collective-permute-start(bf16[112,768]{1,0:T(8,128)(2,1)S(1)} %get-tuple-element.226), channel_id=1, source_target_pairs={{0,16},{8,24},{16,0},{24,8},{1,17},{9,25},{17,1},{25,9},{2,18},{10... | collective-permute-start | bytes 516104 | tf_op jit(solution)/shard_map/ppermute | solution.py:33
  196.6 2.2 %shard_map.217 = (f32[256,768]{1,0:T(8,128)}, bf16[256,768]{1,0:T(8,128)(2,1)}, f32[8,768]{1,0:T(8,128)}) custom-call(s32[8]{0:T(128)S(1)} %concatenate.48.scal, f32[256,768]{1,0:T(8,128)S(1)} %get-tuple-element.197.part, bf16[256,768]{1,0:T(8,128)(2,1)S(1)} %collective-permute-done.30.got, bf16[256,768]{1,0:T(8,128)(2,1)S(1)} %bitcast.83, ...), custom_call_target="tpu_custom_call" | custom-call | tf_op jit(solution)/shard_map/pallas_call | solution.py:113
  200.0 6.7 %collective-permute-done.35 = bf16[112,768]{1,0:T(8,128)(2,1)S(1)} collective-permute-done((bf16[112,768]{1,0:T(8,128)(2,1)S(1)}, bf16[112,768]{1,0:T(8,128)(2,1)S(1)}, u32[]{:S(2)}, u32[]{:S(2)}) %collective-permute-start.35) | collective-permute-done | bytes 172064 | tf_op jit(solution)/shard_map/ppermute | solution.py:33
  (181 shorter events, 53.1 us)
Async XLA Ops:
  0.6 19.3 %collective-permute-start.2 = (bf16[256,768]{1,0:T(8,128)(2,1)}, bf16[256,768]{1,0:T(8,128)(2,1)S(1)}, u32[]{:S(2)}, u32[]{:S(2)}) collective-permute-start(bf16[256,768]{1,0:T(8,128)(2,1)} %bitcast.79), channel_id=1, source_target_pairs={{0,5},{1,4},{2,7},{3,6},{4,1},{5,0},{6,3},{7,2},{8,13},{9,12},{10,... | collective-permute-start | bytes 1179656 | tf_op jit(solution)/shard_map/ppermute | solution.py:743
  4.6 18.0 %collective-permute-start.1 = (bf16[256,768]{1,0:T(8,128)(2,1)}, bf16[256,768]{1,0:T(8,128)(2,1)S(1)}, u32[]{:S(2)}, u32[]{:S(2)}) collective-permute-start(bf16[256,768]{1,0:T(8,128)(2,1)} %bitcast.80), channel_id=1, source_target_pairs={{0,4},{2,6},{4,0},{6,2},{1,5},{3,7},{5,1},{7,3},{8,12},{10,14},{12... | collective-permute-start | bytes 1179656 | tf_op jit(solution)/shard_map/ppermute | solution.py:33
  5.2 17.5 %collective-permute-start = (bf16[256,768]{1,0:T(8,128)(2,1)}, bf16[256,768]{1,0:T(8,128)(2,1)S(1)}, u32[]{:S(2)}, u32[]{:S(2)}) collective-permute-start(bf16[256,768]{1,0:T(8,128)(2,1)} %bitcast.81), channel_id=1, source_target_pairs={{0,1},{1,0},{2,3},{3,2},{4,5},{5,4},{6,7},{7,6},{8,9},{9,8},{10,11... | collective-permute-start | bytes 1179656 | tf_op jit(solution)/shard_map/ppermute | solution.py:33
  8.9 10.3 %collective-permute-start.3 = (bf16[96,896]{1,0:T(8,128)(2,1)S(1)}, bf16[96,896]{1,0:T(8,128)(2,1)S(1)}, u32[]{:S(2)}, u32[]{:S(2)}) collective-permute-start(bf16[96,896]{1,0:T(8,128)(2,1)S(1)} %shard_map.203), channel_id=1, source_target_pairs={{0,16},{8,24},{16,0},{24,8},{1,17},{9,25},{17,1},{25,9},{2,18},{10... | collective-permute-start | bytes 516104 | tf_op jit(solution)/shard_map/ppermute | solution.py:33
  19.2 9.0 %collective-permute-start.6 = (bf16[192,896]{1,0:T(8,128)(2,1)S(1)}, bf16[192,896]{1,0:T(8,128)(2,1)S(1)}, u32[]{:S(2)}, u32[]{:S(2)}) collective-permute-start(bf16[192,896]{1,0:T(8,128)(2,1)S(1)} %pad_maximum_fusion.4), channel_id=1, source_target_pairs={{0,8},{8,0},{16,24},{24,16},{1,9},{9,1},{17,25},{25,17},{2,10},{10... | collective-permute-start | bytes 1032200 | tf_op jit(solution)/shard_map/ppermute | solution.py:33
  24.2 11.0 %collective-permute-start.5 = (bf16[512,768]{1,0:T(8,128)(2,1)}, bf16[512,768]{1,0:T(8,128)(2,1)}, u32[]{:S(2)}, u32[]{:S(2)}) collective-permute-start(bf16[512,768]{1,0:T(8,128)(2,1)} %constant_dynamic-update-slice_fusion.refs_2_), channel_id=1, source_target_pairs={{0,2},{2,0},{4,6},{6,4},{1,3},{3,1},{5,7},{7,5},{8,10},{10,8},{12,... | collective-permute-start | bytes 2359304 | tf_op jit(solution)/shard_map/ppermute | solution.py:33
  24.3 11.7 %collective-permute-start.4 = (bf16[512,768]{1,0:T(8,128)(2,1)S(1)}, bf16[512,768]{1,0:T(8,128)(2,1)S(1)}, u32[]{:S(2)}, u32[]{:S(2)}) collective-permute-start(bf16[512,768]{1,0:T(8,128)(2,1)S(1)} %pad_maximum_fusion.2.refs_0_.refs_8_), channel_id=1, source_target_pairs={{0,2},{2,0},{4,6},{6,4},{1,3},{3,1},{5,7},{7,5},{8,10},{10,8},{12,... | collective-permute-start | bytes 2359304 | tf_op jit(solution)/shard_map/ppermute | solution.py:33
  28.3 15.9 %collective-permute-start.7 = (bf16[4,96,896]{2,1,0:T(8,128)(2,1)S(1)}, bf16[4,96,896]{2,1,0:T(8,128)(2,1)}, u32[]{:S(2)}, u32[]{:S(2)}) collective-permute-start(bf16[4,96,896]{2,1,0:T(8,128)(2,1)S(1)} %pad_maximum_fusion.3.refs_1_), channel_id=1, source_target_pairs={{0,1},{1,0},{2,3},{3,2},{4,5},{5,4},{6,7},{7,6},{8,9},{9,8},{10,11... | collective-permute-start | bytes 2064392 | tf_op jit(solution)/shard_map/ppermute | solution.py:33
  30.8 26.1 %collective-permute-start.16 = (bf16[96,1536]{1,0:T(8,128)(2,1)}, bf16[96,1536]{1,0:T(8,128)(2,1)}, u32[]{:S(2)}, u32[]{:S(2)}) collective-permute-start(bf16[96,1536]{1,0:T(8,128)(2,1)} %pad_maximum_fusion.5), channel_id=1, source_target_pairs={{0,24},{8,16},{16,8},{24,0},{1,25},{9,17},{17,9},{25,1},{2,26},{10... | collective-permute-start | bytes 884744 | tf_op jit(solution)/shard_map/ppermute | solution.py:33
  35.2 24.4 %collective-permute-start.15 = (bf16[96,1536]{1,0:T(8,128)(2,1)}, bf16[96,1536]{1,0:T(8,128)(2,1)}, u32[]{:S(2)}, u32[]{:S(2)}) collective-permute-start(bf16[96,1536]{1,0:T(8,128)(2,1)} %pad_maximum_fusion.5), channel_id=1, source_target_pairs={{0,16},{8,24},{16,0},{24,8},{1,17},{9,25},{17,1},{25,9},{2,18},{10... | collective-permute-start | bytes 884744 | tf_op jit(solution)/shard_map/ppermute | solution.py:33
  35.2 24.4 %collective-permute-start.14 = (bf16[96,1536]{1,0:T(8,128)(2,1)}, bf16[96,1536]{1,0:T(8,128)(2,1)}, u32[]{:S(2)}, u32[]{:S(2)}) collective-permute-start(bf16[96,1536]{1,0:T(8,128)(2,1)} %pad_maximum_fusion.5), channel_id=1, source_target_pairs={{0,8},{8,0},{16,24},{24,16},{1,9},{9,1},{17,25},{25,17},{2,10},{10... | collective-permute-start | bytes 884744 | tf_op jit(solution)/shard_map/ppermute | solution.py:33
  59.6 18.3 %collective-permute-start.12 = (bf16[448,768]{1,0:T(8,128)(2,1)S(1)}, bf16[448,768]{1,0:T(8,128)(2,1)S(1)}, u32[]{:S(2)}, u32[]{:S(2)}) collective-permute-start(bf16[448,768]{1,0:T(8,128)(2,1)S(1)} %get-tuple-element.96.refs_4_.refs_0_), channel_id=1, source_target_pairs={{0,4},{2,6},{4,0},{6,2},{1,5},{3,7},{5,1},{7,3},{8,12},{10,14},{12... | collective-permute-start | bytes 2064392 | tf_op jit(solution)/shard_map/ppermute | solution.py:33
  62.5 26.8 %collective-permute-start.17 = (bf16[4,96,1536]{2,1,0:T(8,128)(2,1)S(1)}, bf16[4,96,1536]{2,1,0:T(8,128)(2,1)S(1)}, u32[]{:S(2)}, u32[]{:S(2)}) collective-permute-start(bf16[4,96,1536]{2,1,0:T(8,128)(2,1)S(1)} %pad_maximum_fusion.1.refs_0_), channel_id=1, source_target_pairs={{0,1},{1,0},{2,3},{3,2},{4,5},{5,4},{6,7},{7,6},{8,9},{9,8},{10,11... | collective-permute-start | bytes 3538952 | tf_op jit(solution)/shard_map/ppermute | solution.py:33
  71.1 13.4 %collective-permute-start.9 = (bf16[1536,128]{1,0:T(8,128)(2,1)S(1)}, bf16[1536,128]{1,0:T(8,128)(2,1)S(1)}, u32[]{:S(2)}, u32[]{:S(2)}) collective-permute-start(bf16[1536,128]{1,0:T(8,128)(2,1)S(1)} %get-tuple-element.95.refs_0_), channel_id=1, source_target_pairs={{0,4},{2,6},{4,0},{6,2},{1,5},{3,7},{5,1},{7,3},{8,12},{10,14},{12... | collective-permute-start | bytes 1179656 | tf_op jit(solution)/shard_map/ppermute | solution.py:33
  71.7 18.3 %collective-permute-start.11 = (bf16[448,768]{1,0:T(8,128)(2,1)S(1)}, bf16[448,768]{1,0:T(8,128)(2,1)S(1)}, u32[]{:S(2)}, u32[]{:S(2)}) collective-permute-start(bf16[448,768]{1,0:T(8,128)(2,1)S(1)} %get-tuple-element.96.refs_4_.refs_0_), channel_id=1, source_target_pairs={{0,2},{2,0},{4,6},{6,4},{1,3},{3,1},{5,7},{7,5},{8,10},{10,8},{12,... | collective-permute-start | bytes 2064392 | tf_op jit(solution)/shard_map/ppermute | solution.py:33
  77.9 12.1 %collective-permute-start.13 = (bf16[448,768]{1,0:T(8,128)(2,1)S(1)}, bf16[448,768]{1,0:T(8,128)(2,1)S(1)}, u32[]{:S(2)}, u32[]{:S(2)}) collective-permute-start(bf16[448,768]{1,0:T(8,128)(2,1)S(1)} %collective-permute-done.12.refs_6_.refs_2_), channel_id=1, source_target_pairs={{0,2},{2,0},{4,6},{6,4},{1,3},{3,1},{5,7},{7,5},{8,10},{10,8},{12,... | collective-permute-start | bytes 2064392 | tf_op jit(solution)/shard_map/ppermute | solution.py:33
  77.9 12.1 %collective-permute-start.8 = (bf16[1536,128]{1,0:T(8,128)(2,1)S(1)}, bf16[1536,128]{1,0:T(8,128)(2,1)S(1)}, u32[]{:S(2)}, u32[]{:S(2)}) collective-permute-start(bf16[1536,128]{1,0:T(8,128)(2,1)S(1)} %get-tuple-element.95.refs_0_), channel_id=1, source_target_pairs={{0,2},{2,0},{4,6},{6,4},{1,3},{3,1},{5,7},{7,5},{8,10},{10,8},{12,... | collective-permute-start | bytes 1179656 | tf_op jit(solution)/shard_map/ppermute | solution.py:33
  101.2 11.3 %collective-permute-start.19 = (bf16[256,768]{1,0:T(8,128)(2,1)S(1)}, bf16[256,768]{1,0:T(8,128)(2,1)S(1)}, u32[]{:S(2)}, u32[]{:S(2)}) collective-permute-start(bf16[256,768]{1,0:T(8,128)(2,1)S(1)} %get-tuple-element.200), channel_id=1, source_target_pairs={{0,4},{2,6},{4,0},{6,2},{1,5},{3,7},{5,1},{7,3},{8,12},{10,14},{12... | collective-permute-start | bytes 1179656 | tf_op jit(solution)/shard_map/ppermute | solution.py:33
  107.4 30.5 %collective-permute-start.25 = (bf16[4,96,1536]{2,1,0:T(8,128)(2,1)}, bf16[4,96,1536]{2,1,0:T(8,128)(2,1)}, u32[]{:S(2)}, u32[]{:S(2)}) collective-permute-start(bf16[4,96,1536]{2,1,0:T(8,128)(2,1)} %get-tuple-element.127), channel_id=1, source_target_pairs={{0,1},{1,0},{2,3},{3,2},{4,5},{5,4},{6,7},{7,6},{8,9},{9,8},{10,11... | collective-permute-start | bytes 3538952 | tf_op jit(solution)/shard_map/ppermute | solution.py:33
  115.3 10.8 %collective-permute-start.22 = (bf16[256,768]{1,0:T(8,128)(2,1)}, bf16[256,768]{1,0:T(8,128)(2,1)}, u32[]{:S(2)}, u32[]{:S(2)}) collective-permute-start(bf16[256,768]{1,0:T(8,128)(2,1)} %get-tuple-element.118.refs_0_), channel_id=1, source_target_pairs={{0,4},{2,6},{4,0},{6,2},{1,5},{3,7},{5,1},{7,3},{8,12},{10,14},{12... | collective-permute-start | bytes 1179656 | tf_op jit(solution)/shard_map/ppermute | solution.py:33
  115.8 16.9 %collective-permute-start.20 = (bf16[512,768]{1,0:T(8,128)(2,1)}, bf16[512,768]{1,0:T(8,128)(2,1)}, u32[]{:S(2)}, u32[]{:S(2)}) collective-permute-start(bf16[512,768]{1,0:T(8,128)(2,1)} %get-tuple-element.119), channel_id=1, source_target_pairs={{0,2},{2,0},{4,6},{6,4},{1,3},{3,1},{5,7},{7,5},{8,10},{10,8},{12,... | collective-permute-start | bytes 2359304 | tf_op jit(solution)/shard_map/ppermute | solution.py:33
  115.8 10.3 %collective-permute-start.21 = (bf16[256,768]{1,0:T(8,128)(2,1)}, bf16[256,768]{1,0:T(8,128)(2,1)}, u32[]{:S(2)}, u32[]{:S(2)}) collective-permute-start(bf16[256,768]{1,0:T(8,128)(2,1)} %get-tuple-element.118.refs_0_), channel_id=1, source_target_pairs={{0,2},{2,0},{4,6},{6,4},{1,3},{3,1},{5,7},{7,5},{8,10},{10,8},{12,... | collective-permute-start | bytes 1179656 | tf_op jit(solution)/shard_map/ppermute | solution.py:33
  133.8 36.1 %collective-permute-start.24 = (bf16[256,768]{1,0:T(8,128)(2,1)S(1)}, bf16[256,768]{1,0:T(8,128)(2,1)S(1)}, u32[]{:S(2)}, u32[]{:S(2)}) collective-permute-start(bf16[256,768]{1,0:T(8,128)(2,1)S(1)} %add_convert_fusion.2), channel_id=1, source_target_pairs={{0,4},{2,6},{4,0},{6,2},{1,5},{3,7},{5,1},{7,3},{8,12},{10,14},{12... | collective-permute-start | bytes 1179656 | tf_op jit(solution)/shard_map/ppermute | solution.py:33
  136.5 25.7 %collective-permute-start.27 = (bf16[1024,384]{1,0:T(8,128)(2,1)S(1)}, bf16[1024,384]{1,0:T(8,128)(2,1)S(1)}, u32[]{:S(2)}, u32[]{:S(2)}) collective-permute-start(bf16[1024,384]{1,0:T(8,128)(2,1)S(1)} %get-tuple-element.129), channel_id=1, source_target_pairs={{1,0},{3,2},{5,4},{7,6},{9,8},{11,10},{13,12},{15,14},{17,16},{19,... | collective-permute-start | bytes 2359304 | tf_op jit(solution)/shard_map/ppermute | solution.py:845
  148.9 15.4 %collective-permute-start.28 = (f32[8,768]{1,0:T(8,128)S(1)}, f32[8,768]{1,0:T(8,128)S(1)}, u32[]{:S(2)}, u32[]{:S(2)}) collective-permute-start(f32[8,768]{1,0:T(8,128)S(1)} %get-tuple-element.138), channel_id=1, source_target_pairs={{1,0},{3,2},{5,4},{7,6},{9,8},{11,10},{13,12},{15,14},{17,16},{19,... | collective-permute-start | bytes 73736 | tf_op jit(solution)/shard_map/ppermute | solution.py:859
  152.4 34.5 %collective-permute-start.39 = (bf16[96,1536]{1,0:T(8,128)(2,1)S(1)}, bf16[96,1536]{1,0:T(8,128)(2,1)S(1)}, u32[]{:S(2)}, u32[]{:S(2)}) collective-permute-start(bf16[96,1536]{1,0:T(8,128)(2,1)S(1)} %get-tuple-element.202), channel_id=1, source_target_pairs={{0,24},{8,16},{16,8},{24,0},{1,25},{9,17},{17,9},{25,1},{2,26},{10... | collective-permute-start | bytes 884744 | tf_op jit(solution)/shard_map/ppermute | solution.py:33
  154.7 32.2 %collective-permute-start.38 = (bf16[96,1536]{1,0:T(8,128)(2,1)S(1)}, bf16[96,1536]{1,0:T(8,128)(2,1)S(1)}, u32[]{:S(2)}, u32[]{:S(2)}) collective-permute-start(bf16[96,1536]{1,0:T(8,128)(2,1)S(1)} %get-tuple-element.203), channel_id=1, source_target_pairs={{0,16},{8,24},{16,0},{24,8},{1,17},{9,25},{17,1},{25,9},{2,18},{10... | collective-permute-start | bytes 884744 | tf_op jit(solution)/shard_map/ppermute | solution.py:33
  162.2 24.7 %collective-permute-start.37 = (bf16[96,1536]{1,0:T(8,128)(2,1)S(1)}, bf16[96,1536]{1,0:T(8,128)(2,1)S(1)}, u32[]{:S(2)}, u32[]{:S(2)}) collective-permute-start(bf16[96,1536]{1,0:T(8,128)(2,1)S(1)} %get-tuple-element.204), channel_id=1, source_target_pairs={{0,8},{8,0},{16,24},{24,16},{1,9},{9,1},{17,25},{25,17},{2,10},{10... | collective-permute-start | bytes 884744 | tf_op jit(solution)/shard_map/ppermute | solution.py:33
  169.8 11.6 %collective-permute-start.33 = (bf16[4,96,640]{2,1,0:T(8,128)(2,1)S(1)}, bf16[4,96,640]{2,1,0:T(8,128)(2,1)S(1)}, u32[]{:S(2)}, u32[]{:S(2)}) collective-permute-start(bf16[4,96,640]{2,1,0:T(8,128)(2,1)S(1)} %get-tuple-element.152), channel_id=1, source_target_pairs={{0,1},{1,0},{2,3},{3,2},{4,5},{5,4},{6,7},{7,6},{8,9},{9,8},{10,11... | collective-permute-start | bytes 1474568 | tf_op jit(solution)/shard_map/ppermute | solution.py:33
  172.0 9.7 %collective-permute-start.29 = (bf16[520,768]{1,0:T(8,128)(2,1)S(1)}, bf16[520,768]{1,0:T(8,128)(2,1)S(1)}, u32[]{:S(2)}, u32[]{:S(2)}) collective-permute-start(bf16[520,768]{1,0:T(8,128)(2,1)S(1)} %get-tuple-element.146), channel_id=1, source_target_pairs={{0,2},{2,0},{4,6},{6,4},{1,3},{3,1},{5,7},{7,5},{8,10},{10,8},{12,... | collective-permute-start | bytes 2396168 | tf_op jit(solution)/shard_map/ppermute | solution.py:33
  182.3 14.3 %collective-permute-start.30 = (bf16[256,768]{1,0:T(8,128)(2,1)S(1)}, bf16[256,768]{1,0:T(8,128)(2,1)S(1)}, u32[]{:S(2)}, u32[]{:S(2)}) collective-permute-start(bf16[256,768]{1,0:T(8,128)(2,1)S(1)} %get-tuple-element.196), channel_id=1, source_target_pairs={{0,4},{2,6},{4,0},{6,2},{1,5},{3,7},{5,1},{7,3},{8,12},{10,14},{12... | collective-permute-start | bytes 1179656 | tf_op jit(solution)/shard_map/ppermute | solution.py:33
  192.8 14.0 %collective-permute-start.35 = (bf16[112,768]{1,0:T(8,128)(2,1)S(1)}, bf16[112,768]{1,0:T(8,128)(2,1)S(1)}, u32[]{:S(2)}, u32[]{:S(2)}) collective-permute-start(bf16[112,768]{1,0:T(8,128)(2,1)S(1)} %get-tuple-element.226), channel_id=1, source_target_pairs={{0,16},{8,24},{16,0},{24,8},{1,17},{9,25},{17,1},{25,9},{2,18},{10... | collective-permute-start | bytes 516104 | tf_op jit(solution)/shard_map/ppermute | solution.py:33
  (41 other events, 309.6 us)

commit v6 on v3

--- a/solution.py
+++ b/solution.py
@@ -813,6 +813,7 @@
         scratch=[pltpu.VMEM((width, model), f32), pltpu.VMEM((model, width), f32)],
         flops=4 * half * model * width, limit=6,
     )
+    pj_got = scatter_seq(pj_send)
     out_here, out_far = scatter_far(out_keep, after(out_got, dout), quarter)
     remote, query_t, kt = call(
         functools.partial(remote_back_body, half, heads),
@@ -825,12 +826,13 @@
         flops=10 * half * half * width, limit=8,
     )
     remote_in = lax.ppermute(remote, "seq", [(1, 0)])
-    ff_own, ff_rest = join_seq((ff_keep, after(ff_got, remote)))
+    ff_got, pj_got = after((ff_got, pj_got), remote)
+    ff_own, ff_rest = join_seq((ff_keep, ff_got))
 
     dq, dk, dv, front = call(
         functools.partial(local_back_body, half, heads),
         [((half, PADW), b16), ((half, PADW), b16), ((half, PADW), b16), ((8, 3 * PADW), f32)],
-        scal, query, key, value, dout, lse, row_dot, kt, after(query_t, ff_rest), taps,
+        scal, query, key, value, dout, lse, row_dot, kt, after(query_t, ff_rest, pj_got), taps,
         scratch=[
             pltpu.VMEM((heads, half, PADW), b16), pltpu.VMEM((heads, half, PADW), b16),
             pltpu.VMEM((KB, PADW), f32), pltpu.VMEM((KB, PADW), f32), pltpu.VMEM((width, half), f32),
@@ -838,9 +840,7 @@
         flops=10 * half * half * width, limit=8,
     )
     front_in = lax.ppermute(front, "seq", [(1, 0)])
-    pj_got = scatter_seq(after(pj_send, ff_rest))
     remote_in = after(remote_in, dq)
-    front_in = after(front_in, pj_got)
     block_output = (middle_own + out_here + after(out_far, dq).astype(f32)).astype(b16)
 
     proj_grad, w_keep, w_send, sums_taps = call(
@@ -865,17 +865,19 @@
     small = jnp.concatenate([small[0:4], sums_taps[4:8]])
     small = small + swap(small, "seq", 1)
     ff_out, _ = scatter_batch(ff_own, ff_rest, None, small)
+    small = jnp.concatenate([small[0:4] + swap(small[0:4], "heads", 2), small[4:8]])
+    qkv_own, qkv_rest = join_seq((w_keep[..., : 3 * width], after(w_got, small)[..., : 3 * width]), (pj_keep, pj_got))
     cut = small.shape[1] // 2
     small = jnp.concatenate([small[:, :cut], small[:, cut:]])
-    qkv_own, qkv_rest = join_seq((w_keep, w_got), (pj_keep, pj_got))
-    qkv_out, small = scatter_batch(qkv_own, qkv_rest, small)
-    pj_out = qkv_out[:, 640:]
-    small = jnp.concatenate([small[:8], small[8:]], axis=1)
     input_grad, _, _ = call(
         functools.partial(norm_back_body, 0),
         [((quarter, model), f32), ((quarter, model), b16), ((8, model), f32)],
         scal, dn_here, dn_far, x_own, middle_grad, norms, limit=6,
     )
+    qkv_out, small = scatter_batch(qkv_own, qkv_rest, small, input_grad)
+    pj_out = qkv_out[:, 3 * width :]
+    small = jnp.concatenate([small[:8], small[8:]], axis=1)
+
     qkv_out = jnp.stack(
         [
             jnp.concatenate([qkv_out[:, 0:128], qkv_out[:, 384:448]], axis=1),
@@ -885,7 +887,6 @@
         axis=1,
     )
     gains = lax.dynamic_slice_in_dim(small[0:4], own * group, group, 1)
-    gains = gains + swap(gains, "heads", 2)
     kernel_out = small[4 : 4 + KERNEL].reshape(KERNEL, 3, PADW)[:, :, :width].reshape(KERNEL, 3, heads, HEAD_DIM)
     kernel_out = kernel_out.transpose(1, 2, 3, 0).reshape(3, heads, HEAD_DIM * KERNEL)
     kernel_out = lax.dynamic_slice_in_dim(kernel_out, own * share, share, 2)

time: 217 us -> 213 us (0.982)
  starting transfers between devices: 53.5 us -> 38 us
  waiting for transfers between devices: 74.1 us -> 87.1 us
  Pallas kernels: 62.6 us -> 60 us
    ppermute x37, starting transfers between devices: 46.6 us -> 31.1 us  [swap(): lax.ppermute(shard, axis, [(i, i ^ by) for i in range(lax.axis_size(axis))])]
    ppermute x1, waiting for transfers between devices: 0.01 us -> 10.6 us  [on_device(): remote_in = lax.ppermute(remote, 'seq', [(1, 0)])]
    pallas_call x15, Pallas kernels: 62.6 us -> 60 us  [call(): pl.pallas_call(body, out_shape=[jax.ShapeDtypeStruct(*o) for o in outs],...]
    ppermute x37, waiting for transfers between devices: 74.1 us -> 76.3 us  [swap(): lax.ppermute(shard, axis, [(i, i ^ by) for i in range(lax.axis_size(axis))])]
  transfers between devices with their start and end apart: 40 -> 40, of which waited for: 16 -> 20; matrix products, arithmetic and copies ran while one was open for 7% -> 5% of each run, Pallas kernels for 24% -> 24%
where the time goes in v6:
time: 213 us; the launch traced here: 211 us
  waiting for transfers between devices  87.1 us (41%)
  Pallas kernels  60 us (28%)
  starting transfers between devices  38 us (18%)
  local copies, waits for them, and re-layouts  15.2 us (7%)
  other arithmetic  9.73 us (5%)
    ppermute x37, waiting for transfers between devices, swap(): lax.ppermute(shard, axis, [(i, i ^ by) for i in range(lax.axis_size(axis))])  76.3 us
    pallas_call x15, Pallas kernels, call(): pl.pallas_call(body, out_shape=[jax.ShapeDtypeStruct(*o) for o in outs],...  60 us
    ppermute x37, starting transfers between devices, swap(): lax.ppermute(shard, axis, [(i, i ^ by) for i in range(lax.axis_size(axis))])  31.1 us
    unnamed x68, local copies, waits for them, and re-layouts  11.5 us
    ppermute x1, waiting for transfers between devices, on_device(): remote_in = lax.ppermute(remote, 'seq', [(1, 0)])  10.6 us
  transfers between devices with their start and end apart: 40, of which 20 were waited for; matrix products, arithmetic and copies ran while one was open for 5% of the time, Pallas kernels for 24%

profile of v6, /device:TPU:0, one launch (start us, length us, event | category | flops | bytes accessed | tf_op | source)
XLA Modules:
  0.0 211.4 jit_solution(13463302050629623174)
XLA Ops:
  0.6 4.0 %collective-permute-start.2 = (bf16[256,768]{1,0:T(8,128)(2,1)}, bf16[256,768]{1,0:T(8,128)(2,1)S(1)}, u32[]{:S(2)}, u32[]{:S(2)}) collective-permute-start(bf16[256,768]{1,0:T(8,128)(2,1)} %bitcast.79), channel_id=1, source_target_pairs={{0,5},{1,4},{2,7},{3,6},{4,1},{5,0},{6,3},{7,2},{8,13},{9,12},{10,... | collective-permute-start | bytes 1179656 | tf_op jit(solution)/shard_map/ppermute | solution.py:728
  8.9 3.1 %collective-permute-start.3 = (bf16[96,896]{1,0:T(8,128)(2,1)S(1)}, bf16[96,896]{1,0:T(8,128)(2,1)S(1)}, u32[]{:S(2)}, u32[]{:S(2)}) collective-permute-start(bf16[96,896]{1,0:T(8,128)(2,1)S(1)} %shard_map.203), channel_id=1, source_target_pairs={{0,16},{8,24},{16,0},{24,8},{1,17},{9,25},{17,1},{25,9},{2,18},{10... | collective-permute-start | bytes 516104 | tf_op jit(solution)/shard_map/ppermute | solution.py:32
  11.9 7.2 %collective-permute-done.3 = bf16[96,896]{1,0:T(8,128)(2,1)S(1)} collective-permute-done((bf16[96,896]{1,0:T(8,128)(2,1)S(1)}, bf16[96,896]{1,0:T(8,128)(2,1)S(1)}, u32[]{:S(2)}, u32[]{:S(2)}) %collective-permute-start.3) | collective-permute-done | bytes 172064 | tf_op jit(solution)/shard_map/ppermute | solution.py:32
  20.0 2.7 %collective-permute-done.1 = bf16[256,768]{1,0:T(8,128)(2,1)S(1)} collective-permute-done((bf16[256,768]{1,0:T(8,128)(2,1)}, bf16[256,768]{1,0:T(8,128)(2,1)S(1)}, u32[]{:S(2)}, u32[]{:S(2)}) %collective-permute-start.1) | collective-permute-done | bytes 393248 | tf_op jit(solution)/shard_map/ppermute | solution.py:32
  24.9 3.3 %collective-permute-done.6 = bf16[192,896]{1,0:T(8,128)(2,1)S(1)} collective-permute-done((bf16[192,896]{1,0:T(8,128)(2,1)S(1)}, bf16[192,896]{1,0:T(8,128)(2,1)S(1)}, u32[]{:S(2)}, u32[]{:S(2)}) %collective-permute-start.6) | collective-permute-done | bytes 344096 | tf_op jit(solution)/shard_map/ppermute | solution.py:32
  30.8 4.5 %collective-permute-start.16 = (bf16[96,1536]{1,0:T(8,128)(2,1)}, bf16[96,1536]{1,0:T(8,128)(2,1)}, u32[]{:S(2)}, u32[]{:S(2)}) collective-permute-start(bf16[96,1536]{1,0:T(8,128)(2,1)} %pad_maximum_fusion.5), channel_id=1, source_target_pairs={{0,24},{8,16},{16,8},{24,0},{1,25},{9,17},{17,9},{25,1},{2,26},{10... | collective-permute-start | bytes 884744 | tf_op jit(solution)/shard_map/ppermute | solution.py:32
  36.0 3.6 %shard_map.204 = (f32[2048,768]{1,0:T(8,128)S(1)}, bf16[1024,768]{1,0:T(8,128)(2,1)S(1)}) custom-call(s32[8]{0:T(128)S(1)} %concatenate.48.scal, bf16[512,768]{1,0:T(8,128)(2,1)S(1)} %pad_maximum_fusion.2.refs_0_.refs_8_, bf16[512,768]{1,0:T(8,128)(2,1)S(1)} %collective-permute-done.4.refs_1_.refs_9_, ...), custom_call_target="tpu_custom_call" | custom-call | flops 98304 | tf_op jit(solution)/shard_map/pallas_call | solution.py:112
  40.8 3.4 %collective-permute-done.7.refs_2_ = bf16[4,96,896]{2,1,0:T(8,128)(2,1)} collective-permute-done((bf16[4,96,896]{2,1,0:T(8,128)(2,1)S(1)}, bf16[4,96,896]{2,1,0:T(8,128)(2,1)}, u32[]{:S(2)}, u32[]{:S(2)}) %collective-permute-start.7) | collective-permute-done | bytes 688160 | tf_op jit(solution)/shard_map/ppermute | solution.py:32
  45.3 8.7 %shard_map.205 = (bf16[1024,768]{1,0:T(8,128)(2,1)S(1)}, bf16[1040,768]{1,0:T(8,128)(2,1)S(1)}, bf16[768,768]{1,0:T(8,128)(2,1)S(1)}, bf16[1024,256]{1,0:T(8,128...) custom-call(s32[8]{0:T(128)S(1)} %concatenate.48.scal, ...), custom_call_target="tpu_custom_call" | custom-call | flops 113246208 | tf_op jit(solution)/shard_map/pallas_call | solution.py:112
  56.4 3.2 %collective-permute-done.15 = bf16[96,1536]{1,0:T(8,128)(2,1)} collective-permute-done((bf16[96,1536]{1,0:T(8,128)(2,1)}, bf16[96,1536]{1,0:T(8,128)(2,1)}, u32[]{:S(2)}, u32[]{:S(2)}) %collective-permute-start.15) | collective-permute-done | bytes 294944 | tf_op jit(solution)/shard_map/ppermute | solution.py:32
  63.1 6.8 %shard_map.206 = (bf16[1536,128]{1,0:T(8,128)(2,1)S(1)}, f32[192,1024]{1,0:T(8,128)S(1)}, f32[8,1024]{1,0:T(8,128)S(1)}) custom-call(s32[8]{0:T(128)S(1)} %concatenate.48.scal, bf16[1024,256]{1,0:T(8,128)(2,1)S(1)} %get-tuple-element.92.query.refs_0_, bf16[2048,256]{1,0:T(8,128)(2,1)S(1)} %get-tuple-element.93.key.refs_1_, ...), custom_call_target="tpu_custom_call" | custom-call | flops 50331648 | tf_op jit(solution)/shard_map/pallas_call | solution.py:112
  70.5 7.4 %collective-permute-done.12.refs_6_.refs_2_ = bf16[448,768]{1,0:T(8,128)(2,1)S(1)} collective-permute-done((bf16[448,768]{1,0:T(8,128)(2,1)S(1)}, bf16[448,768]{1,0:T(8,128)(2,1)S(1)}, u32[]{:S(2)}, u32[]{:S(2)}) %collective-permute-start.12) | collective-permute-done | bytes 688160 | tf_op jit(solution)/shard_map/ppermute | solution.py:32
  78.4 6.1 %collective-permute-done.9.refs_2_ = bf16[1536,128]{1,0:T(8,128)(2,1)S(1)} collective-permute-done((bf16[1536,128]{1,0:T(8,128)(2,1)S(1)}, bf16[1536,128]{1,0:T(8,128)(2,1)S(1)}, u32[]{:S(2)}, u32[]{:S(2)}) %collective-permute-start.9) | collective-permute-done | bytes 393248 | tf_op jit(solution)/shard_map/ppermute | solution.py:32
  84.5 4.8 %collective-permute-done.17.refs_1_ = bf16[4,96,1536]{2,1,0:T(8,128)(2,1)S(1)} collective-permute-done((bf16[4,96,1536]{2,1,0:T(8,128)(2,1)S(1)}, bf16[4,96,1536]{2,1,0:T(8,128)(2,1)S(1)}, u32[]{:S(2)}, u32[]{:S(2)}) %collective-permute-start.17) | collective-permute-done | bytes 1179680 | tf_op jit(solution)/shard_map/ppermute | solution.py:32
  90.0 8.6 %shard_map.208 = (bf16[1024,768]{1,0:T(8,128)(2,1)S(1)}, bf16[1024,768]{1,0:T(8,128)(2,1)S(1)}, bf16[1024,768]{1,0:T(8,128)(2,1)S(1)}, f32[512,768]{1,0:T(8,128)...) custom-call(s32[8]{0:T(128)S(1)} %concatenate.48.scal, bf16[1536,128]{1,0:T(8,128)(2,1)S(1)} %get-tuple-element.95.refs_0_, ...), custom_call_target="tpu_custom_call" | custom-call | flops 301989888 | tf_op jit(solution)/shard_map/pallas_call | solution.py:112
  98.7 2.0 shard_map.209.refs_4_
  101.8 4.6 %shard_map.210 = (f32[512,768]{1,0:T(8,128)S(1)}, bf16[512,768]{1,0:T(8,128)(2,1)}, bf16[4,96,1536]{2,1,0:T(8,128)(2,1)S(1)}, bf16[4,96,1536]{2,1,0:T(8,128)(2,1)}) custom-call(s32[8]{0:T(128)S(1)} %concatenate.48.scal, bf16[1024,768]{1,0:T(8,128)(2,1)S(1)} %get-tuple-element.112.refs_0_, bf16[1024,768]{1,0:T(8,128)(2,1)S(1)} %get-tuple-element.110.refs_4_.refs_1_, ...), custom_call_target="tpu_custom_call" | custom-call | flops 150994944 | tf_op jit(solution)/shard_map/pallas_call | solution.py:112
  108.6 3.9 %collective-permute-done.19.got = bf16[256,768]{1,0:T(8,128)(2,1)S(1)} collective-permute-done((bf16[256,768]{1,0:T(8,128)(2,1)S(1)}, bf16[256,768]{1,0:T(8,128)(2,1)S(1)}, u32[]{:S(2)}, u32[]{:S(2)}) %collective-permute-start.19) | collective-permute-done | bytes 393248 | tf_op jit(solution)/shard_map/ppermute | solution.py:32
  116.3 9.8 %collective-permute-done.22.refs_2_ = bf16[256,768]{1,0:T(8,128)(2,1)} collective-permute-done((bf16[256,768]{1,0:T(8,128)(2,1)}, bf16[256,768]{1,0:T(8,128)(2,1)}, u32[]{:S(2)}, u32[]{:S(2)}) %collective-permute-start.22) | collective-permute-done | bytes 393248 | tf_op jit(solution)/shard_map/ppermute | solution.py:32
  126.1 2.1 collective-permute-done.23.refs_3_
  129.3 2.8 %shard_map.212 = (bf16[1024,256]{1,0:T(8,128)(2,1)S(1)}, f32[8,1024]{1,0:T(8,128)S(1)}, f32[4,96,192]{2,1,0:T(8,128)S(1)}, bf16[4,96,192]{2,1,0:T(8,128)(2,1)S(1)}) custom-call(s32[8]{0:T(128)S(1)} %concatenate.48.scal, bf16[256,768]{1,0:T(8,128)(2,1)} %get-tuple-element.118.refs_0_, bf16[256,768]{1,0:T(8,128)(2,1)} %collective-permute-done.21.refs_1_, ...), custom_call_target="tpu_custom_call" | custom-call | flops 37748736 | tf_op jit(solution)/shard_map/pallas_call | solution.py:112
  135.0 2.2 %shard_map.213 = (bf16[1024,384]{1,0:T(8,128)(2,1)S(1)}, f32[192,1024]{1,0:T(8,128)S(1)}, bf16[192,2048]{1,0:T(8,128)(2,1)S(1)}) custom-call(s32[8]{0:T(128)S(1)} %concatenate.48.scal, bf16[1024,256]{1,0:T(8,128)(2,1)S(1)} %get-tuple-element.92.query.refs_0_, bf16[2048,256]{1,0:T(8,128)(2,1)S(1)} %get-tuple-element.93.key.refs_1_, ...), custom_call_target="tpu_custom_call" | custom-call | flops 125829120 | tf_op jit(solution)/shard_map/pallas_call | solution.py:112
  139.6 8.0 %shard_map.214 = (bf16[1024,256]{1,0:T(8,128)(2,1)S(1)}, bf16[1024,256]{1,0:T(8,128)(2,1)S(1)}, bf16[1024,256]{1,0:T(8,128)(2,1)S(1)}, f32[8,768]{1,0:T(8,128)S(1)}) custom-call(s32[8]{0:T(128)S(1)} %concatenate.48.scal, bf16[1024,256]{1,0:T(8,128)(2,1)S(1)} %get-tuple-element.92.query.refs_0_, bf16[2048,256]{1,0:T(8,128)(2,1)S(1)} %get-tuple-element.93.key.refs_1_, ...), custom_call_target="tpu_custom_call" | custom-call | flops 125829120 | tf_op jit(solution)/shard_map/pallas_call | solution.py:112
  151.0 3.2 %collective-permute-start.39 = (bf16[96,1536]{1,0:T(8,128)(2,1)S(1)}, bf16[96,1536]{1,0:T(8,128)(2,1)S(1)}, u32[]{:S(2)}, u32[]{:S(2)}) collective-permute-start(bf16[96,1536]{1,0:T(8,128)(2,1)S(1)} %get-tuple-element.202), channel_id=1, source_target_pairs={{0,24},{8,16},{16,8},{24,0},{1,25},{9,17},{17,9},{25,1},{2,26},{10... | collective-permute-start | bytes 884744 | tf_op jit(solution)/shard_map/ppermute | solution.py:32
  154.2 10.6 %collective-permute-done.27.refs_3_ = bf16[1024,384]{1,0:T(8,128)(2,1)S(1)} collective-permute-done((bf16[1024,384]{1,0:T(8,128)(2,1)S(1)}, bf16[1024,384]{1,0:T(8,128)(2,1)S(1)}, u32[]{:S(2)}, u32[]{:S(2)}) %collective-permute-start.27) | collective-permute-done | bytes 786464 | tf_op jit(solution)/shard_map/ppermute | solution.py:828
  165.1 5.4 %shard_map.215 = (bf16[1024,768]{1,0:T(8,128)(2,1)S(1)}, f32[4,96,640]{2,1,0:T(8,128)S(1)}, bf16[4,96,640]{2,1,0:T(8,128)(2,1)S(1)}, f32[8,768]{1,0:T(8,128)S(1)}) custom-call(s32[8]{0:T(128)S(1)} %concatenate.48.scal, bf16[1024,256]{1,0:T(8,128)(2,1)S(1)} %get-tuple-element.133.refs_0_, bf16[1024,256]{1,0:T(8,128)(2,1)S(1)} %get-tuple-element.135.refs_1_, ...), custom_call_target="tpu_custom_call" | custom-call | flops 56623104 | tf_op jit(solution)/shard_map/pallas_call | solution.py:112
  170.7 2.1 shard_map.216
  174.8 7.9 %collective-permute-done.33 = bf16[4,96,640]{2,1,0:T(8,128)(2,1)S(1)} collective-permute-done((bf16[4,96,640]{2,1,0:T(8,128)(2,1)S(1)}, bf16[4,96,640]{2,1,0:T(8,128)(2,1)S(1)}, u32[]{:S(2)}, u32[]{:S(2)}) %collective-permute-start.33) | collective-permute-done | bytes 491552 | tf_op jit(solution)/shard_map/ppermute | solution.py:32
  188.8 4.2 %collective-permute-done.32 = f32[4,768]{1,0:T(4,128)S(1)} collective-permute-done((f32[4,768]{1,0:T(4,128)S(1)}, f32[4,768]{1,0:T(4,128)S(1)}, u32[]{:S(2)}, u32[]{:S(2)}) %collective-permute-start.32) | collective-permute-done | bytes 12320 | tf_op jit(solution)/shard_map/ppermute | solution.py:32
  193.9 3.6 %collective-permute-start.35 = (bf16[112,768]{1,0:T(8,128)(2,1)S(1)}, bf16[112,768]{1,0:T(8,128)(2,1)S(1)}, u32[]{:S(2)}, u32[]{:S(2)}) collective-permute-start(bf16[112,768]{1,0:T(8,128)(2,1)S(1)} %get-tuple-element.226), channel_id=1, source_target_pairs={{0,16},{8,24},{16,0},{24,8},{1,17},{9,25},{17,1},{25,9},{2,18},{10... | collective-permute-start | bytes 516104 | tf_op jit(solution)/shard_map/ppermute | solution.py:32
  198.4 2.2 %shard_map.217 = (f32[256,768]{1,0:T(8,128)}, bf16[256,768]{1,0:T(8,128)(2,1)}, f32[8,768]{1,0:T(8,128)}) custom-call(s32[8]{0:T(128)S(1)} %concatenate.48.scal, f32[256,768]{1,0:T(8,128)S(1)} %get-tuple-element.197.part, bf16[256,768]{1,0:T(8,128)(2,1)S(1)} %collective-permute-done.30.got, bf16[256,768]{1,0:T(8,128)(2,1)S(1)} %bitcast.83, ...), custom_call_target="tpu_custom_call" | custom-call | tf_op jit(solution)/shard_map/pallas_call | solution.py:112
  202.3 5.5 %collective-permute-done.35 = bf16[112,768]{1,0:T(8,128)(2,1)S(1)} collective-permute-done((bf16[112,768]{1,0:T(8,128)(2,1)S(1)}, bf16[112,768]{1,0:T(8,128)(2,1)S(1)}, u32[]{:S(2)}, u32[]{:S(2)}) %collective-permute-start.35) | collective-permute-done | bytes 172064 | tf_op jit(solution)/shard_map/ppermute | solution.py:32
  (181 shorter events, 52.7 us)
Async XLA Ops:
  0.6 19.3 %collective-permute-start.2 = (bf16[256,768]{1,0:T(8,128)(2,1)}, bf16[256,768]{1,0:T(8,128)(2,1)S(1)}, u32[]{:S(2)}, u32[]{:S(2)}) collective-permute-start(bf16[256,768]{1,0:T(8,128)(2,1)} %bitcast.79), channel_id=1, source_target_pairs={{0,5},{1,4},{2,7},{3,6},{4,1},{5,0},{6,3},{7,2},{8,13},{9,12},{10,... | collective-permute-start | bytes 1179656 | tf_op jit(solution)/shard_map/ppermute | solution.py:728
  4.6 18.0 %collective-permute-start.1 = (bf16[256,768]{1,0:T(8,128)(2,1)}, bf16[256,768]{1,0:T(8,128)(2,1)S(1)}, u32[]{:S(2)}, u32[]{:S(2)}) collective-permute-start(bf16[256,768]{1,0:T(8,128)(2,1)} %bitcast.80), channel_id=1, source_target_pairs={{0,4},{2,6},{4,0},{6,2},{1,5},{3,7},{5,1},{7,3},{8,12},{10,14},{12... | collective-permute-start | bytes 1179656 | tf_op jit(solution)/shard_map/ppermute | solution.py:32
  5.2 17.5 %collective-permute-start = (bf16[256,768]{1,0:T(8,128)(2,1)}, bf16[256,768]{1,0:T(8,128)(2,1)S(1)}, u32[]{:S(2)}, u32[]{:S(2)}) collective-permute-start(bf16[256,768]{1,0:T(8,128)(2,1)} %bitcast.81), channel_id=1, source_target_pairs={{0,1},{1,0},{2,3},{3,2},{4,5},{5,4},{6,7},{7,6},{8,9},{9,8},{10,11... | collective-permute-start | bytes 1179656 | tf_op jit(solution)/shard_map/ppermute | solution.py:32
  8.9 10.3 %collective-permute-start.3 = (bf16[96,896]{1,0:T(8,128)(2,1)S(1)}, bf16[96,896]{1,0:T(8,128)(2,1)S(1)}, u32[]{:S(2)}, u32[]{:S(2)}) collective-permute-start(bf16[96,896]{1,0:T(8,128)(2,1)S(1)} %shard_map.203), channel_id=1, source_target_pairs={{0,16},{8,24},{16,0},{24,8},{1,17},{9,25},{17,1},{25,9},{2,18},{10... | collective-permute-start | bytes 516104 | tf_op jit(solution)/shard_map/ppermute | solution.py:32
  24.2 11.0 %collective-permute-start.5 = (bf16[512,768]{1,0:T(8,128)(2,1)}, bf16[512,768]{1,0:T(8,128)(2,1)}, u32[]{:S(2)}, u32[]{:S(2)}) collective-permute-start(bf16[512,768]{1,0:T(8,128)(2,1)} %constant_dynamic-update-slice_fusion.refs_2_), channel_id=1, source_target_pairs={{0,2},{2,0},{4,6},{6,4},{1,3},{3,1},{5,7},{7,5},{8,10},{10,8},{12,... | collective-permute-start | bytes 2359304 | tf_op jit(solution)/shard_map/ppermute | solution.py:32
  24.3 11.7 %collective-permute-start.4 = (bf16[512,768]{1,0:T(8,128)(2,1)S(1)}, bf16[512,768]{1,0:T(8,128)(2,1)S(1)}, u32[]{:S(2)}, u32[]{:S(2)}) collective-permute-start(bf16[512,768]{1,0:T(8,128)(2,1)S(1)} %pad_maximum_fusion.2.refs_0_.refs_8_), channel_id=1, source_target_pairs={{0,2},{2,0},{4,6},{6,4},{1,3},{3,1},{5,7},{7,5},{8,10},{10,8},{12,... | collective-permute-start | bytes 2359304 | tf_op jit(solution)/shard_map/ppermute | solution.py:32
  28.3 15.9 %collective-permute-start.7 = (bf16[4,96,896]{2,1,0:T(8,128)(2,1)S(1)}, bf16[4,96,896]{2,1,0:T(8,128)(2,1)}, u32[]{:S(2)}, u32[]{:S(2)}) collective-permute-start(bf16[4,96,896]{2,1,0:T(8,128)(2,1)S(1)} %pad_maximum_fusion.3.refs_1_), channel_id=1, source_target_pairs={{0,1},{1,0},{2,3},{3,2},{4,5},{5,4},{6,7},{7,6},{8,9},{9,8},{10,11... | collective-permute-start | bytes 2064392 | tf_op jit(solution)/shard_map/ppermute | solution.py:32
  30.8 25.6 %collective-permute-start.16 = (bf16[96,1536]{1,0:T(8,128)(2,1)}, bf16[96,1536]{1,0:T(8,128)(2,1)}, u32[]{:S(2)}, u32[]{:S(2)}) collective-permute-start(bf16[96,1536]{1,0:T(8,128)(2,1)} %pad_maximum_fusion.5), channel_id=1, source_target_pairs={{0,24},{8,16},{16,8},{24,0},{1,25},{9,17},{17,9},{25,1},{2,26},{10... | collective-permute-start | bytes 884744 | tf_op jit(solution)/shard_map/ppermute | solution.py:32
  35.2 24.4 %collective-permute-start.15 = (bf16[96,1536]{1,0:T(8,128)(2,1)}, bf16[96,1536]{1,0:T(8,128)(2,1)}, u32[]{:S(2)}, u32[]{:S(2)}) collective-permute-start(bf16[96,1536]{1,0:T(8,128)(2,1)} %pad_maximum_fusion.5), channel_id=1, source_target_pairs={{0,16},{8,24},{16,0},{24,8},{1,17},{9,25},{17,1},{25,9},{2,18},{10... | collective-permute-start | bytes 884744 | tf_op jit(solution)/shard_map/ppermute | solution.py:32
  35.2 24.4 %collective-permute-start.14 = (bf16[96,1536]{1,0:T(8,128)(2,1)}, bf16[96,1536]{1,0:T(8,128)(2,1)}, u32[]{:S(2)}, u32[]{:S(2)}) collective-permute-start(bf16[96,1536]{1,0:T(8,128)(2,1)} %pad_maximum_fusion.5), channel_id=1, source_target_pairs={{0,8},{8,0},{16,24},{24,16},{1,9},{9,1},{17,25},{25,17},{2,10},{10... | collective-permute-start | bytes 884744 | tf_op jit(solution)/shard_map/ppermute | solution.py:32
  59.6 18.3 %collective-permute-start.12 = (bf16[448,768]{1,0:T(8,128)(2,1)S(1)}, bf16[448,768]{1,0:T(8,128)(2,1)S(1)}, u32[]{:S(2)}, u32[]{:S(2)}) collective-permute-start(bf16[448,768]{1,0:T(8,128)(2,1)S(1)} %get-tuple-element.96.refs_4_.refs_0_), channel_id=1, source_target_pairs={{0,4},{2,6},{4,0},{6,2},{1,5},{3,7},{5,1},{7,3},{8,12},{10,14},{12... | collective-permute-start | bytes 2064392 | tf_op jit(solution)/shard_map/ppermute | solution.py:32
  62.5 26.8 %collective-permute-start.17 = (bf16[4,96,1536]{2,1,0:T(8,128)(2,1)S(1)}, bf16[4,96,1536]{2,1,0:T(8,128)(2,1)S(1)}, u32[]{:S(2)}, u32[]{:S(2)}) collective-permute-start(bf16[4,96,1536]{2,1,0:T(8,128)(2,1)S(1)} %pad_maximum_fusion.1.refs_0_), channel_id=1, source_target_pairs={{0,1},{1,0},{2,3},{3,2},{4,5},{5,4},{6,7},{7,6},{8,9},{9,8},{10,11... | collective-permute-start | bytes 3538952 | tf_op jit(solution)/shard_map/ppermute | solution.py:32
  69.9 14.6 %collective-permute-start.9 = (bf16[1536,128]{1,0:T(8,128)(2,1)S(1)}, bf16[1536,128]{1,0:T(8,128)(2,1)S(1)}, u32[]{:S(2)}, u32[]{:S(2)}) collective-permute-start(bf16[1536,128]{1,0:T(8,128)(2,1)S(1)} %get-tuple-element.95.refs_0_), channel_id=1, source_target_pairs={{0,4},{2,6},{4,0},{6,2},{1,5},{3,7},{5,1},{7,3},{8,12},{10,14},{12... | collective-permute-start | bytes 1179656 | tf_op jit(solution)/shard_map/ppermute | solution.py:32
  70.5 19.5 %collective-permute-start.11 = (bf16[448,768]{1,0:T(8,128)(2,1)S(1)}, bf16[448,768]{1,0:T(8,128)(2,1)S(1)}, u32[]{:S(2)}, u32[]{:S(2)}) collective-permute-start(bf16[448,768]{1,0:T(8,128)(2,1)S(1)} %get-tuple-element.96.refs_4_.refs_0_), channel_id=1, source_target_pairs={{0,2},{2,0},{4,6},{6,4},{1,3},{3,1},{5,7},{7,5},{8,10},{10,8},{12,... | collective-permute-start | bytes 2064392 | tf_op jit(solution)/shard_map/ppermute | solution.py:32
  77.9 12.1 %collective-permute-start.13 = (bf16[448,768]{1,0:T(8,128)(2,1)S(1)}, bf16[448,768]{1,0:T(8,128)(2,1)S(1)}, u32[]{:S(2)}, u32[]{:S(2)}) collective-permute-start(bf16[448,768]{1,0:T(8,128)(2,1)S(1)} %collective-permute-done.12.refs_6_.refs_2_), channel_id=1, source_target_pairs={{0,2},{2,0},{4,6},{6,4},{1,3},{3,1},{5,7},{7,5},{8,10},{10,8},{12,... | collective-permute-start | bytes 2064392 | tf_op jit(solution)/shard_map/ppermute | solution.py:32
  77.9 12.1 %collective-permute-start.8 = (bf16[1536,128]{1,0:T(8,128)(2,1)S(1)}, bf16[1536,128]{1,0:T(8,128)(2,1)S(1)}, u32[]{:S(2)}, u32[]{:S(2)}) collective-permute-start(bf16[1536,128]{1,0:T(8,128)(2,1)S(1)} %get-tuple-element.95.refs_0_), channel_id=1, source_target_pairs={{0,2},{2,0},{4,6},{6,4},{1,3},{3,1},{5,7},{7,5},{8,10},{10,8},{12,... | collective-permute-start | bytes 1179656 | tf_op jit(solution)/shard_map/ppermute | solution.py:32
  101.2 11.3 %collective-permute-start.19 = (bf16[256,768]{1,0:T(8,128)(2,1)S(1)}, bf16[256,768]{1,0:T(8,128)(2,1)S(1)}, u32[]{:S(2)}, u32[]{:S(2)}) collective-permute-start(bf16[256,768]{1,0:T(8,128)(2,1)S(1)} %get-tuple-element.200), channel_id=1, source_target_pairs={{0,4},{2,6},{4,0},{6,2},{1,5},{3,7},{5,1},{7,3},{8,12},{10,14},{12... | collective-permute-start | bytes 1179656 | tf_op jit(solution)/shard_map/ppermute | solution.py:32
  107.4 31.2 %collective-permute-start.25 = (bf16[4,96,1536]{2,1,0:T(8,128)(2,1)}, bf16[4,96,1536]{2,1,0:T(8,128)(2,1)}, u32[]{:S(2)}, u32[]{:S(2)}) collective-permute-start(bf16[4,96,1536]{2,1,0:T(8,128)(2,1)} %get-tuple-element.127), channel_id=1, source_target_pairs={{0,1},{1,0},{2,3},{3,2},{4,5},{5,4},{6,7},{7,6},{8,9},{9,8},{10,11... | collective-permute-start | bytes 3538952 | tf_op jit(solution)/shard_map/ppermute | solution.py:32
  115.3 10.8 %collective-permute-start.22 = (bf16[256,768]{1,0:T(8,128)(2,1)}, bf16[256,768]{1,0:T(8,128)(2,1)}, u32[]{:S(2)}, u32[]{:S(2)}) collective-permute-start(bf16[256,768]{1,0:T(8,128)(2,1)} %get-tuple-element.118.refs_0_), channel_id=1, source_target_pairs={{0,4},{2,6},{4,0},{6,2},{1,5},{3,7},{5,1},{7,3},{8,12},{10,14},{12... | collective-permute-start | bytes 1179656 | tf_op jit(solution)/shard_map/ppermute | solution.py:32
  115.8 17.6 %collective-permute-start.20 = (bf16[512,768]{1,0:T(8,128)(2,1)}, bf16[512,768]{1,0:T(8,128)(2,1)}, u32[]{:S(2)}, u32[]{:S(2)}) collective-permute-start(bf16[512,768]{1,0:T(8,128)(2,1)} %get-tuple-element.119), channel_id=1, source_target_pairs={{0,2},{2,0},{4,6},{6,4},{1,3},{3,1},{5,7},{7,5},{8,10},{10,8},{12,... | collective-permute-start | bytes 2359304 | tf_op jit(solution)/shard_map/ppermute | solution.py:32
  115.8 10.3 %collective-permute-start.21 = (bf16[256,768]{1,0:T(8,128)(2,1)}, bf16[256,768]{1,0:T(8,128)(2,1)}, u32[]{:S(2)}, u32[]{:S(2)}) collective-permute-start(bf16[256,768]{1,0:T(8,128)(2,1)} %get-tuple-element.118.refs_0_), channel_id=1, source_target_pairs={{0,2},{2,0},{4,6},{6,4},{1,3},{3,1},{5,7},{7,5},{8,10},{10,8},{12,... | collective-permute-start | bytes 1179656 | tf_op jit(solution)/shard_map/ppermute | solution.py:32
  134.5 36.2 %collective-permute-start.24 = (bf16[256,768]{1,0:T(8,128)(2,1)S(1)}, bf16[256,768]{1,0:T(8,128)(2,1)S(1)}, u32[]{:S(2)}, u32[]{:S(2)}) collective-permute-start(bf16[256,768]{1,0:T(8,128)(2,1)S(1)} %add_convert_fusion.2), channel_id=1, source_target_pairs={{0,4},{2,6},{4,0},{6,2},{1,5},{3,7},{5,1},{7,3},{8,12},{10,14},{12... | collective-permute-start | bytes 1179656 | tf_op jit(solution)/shard_map/ppermute | solution.py:32
  137.2 27.6 %collective-permute-start.27 = (bf16[1024,384]{1,0:T(8,128)(2,1)S(1)}, bf16[1024,384]{1,0:T(8,128)(2,1)S(1)}, u32[]{:S(2)}, u32[]{:S(2)}) collective-permute-start(bf16[1024,384]{1,0:T(8,128)(2,1)S(1)} %get-tuple-element.129), channel_id=1, source_target_pairs={{1,0},{3,2},{5,4},{7,6},{9,8},{11,10},{13,12},{15,14},{17,16},{19,... | collective-permute-start | bytes 2359304 | tf_op jit(solution)/shard_map/ppermute | solution.py:828
  147.6 17.5 %collective-permute-start.28 = (f32[8,768]{1,0:T(8,128)S(1)}, f32[8,768]{1,0:T(8,128)S(1)}, u32[]{:S(2)}, u32[]{:S(2)}) collective-permute-start(f32[8,768]{1,0:T(8,128)S(1)} %get-tuple-element.138), channel_id=1, source_target_pairs={{1,0},{3,2},{5,4},{7,6},{9,8},{11,10},{13,12},{15,14},{17,16},{19,... | collective-permute-start | bytes 73736 | tf_op jit(solution)/shard_map/ppermute | solution.py:842
  151.0 37.6 %collective-permute-start.39 = (bf16[96,1536]{1,0:T(8,128)(2,1)S(1)}, bf16[96,1536]{1,0:T(8,128)(2,1)S(1)}, u32[]{:S(2)}, u32[]{:S(2)}) collective-permute-start(bf16[96,1536]{1,0:T(8,128)(2,1)S(1)} %get-tuple-element.202), channel_id=1, source_target_pairs={{0,24},{8,16},{16,8},{24,0},{1,25},{9,17},{17,9},{25,1},{2,26},{10... | collective-permute-start | bytes 884744 | tf_op jit(solution)/shard_map/ppermute | solution.py:32
  154.2 34.4 %collective-permute-start.38 = (bf16[96,1536]{1,0:T(8,128)(2,1)S(1)}, bf16[96,1536]{1,0:T(8,128)(2,1)S(1)}, u32[]{:S(2)}, u32[]{:S(2)}) collective-permute-start(bf16[96,1536]{1,0:T(8,128)(2,1)S(1)} %get-tuple-element.203), channel_id=1, source_target_pairs={{0,16},{8,24},{16,0},{24,8},{1,17},{9,25},{17,1},{25,9},{2,18},{10... | collective-permute-start | bytes 884744 | tf_op jit(solution)/shard_map/ppermute | solution.py:32
  164.8 23.8 %collective-permute-start.37 = (bf16[96,1536]{1,0:T(8,128)(2,1)S(1)}, bf16[96,1536]{1,0:T(8,128)(2,1)S(1)}, u32[]{:S(2)}, u32[]{:S(2)}) collective-permute-start(bf16[96,1536]{1,0:T(8,128)(2,1)S(1)} %get-tuple-element.204), channel_id=1, source_target_pairs={{0,8},{8,0},{16,24},{24,16},{1,9},{9,1},{17,25},{25,17},{2,10},{10... | collective-permute-start | bytes 884744 | tf_op jit(solution)/shard_map/ppermute | solution.py:32
  170.5 12.2 %collective-permute-start.33 = (bf16[4,96,640]{2,1,0:T(8,128)(2,1)S(1)}, bf16[4,96,640]{2,1,0:T(8,128)(2,1)S(1)}, u32[]{:S(2)}, u32[]{:S(2)}) collective-permute-start(bf16[4,96,640]{2,1,0:T(8,128)(2,1)S(1)} %get-tuple-element.152), channel_id=1, source_target_pairs={{0,1},{1,0},{2,3},{3,2},{4,5},{5,4},{6,7},{7,6},{8,9},{9,8},{10,11... | collective-permute-start | bytes 1474568 | tf_op jit(solution)/shard_map/ppermute | solution.py:32
  172.8 10.2 %collective-permute-start.29 = (bf16[520,768]{1,0:T(8,128)(2,1)S(1)}, bf16[520,768]{1,0:T(8,128)(2,1)S(1)}, u32[]{:S(2)}, u32[]{:S(2)}) collective-permute-start(bf16[520,768]{1,0:T(8,128)(2,1)S(1)} %get-tuple-element.146), channel_id=1, source_target_pairs={{0,2},{2,0},{4,6},{6,4},{1,3},{3,1},{5,7},{7,5},{8,10},{10,8},{12,... | collective-permute-start | bytes 2396168 | tf_op jit(solution)/shard_map/ppermute | solution.py:32
  183.5 14.9 %collective-permute-start.30 = (bf16[256,768]{1,0:T(8,128)(2,1)S(1)}, bf16[256,768]{1,0:T(8,128)(2,1)S(1)}, u32[]{:S(2)}, u32[]{:S(2)}) collective-permute-start(bf16[256,768]{1,0:T(8,128)(2,1)S(1)} %get-tuple-element.196), channel_id=1, source_target_pairs={{0,4},{2,6},{4,0},{6,2},{1,5},{3,7},{5,1},{7,3},{8,12},{10,14},{12... | collective-permute-start | bytes 1179656 | tf_op jit(solution)/shard_map/ppermute | solution.py:32
  193.1 9.2 %collective-permute-start.36 = (bf16[112,768]{1,0:T(8,128)(2,1)S(1)}, bf16[112,768]{1,0:T(8,128)(2,1)S(1)}, u32[]{:S(2)}, u32[]{:S(2)}) collective-permute-start(bf16[112,768]{1,0:T(8,128)(2,1)S(1)} %get-tuple-element.224), channel_id=1, source_target_pairs={{0,24},{8,16},{16,8},{24,0},{1,25},{9,17},{17,9},{25,1},{2,26},{10... | collective-permute-start | bytes 516104 | tf_op jit(solution)/shard_map/ppermute | solution.py:32
  193.9 13.8 %collective-permute-start.35 = (bf16[112,768]{1,0:T(8,128)(2,1)S(1)}, bf16[112,768]{1,0:T(8,128)(2,1)S(1)}, u32[]{:S(2)}, u32[]{:S(2)}) collective-permute-start(bf16[112,768]{1,0:T(8,128)(2,1)S(1)} %get-tuple-element.226), channel_id=1, source_target_pairs={{0,16},{8,24},{16,0},{24,8},{1,17},{9,25},{17,1},{25,9},{2,18},{10... | collective-permute-start | bytes 516104 | tf_op jit(solution)/shard_map/ppermute | solution.py:32
  (41 other events, 318.5 us)
